TPU v7x, 32 devices: a whole 2x2x4 slice. The times are simulated.
32 devices in a mesh: row: 4 (over y, x), col: 8 (over z, core).
Axes of the slice: x: 2, y: 2, z: 4, core: 2. Of those that a mesh axis runs over, the one named last changes fastest.
Arguments:
- vectors: bfloat16 [64, 131072], P(None, ('col', 'row')), may hold values from -6 to 6
- blocks: bfloat16 [4, 4096, 128, 128], P('row', 'col'), may hold values from -0.1875 to 0.1875
- block_rows: int32 [4, 4096], P('row', 'col'), may hold values from 0 to 255, as said below
- block_cols: int32 [4, 4096], P('row', 'col'), may hold values from 0 to 127, as said below
- counts: int32 [4, 8], P('row', 'col'), may hold values from 1 to 512, as said below
Outputs:
- result: float32 [64, 131072], P(None, ('row', 'col'))
Inputs may be any that keep to these rules, and one draw needn't show every extreme that they name: Within one owner pair the slots below its count name distinct positions (block_rows, block_cols) of its 256 x 256/2 grid of blocks; later slots hold 0. `block_cols`: see block_rows. `counts`: some owner pair holds exactly 512 blocks, and some other exactly one.
All inputs are finite; a program needn't handle non-finite values.
Results may differ from a plain program's by a relative error of at most 0.0029.
Values may be sent and summed in bfloat16 or wider, within the bound.
No kernel may reach another device: no remote copies, remote signals or barrier semaphores. Data moves between devices by JAX's collectives and lax.ppermute only.
A program may use at most 128 MiB of HBM per device.

v0:
```python
import jax
import jax.numpy as jnp
from jax import lax
from jax.sharding import PartitionSpec as P


def from_root(block, axis, owner):
    block = jnp.where(lax.axis_index(axis) == owner, block, jnp.zeros_like(block))
    return lax.psum(block, axis)


def block_product(vec_panel, blocks, block_rows, block_cols, counts):
    slot_total = blocks.shape[1]
    tile_size = blocks.shape[2]
    vec_width = vec_panel.shape[0]
    row_blocks = 2 * vec_panel.shape[1] // tile_size
    vec_tiles = vec_panel.reshape(vec_width, -1, tile_size)
    picked = jnp.take(vec_tiles, block_cols.reshape(-1), axis=1)
    product = jnp.einsum("ksc,src->ksr", picked, blocks[0], preferred_element_type=jnp.float32)
    live_slots = jnp.arange(slot_total, dtype=jnp.int32) < counts.reshape(())
    owner_map = (block_rows == jnp.arange(row_blocks, dtype=jnp.int32)[:, None]) & live_slots[
        None, :
    ]
    summed = jnp.einsum(
        "is,ksr->kir", owner_map.astype(jnp.float32), product, precision=lax.Precision.HIGHEST
    )
    return summed.reshape(vec_width, row_blocks * tile_size)


def relay_group(group_rows):
    half_width = group_rows.shape[1] // 2
    col_owner = lax.axis_index("col")
    own_half = lax.dynamic_slice_in_dim(group_rows, col_owner % 2 * half_width, half_width, 1)
    return from_root(own_half, "row", col_owner // 2)


def shards(vectors, blocks, block_rows, block_cols, counts):
    vec_panel = lax.all_gather(vectors, "row", axis=1, tiled=True)
    first_part = block_product(vec_panel, blocks, block_rows, block_cols, counts)
    group_rows = lax.psum(first_part, "col").astype(jnp.bfloat16)
    second_panel = relay_group(group_rows)
    second_part = block_product(second_panel, blocks, block_rows, block_cols, counts)
    return lax.psum_scatter(second_part, "col", scatter_dimension=1, tiled=True)


def solution(mesh):
    in_specs = (
        P(None, ("col", "row")),
        P("row", "col", None, None),
        P("row", "col"),
        P("row", "col"),
        P("row", "col"),
    )
    out_specs = P(None, ("row", "col"))
    return jax.shard_map(shards, mesh=mesh, in_specs=in_specs, out_specs=out_specs, check_vma=False)
```

profile of v0, /device:TPU:0, one launch (start us, length us, event | category | flops | bytes accessed | tf_op | source)
XLA Modules:
  0.0 558.9 jit_solution(10236251056222093758)
XLA Ops:
  6.5 0.0 all-gather.2.cloned.1.call-start
  6.5 0.7 all-gather.2.cloned.1.call-update
  7.3 0.0 all-reduce.3.cloned.1.call-start
  8.0 0.7 compare_select_fusion
  8.7 0.7 compare_and_fusion
  9.4 37.7 %all-gather.2.cloned.1.call-done = bf16[64,16384]{1,0:T(8,128)(2,1)} async-done(((bf16[64,4096]{1,0:T(8,128)(2,1)}), bf16[64,16384]{1,0:T(8,128)(2,1)}) %all-gather.2.cloned.1.call-update) | async-done | bytes 2097168 | tf_op jit(solution)/shard_map/all_gather | solution.py:38
  47.1 2.2 copy_bitcast_fusion.3
  49.3 13.5 %gather_fusion = bf16[512,64,128]{2,1,0:T(8,128)(2,1)} fusion(bf16[64,128,128]{2,0,1:T(8,128)(2,1)S(1)} %copy_bitcast_fusion.3, s32[1024]{0:T(1024)S(1)} %pad_clamp_fusion), kind=kCustom, calls=%fused_computation.clone | custom fusion | bytes 16779264 | tf_op jit(solution)/shard_map/jit(_take)/gather | solution.py:18
  62.8 0.0 copy-start
  62.8 20.4 %fusion.8 = f32[64,512,128]{2,0,1:T(8,128)} fusion(bf16[1,512,128,128]{3,2,1,0:T(8,128)(2,1)} %param.8, bf16[512,64,128]{2,1,0:T(8,128)(2,1)} %gather_fusion, pred[512]{0:T(512)(128)(4,1)S(1)} %compare_and_fusion), kind=kOutput, calls=%fused_computation.10 | convolution fusion | flops 1077936128 | bytes 41943552 | tf_op jit(solution)/shard_map/ksc,src->ksr/dot_general | solution.py:19
  83.2 0.0 copy-done
  83.2 27.8 %fusion.22 = f32[64,256,128]{1,2,0:T(8,128)} fusion(f32[64,512,128]{2,0,1:T(8,128)} %fusion.8, s32[512]{0:T(512)S(1)} %bitcast.53, pred[512]{0:T(512)(128)(4,1)S(1)} %iota_compare_fusion.1), kind=kOutput, calls=%fused_computation.23 | convolution fusion | flops 12885164032 | bytes 25168384 | tf_op jit(solution)/shard_map/is,ksr->kir/dot_general | solution.py:24
  111.0 9.2 %copy.10 = f32[64,256,128]{2,1,0:T(8,128)} copy(f32[64,256,128]{1,2,0:T(8,128)} %fusion.22) | data formatting | bytes 16777216 | tf_op jit(solution)/shard_map/is,ksr->kir/transpose | solution.py:24
  120.2 11.3 %copy.31 = f32[8,8,256,128]{3,1,2,0:T(8,128)} copy(f32[8,8,256,128]{3,2,1,0:T(8,128)} %bitcast.50) | data formatting | bytes 16777216
  131.5 169.6 %all-reduce.4 = bf16[64,32768]{1,0:T(8,128)(2,1)} all-reduce(f32[64,32768]{1,0:T(8,128)} %bitcast.51), channel_id=1, replica_groups=mesh['row'=4,'col'=8] {'col'}, use_global_device_ids=true, to_apply=%region_0.0 | all-reduce | flops 2097152 | bytes 12582912 | tf_op jit(solution)/shard_map/psum | solution.py:40
  301.1 3.5 copy_bitcast_fusion.2
  304.6 0.0 all-reduce.3.cloned.1.call-update
  304.6 0.0 reduce-scatter.2.cloned.1.call-start
  304.7 67.5 %all-reduce.3.cloned.1.call-done = bf16[64,128,128]{2,0,1:T(8,128)(2,1)} async-done(((bf16[64,128,128]{2,0,1:T(8,128)(2,1)}), bf16[64,128,128]{2,0,1:T(8,128)(2,1)}) %all-reduce.3.cloned.1.call-update) | async-done | bytes 2097168 | tf_op jit(solution)/shard_map/psum | solution.py:9
  372.2 21.6 %gather_fusion.1 = bf16[512,64,128]{2,1,0:T(8,128)(2,1)} fusion(bf16[64,128,128]{2,0,1:T(8,128)(2,1)} %all-reduce.3.cloned.1.call-done, s32[1024]{0:T(1024)S(1)} %pad_clamp_fusion), kind=kCustom, calls=%fused_computation.1.clone | custom fusion | bytes 16779264 | tf_op jit(solution)/shard_map/jit(_take)/gather | solution.py:18
  393.8 20.5 %fusion.11 = f32[64,512,128]{2,0,1:T(8,128)} fusion(bf16[1,512,128,128]{3,2,1,0:T(8,128)(2,1)} %param.8, bf16[512,64,128]{2,1,0:T(8,128)(2,1)} %gather_fusion.1, pred[512]{0:T(512)(128)(4,1)S(1)} %compare_and_fusion), kind=kOutput, calls=%fused_computation.11 | convolution fusion | flops 1077936128 | bytes 41943552 | tf_op jit(solution)/shard_map/ksc,src->ksr/dot_general | solution.py:19
  414.3 27.8 %fusion.25 = f32[64,256,128]{1,2,0:T(8,128)} fusion(f32[64,512,128]{2,0,1:T(8,128)} %fusion.11, s32[512]{0:T(512)S(1)} %bitcast.54, pred[512]{0:T(512)(128)(4,1)S(1)} %iota_compare_fusion.1), kind=kOutput, calls=%fused_computation.24 | convolution fusion | flops 12885164032 | bytes 25168384 | tf_op jit(solution)/shard_map/is,ksr->kir/dot_general | solution.py:24
  442.1 9.2 %copy.13 = f32[64,256,128]{2,1,0:T(8,128)} copy(f32[64,256,128]{1,2,0:T(8,128)} %fusion.25) | data formatting | bytes 16777216 | tf_op jit(solution)/shard_map/is,ksr->kir/transpose | solution.py:24
  451.2 11.3 %copy.30 = f32[8,8,256,128]{3,1,2,0:T(8,128)} copy(f32[8,8,256,128]{3,2,1,0:T(8,128)} %bitcast.52) | data formatting | bytes 16777216
  462.6 0.0 reduce-scatter.2.cloned.1.call-update
  462.6 89.6 %reduce-scatter.2.cloned.1.call-done = f32[64,4096]{1,0:T(8,128)} async-done(((f32[64,32768]{1,0:T(8,128)}), f32[64,4096]{1,0:T(8,128)}) %reduce-scatter.2.cloned.1.call-update) | async-done | bytes 1048592 | tf_op jit(solution)/shard_map/reduce_scatter | solution.py:43
  (2 shorter events, 0.0 us)
Async XLA Ops:
  6.5 40.6 %all-gather.2.cloned.1.call-start = ((), (), s32[]{:S(2)}) async-start(), calls=%async_computation.1 | async-start | bytes 2621440 | tf_op jit(solution)/shard_map/all_gather | solution.py:38
  7.3 364.9 %all-reduce.3.cloned.1.call-start = ((), (), s32[]{:S(2)}) async-start(), calls=%async_computation.2 | async-start | bytes 4194304 | tf_op jit(solution)/shard_map/psum | solution.py:9
  62.8 20.5 %copy-start = (s32[1,512]{1,0:T(1,128)S(1)}, s32[1,512]{1,0:T(1,128)}, u32[]{:S(2)}) copy-start(s32[1,512]{1,0:T(1,128)} %param.9) | copy-start | bytes 6148
  304.6 247.6 %reduce-scatter.2.cloned.1.call-start = ((), (), s32[]{:S(2)}) async-start(), calls=%async_computation.3 | async-start | bytes 9437184 | tf_op jit(solution)/shard_map/reduce_scatter | solution.py:43
Sparse Core Ops, SparseCore 0:
  9.2 37.8 all-gather.1
  304.7 67.4 all-reduce.2
  462.7 89.4 reduce-scatter.1
where the time goes:
time: 565 us; the launch traced here: 559 us
  waiting for transfers between devices  196 us (35%)
  blocking collectives  170 us (30%)
  matrix products  96.5 us (17%)
  local copies, waits for them, and re-layouts  78.3 us (14%)
  between operations  14.1 us (2%)
    psum x1, blocking collectives, shards(): group_rows = lax.psum(first_part, 'col').astype(jnp.bfloat16)  170 us
    reduce_scatter x1, waiting for transfers between devices, shards(): return lax.psum_scatter(second_part, 'col', scatter_dimension=1, tiled=True)  89.6 us
    psum x1, waiting for transfers between devices, from_root(): return lax.psum(block, axis)  67.5 us
    dot_general x2, matrix products, block_product(): jnp.einsum('is,ksr->kir', owner_map.astype(jnp.float32), product, precisi...  55.6 us
    dot_general x2, matrix products, block_product(): jnp.einsum('ksc,src->ksr', picked, blocks[0], preferred_element_type=jnp....  40.9 us
    all_gather x1, waiting for transfers between devices, shards(): vec_panel = lax.all_gather(vectors, 'row', axis=1, tiled=True)  37.7 us
    gather x2, local copies, waits for them, and re-layouts, block_product(): picked = jnp.take(vec_tiles, block_cols.reshape(-1), axis=1)  35.1 us
    unnamed x4, local copies, waits for them, and re-layouts  22.7 us
  transfers between devices with their start and end apart: 3, of which 3 were waited for; matrix products, arithmetic and copies ran while one was open for 0% of the time, Pallas kernels for 0%

commit v1 on v0

v1 whole, which is shorter than its diff:
```python
import functools

import jax
import jax.numpy as jnp
from jax import lax
from jax.experimental import pallas as pl
from jax.experimental.pallas import tpu as pltpu
from jax.sharding import PartitionSpec as P

GROUP = 8
STEP = 32
TOP = 14.0
VMEM_LIMIT = 60 * 1024 * 1024

def message_rows(vec_width):
    return GROUP * vec_width + 16


def encode(tiles, ref):
    k = tiles[0].shape[0]
    exponents = []
    for i, tile in enumerate(tiles):
        peak = jnp.max(jnp.abs(tile), axis=0, keepdims=True)
        exponent = jnp.ceil(jnp.log2(jnp.maximum(peak, 1e-30)))
        scaled = jnp.round(tile * jnp.exp2(TOP - exponent))
        ref[i * k : (i + 1) * k, :] = scaled.astype(jnp.int32).astype(jnp.int16)
        exponents.append(exponent)
    rest = jnp.zeros((16 - len(tiles), tiles[0].shape[1]), jnp.float32)
    table = jnp.concatenate(exponents + [rest], axis=0)
    ref[len(tiles) * k :, :] = table.astype(jnp.int32).astype(jnp.int16)


def decoder(ref, k, factor=None):
    table = ref[GROUP * k :, :].astype(jnp.int32).astype(jnp.float32)
    scale = jnp.exp2(table - TOP)
    if factor is not None:
        scale = scale * factor

    def tile(i):
        codes = ref[i * k : (i + 1) * k, :].astype(jnp.int32).astype(jnp.float32)
        return codes * scale[i : i + 1, :]

    return tile


def product_kernel(places, shard, rows, cols, count, *refs):
    total = len(refs) - 12
    pieces = refs[:total]
    blocks, own, msg_low, msg_high, panel, held, acc, out, piece_sem, block_sem, own_sem, msg_sem = refs[total:]
    chips, groups = out.shape[:2]
    k = panel.shape[1]
    row_total = acc.shape[0] - 1
    slots = blocks.shape[0]
    n = count[0, 0]
    core = lax.axis_index("col") % 2
    row_owner = lax.axis_index("row")

    def piece_copy(i):
        piece, start, tiles, at = places[i]
        return pltpu.make_async_copy(
            pieces[piece].at[pl.ds(start, tiles)], panel.at[pl.ds(at(row_owner), tiles)], piece_sem.at[i]
        )

    def block_copy(i):
        span = pl.ds(i * STEP, STEP)
        return pltpu.make_async_copy(blocks.at[span], held.at[span], block_sem.at[i])

    for i in range(len(places)):
        piece_copy(i).start()
    for i in range(slots // STEP):

        @pl.when(i * STEP < n)
        def _():
            block_copy(i).start()

    @pl.loop(0, row_total + 1)
    def _(i):
        acc[i] = jnp.zeros_like(acc[0])

    for i in range(len(places)):
        piece_copy(i).wait()

    @pl.loop(0, (n + STEP - 1) // STEP)
    def _(step):
        block_copy(step).wait()
        base = step * STEP
        nil = jnp.zeros(panel.shape[1:], panel.dtype)
        products = []
        for u in range(0, STEP, 2):
            upper = jnp.concatenate([panel[cols[0, base + u]], nil], axis=1)
            lower = jnp.concatenate([nil, panel[cols[0, base + u + 1]]], axis=1)
            both = lax.dot_general(
                jnp.concatenate([upper, lower], axis=0),
                jnp.concatenate([held[base + u], held[base + u + 1]], axis=1),
                (((1,), (1,)), ((), ())),
                preferred_element_type=jnp.float32,
            )
            products += [both[:k], both[k:]]
        for u in range(STEP):
            at = jnp.where(base + u < n, rows[0, base + u], row_total)
            acc[at] += products[u]

    def own_copy(d):
        return pltpu.make_async_copy(
            acc.at[pl.ds((2 * d + core) * shard, shard)], own.at[d], own_sem.at[d]
        )

    def msg_copy(half, d):
        there = (msg_low, msg_high)[half].at[d]
        return pltpu.make_async_copy(out.at[d, pl.ds(half * (groups // 2), groups // 2)], there, msg_sem.at[half, d])

    for d in range(chips):
        own_copy(d).start()
    for half in range(2):
        for d in range(chips):
            base = (2 * d + 1 - core) * shard

            @pl.loop(half * (groups // 2), (half + 1) * (groups // 2))
            def _(g):
                tiles = [acc[base + g * GROUP + i] for i in range(GROUP)]
                encode(tiles, out.at[d, g])

            msg_copy(half, d).start()
    for d in range(chips):
        own_copy(d).wait()
        msg_copy(0, d).wait()
        msg_copy(1, d).wait()


def block_product(pieces, places, blocks, block_rows, block_cols, counts, shard, col_total):
    slots, order, _ = blocks.shape
    k = pieces[0].shape[1]
    chips = col_total // 2
    groups = shard // GROUP
    panel_tiles = sum(place[2] for place in places)
    scalars = pl.BlockSpec(memory_space=pltpu.SMEM)
    far = pl.BlockSpec(memory_space=pltpu.HBM)
    message = jax.ShapeDtypeStruct((chips, groups // 2, message_rows(k), order), jnp.int16)
    return pl.pallas_call(
        functools.partial(product_kernel, places, shard),
        out_shape=(jax.ShapeDtypeStruct((chips, shard, k, order), jnp.float32), message, message),
        in_specs=[scalars] * 3 + [far] * (len(pieces) + 1),
        out_specs=(far, far, far),
        scratch_shapes=[
            pltpu.VMEM((panel_tiles, k, order), jnp.bfloat16),
            pltpu.VMEM((slots, order, order), jnp.bfloat16),
            pltpu.VMEM((col_total * shard + 1, k, order), jnp.float32),
            pltpu.VMEM((chips, groups, message_rows(k), order), jnp.int16),
            pltpu.SemaphoreType.DMA((len(places),)),
            pltpu.SemaphoreType.DMA((slots // STEP,)),
            pltpu.SemaphoreType.DMA((chips,)),
            pltpu.SemaphoreType.DMA((2, chips)),
        ],
        compiler_params=pltpu.CompilerParams(vmem_limit_bytes=VMEM_LIMIT),
        name="block_product",
    )(block_rows, block_cols, counts, *pieces, blocks)


def combine_kernel(half, which, gates, form, own, sib, *refs):
    arrived = refs[: len(gates)]
    result, near_own, near, out, in_sem, out_sem = refs[-6:]
    groups, tiles, k, order = near_own.shape
    chip = lax.axis_index("col") // 2
    d = which(chip)
    first = half * groups

    def copies(g):
        sources = [sib.at[d, g]] + [ref.at[g] for ref in arrived]
        span = pl.ds((first + g) * tiles, tiles)
        return [pltpu.make_async_copy(own.at[d, span], near_own.at[g], in_sem.at[g, 0])] + [
            pltpu.make_async_copy(ref, near.at[i, g], in_sem.at[g, i + 1]) for i, ref in enumerate(sources)
        ]

    def out_copy(g):
        at = first + g
        if form == "message":
            there = result.at[g]
        elif form == "tiles":
            there = result.at[pl.ds(at * tiles, tiles)]
        else:
            there = result.at[:, pl.ds(at * tiles * order, tiles * order)]
        return pltpu.make_async_copy(out.at[g], there, out_sem.at[g])

    for g in range(groups):
        for copy in copies(g):
            copy.start()
    for g in range(groups):
        for copy in copies(g):
            copy.wait()
        parts = [decoder(near.at[0, g], k)]
        for i, gate in enumerate(gates):
            factor = None if gate is None else jnp.where(gate(chip), 1.0, 0.0)
            parts.append(decoder(near.at[i + 1, g], k, factor))
        sums = []
        for i in range(tiles):
            tile = near_own[g, i]
            for part in parts:
                tile = tile + part(i)
            if form == "message":
                sums.append(tile)
            elif form == "tiles":
                out[g, i] = tile.astype(out.dtype)
            else:
                out[g, :, i * order : (i + 1) * order] = tile
        if form == "message":
            encode(sums, out.at[g])
        out_copy(g).start()
    for g in range(groups):
        out_copy(g).wait()


def combine(half, which, own, sib, arrived, gates, form, into=None):
    _, shard, k, order = own.shape
    groups = sib.shape[1]
    rows = message_rows(k)
    far = pl.BlockSpec(memory_space=pltpu.HBM)
    if form == "message":
        out_shape = jax.ShapeDtypeStruct((groups, rows, order), jnp.int16)
        held = pltpu.VMEM((groups, rows, order), jnp.int16)
    elif form == "tiles":
        out_shape = jax.ShapeDtypeStruct((shard, k, order), jnp.bfloat16)
        held = pltpu.VMEM((groups, GROUP, k, order), jnp.bfloat16)
    else:
        out_shape = jax.ShapeDtypeStruct((k, shard * order), jnp.float32)
        held = pltpu.VMEM((groups, k, GROUP * order), jnp.float32)
    operands = (own, sib, *arrived) + (() if into is None else (into,))
    return pl.pallas_call(
        functools.partial(combine_kernel, half, which, gates, form),
        out_shape=out_shape,
        in_specs=[far] * len(operands),
        out_specs=far,
        input_output_aliases={} if into is None else {len(operands) - 1: 0},
        scratch_shapes=[
            pltpu.VMEM((groups, GROUP, k, order), jnp.float32),
            pltpu.VMEM((1 + len(arrived), groups, rows, order), jnp.int16),
            held,
            pltpu.SemaphoreType.DMA((groups, 2 + len(arrived))),
            pltpu.SemaphoreType.DMA((groups,)),
        ],
        name="combine_" + form,
    )(*operands)


def chip_moves(moves):
    return [(2 * a + core, 2 * b + core) for a, b in moves for core in range(2)]


def is_end(chip):
    return (chip == 0) | (chip == 3)


def is_inner(chip):
    return (chip == 1) | (chip == 2)


def line_sum(half, own, msg, form, into):
    chips = own.shape[0]
    sib = lax.ppermute(msg, "col", [(c, c ^ 1) for c in range(2 * chips)])
    if chips == 4:
        send = combine(half, lambda z: 3 - 3 * (z % 2), own, sib, (), (), "message")
        got_a = lax.ppermute(send, "col", chip_moves([(0, 1), (1, 0), (2, 3), (3, 2)]))
        send = combine(half, lambda z: z ^ 2, own, sib, (got_a,), (is_inner,), "message")
        got_b = lax.ppermute(send, "col", chip_moves([(0, 1), (3, 2), (1, 3), (2, 0)]))
        send = combine(half, lambda z: 1 + z % 2, own, sib, (got_b,), (is_inner,), "message")
        got_c = lax.ppermute(send, "col", chip_moves([(0, 1), (3, 2)]))
        got_d = lax.ppermute(send, "col", chip_moves([(1, 2), (2, 1)]))
        arrived, gates = (got_a, got_b, got_c, got_d), (is_end, is_end, None, None)
    else:
        arrived = ()
        for step in range(1, chips):
            send = combine(half, lambda z: (z + step) % chips, own, sib, (), (), "message")
            moves = chip_moves([(a, (a + step) % chips) for a in range(chips)])
            arrived += (lax.ppermute(send, "col", moves),)
        gates = (None,) * len(arrived)
    return combine(half, lambda z: z, own, sib, arrived, gates, form, into)


def sum_over_col(partial, form):
    own, low, high = partial
    return line_sum(1, own, high, form, line_sum(0, own, low, form, None))


def gather_square(low, high):
    across_x = [(r, r ^ 1) for r in range(4)]
    across_y = [(r, r ^ 2) for r in range(4)]
    y_low = lax.ppermute(low, "row", across_y)
    x_high = lax.ppermute(high, "row", across_x)
    x_low = lax.ppermute(low, "row", across_x)
    y_high = lax.ppermute(high, "row", across_y)
    far_low = lax.ppermute(y_low, "row", across_x)
    far_high = lax.ppermute(x_high, "row", across_y)
    return low, high, x_low, x_high, y_low, y_high, far_low, far_high


def vector_panel(tiles, row_total):
    shard = tiles.shape[0]
    if row_total != 4:
        whole = lax.all_gather(tiles, "row", axis=0, tiled=True)
        return (whole,), ((0, 0, row_total * shard, lambda r: 0),)
    half = shard // 2
    places = []
    for piece in range(8):
        at = lambda r, piece=piece: (r ^ (piece // 2)) * shard + piece % 2 * half
        places.append((piece, 0, half, at))
    return gather_square(tiles[:half], tiles[half:]), tuple(places)


def first_panel(tiles, row_total, col_total):
    shard = tiles.shape[0]
    if (row_total, col_total) != (4, 8):
        moves = []
        for s in range(row_total * col_total):
            moves.append((s, (s % row_total) * col_total + s // row_total))
        return vector_panel(lax.ppermute(tiles, ("row", "col"), moves), row_total)
    quarter = shard // 4
    place = lax.axis_index("col") % 4
    got = []
    for j in range(4):
        moves = []
        for r in range(4):
            for c in range(8):
                moves.append((r * 8 + c, (c % 4 ^ j) * 8 + 2 * r + c // 4))
        part = lax.dynamic_slice_in_dim(tiles, (place ^ j) * quarter, quarter, 0)
        got.append(lax.ppermute(part, ("row", "col"), moves))
    places = []
    for piece in range(8):
        for i in range(2):

            def at(r, flip=piece // 2, j=piece % 2 * 2 + i):
                owner = r ^ flip
                return (owner ^ j) * shard + owner * quarter

            places.append((piece, i * quarter, quarter, at))
    low, high = jnp.concatenate(got[:2], axis=0), jnp.concatenate(got[2:], axis=0)
    return gather_square(low, high), tuple(places)


def shards(row_total, col_total, vectors, blocks, block_rows, block_cols, counts):
    k, width = vectors.shape
    order = blocks.shape[2]
    shard = width // order
    matrix = (blocks[0], block_rows, block_cols, counts, shard, col_total)
    tiles = vectors.reshape(k, shard, order).transpose(1, 0, 2)
    first = sum_over_col(block_product(*vector_panel(tiles, row_total), *matrix), "tiles")
    return sum_over_col(block_product(*first_panel(first, row_total, col_total), *matrix), "rows")


def solution(mesh):
    in_specs = (
        P(None, ("col", "row")),
        P("row", "col", None, None),
        P("row", "col"),
        P("row", "col"),
        P("row", "col"),
    )
    out_specs = P(None, ("row", "col"))
    body = functools.partial(shards, mesh.shape["row"], mesh.shape["col"])
    return jax.shard_map(body, mesh=mesh, in_specs=in_specs, out_specs=out_specs, check_vma=False)
```

time: 565 us -> 205 us (0.36)
  the two profiles are of different devices: /device:TPU:0 before, /device:TPU:14 now
where the time goes in v1:
time: 205 us; the launch traced here: 206 us
  starting transfers between devices  76.9 us (38%)
  Pallas kernels  59.7 us (29%)
  waiting for transfers between devices  50.5 us (25%)
  local copies, waits for them, and re-layouts  18 us (9%)
    pallas_call x16, Pallas kernels, combine(): pl.pallas_call(functools.partial(combine_kernel, half, which, gates, form...  34.2 us
    pallas_call x2, Pallas kernels, block_product(): pl.pallas_call(functools.partial(product_kernel, places, shard), out_shap...  25.4 us
    ppermute x4, starting transfers between devices, line_sum(): lax.ppermute(send, 'col', chip_moves([(0, 1), (3, 2), (1, 3), (2, 0)]))  17.1 us
    unnamed x76, local copies, waits for them, and re-layouts  16.7 us
    ppermute x4, starting transfers between devices, line_sum(): got_d = lax.ppermute(send, 'col', chip_moves([(1, 2), (2, 1)]))  15.2 us
    ppermute x4, waiting for transfers between devices, first_panel(): got.append(lax.ppermute(part, ('row', 'col'), moves))  13.3 us
    ppermute x4, waiting for transfers between devices, line_sum(): lax.ppermute(send, 'col', chip_moves([(0, 1), (1, 0), (2, 3), (3, 2)]))  8.98 us
    ppermute x2, waiting for transfers between devices, gather_square(): far_low = lax.ppermute(y_low, 'row', across_x)  7.62 us
  transfers between devices with their start and end apart: 36, of which 18 were waited for; matrix products, arithmetic and copies ran while one was open for 0% of the time, Pallas kernels for 14%

profile of v1, /device:TPU:14, one launch (start us, length us, event | category | flops | bytes accessed | tf_op | source)
XLA Modules:
  0.0 206.3 jit_solution(4480890928755476574)
XLA Ops:
  2.4 1.5 collective-permute-start
  3.8 1.5 collective-permute-start.3
  5.4 5.1 %collective-permute-done.2.refs_4_ = bf16[16,64,128]{2,1,0:T(8,128)(2,1)S(1)} collective-permute-done((bf16[16,64,128]{2,1,0:T(8,128)(2,1)S(1)}, bf16[16,64,128]{2,1,0:T(8,128)(2,1)S(1)}, u32[]{:S(2)}, u32[]{:S(2)}) %collective-permute-start.2) | collective-permute-done | bytes 262176 | tf_op jit(solution)/shard_map/ppermute | solution.py:286
  13.2 3.4 %collective-permute-done.refs_2_ = bf16[16,64,128]{2,1,0:T(8,128)(2,1)S(1)} collective-permute-done((bf16[16,64,128]{2,1,0:T(8,128)(2,1)S(1)}, bf16[16,64,128]{2,1,0:T(8,128)(2,1)S(1)}, u32[]{:S(2)}, u32[]{:S(2)}) %collective-permute-start) | collective-permute-done | bytes 262176 | tf_op jit(solution)/shard_map/ppermute | solution.py:288
  16.6 4.2 %collective-permute-done.4.refs_6_ = bf16[16,64,128]{2,1,0:T(8,128)(2,1)S(1)} collective-permute-done((bf16[16,64,128]{2,1,0:T(8,128)(2,1)S(1)}, bf16[16,64,128]{2,1,0:T(8,128)(2,1)S(1)}, u32[]{:S(2)}, u32[]{:S(2)}) %collective-permute-start.4) | collective-permute-done | bytes 262176 | tf_op jit(solution)/shard_map/ppermute | solution.py:290
  21.7 12.7 %block_product.2 = (f32[4,32,64,128]{3,2,1,0:T(8,128)}, s16[4,2,528,128]{3,2,1,0:T(8,128)(2,1)}, s16[4,2,528,128]{3,2,1,0:T(8,128)(2,1)}) custom-call(s32[1,512]{1,0:T(1,128)} %rows.3, s32[1,512]{1,0:T(1,128)} %cols.3, s32[1,1]{1,0:T(1,128)S(6)} %copy.15.count, bf16[16,64,128]{2,1,0:T(8,128)(2,1)} %copy-done.14, bf16[16,64,128]{2,1,0:T(8,128)(2,1)} %copy-done.13, ...), custom_call_target="tpu_custom_call" | custom-call | tf_op jit(solution)/shard_map/block_product/pallas_call | solution.py:139
  35.0 2.4 %collective-permute-done.11.sib = s16[4,2,528,128]{3,2,1,0:T(8,128)(2,1)S(1)} collective-permute-done((s16[4,2,528,128]{3,2,1,0:T(8,128)(2,1)}, s16[4,2,528,128]{3,2,1,0:T(8,128)(2,1)S(1)}, u32[]{:S(2)}, u32[]{:S(2)}) %collective-permute-start.11) | collective-permute-done | bytes 1081376 | tf_op jit(solution)/shard_map/ppermute | solution.py:258
  38.4 1.9 combine_message.15
  40.3 3.0 %collective-permute-start.12 = (s16[2,528,128]{2,1,0:T(8,128)(2,1)}, s16[2,528,128]{2,1,0:T(8,128)(2,1)S(1)}, u32[]{:S(2)}, u32[]{:S(2)}) collective-permute-start(s16[2,528,128]{2,1,0:T(8,128)(2,1)} %combine_message.15), channel_id=1, source_target_pairs={{0,2},{1,3},{2,0},{3,1},{4,6},{5,7},{6,4},{7,5},{8,10},{9,11},{10,... | collective-permute-start | bytes 811016 | tf_op jit(solution)/shard_map/ppermute | solution.py:261
  44.3 1.9 combine_message.12
  46.4 4.5 %collective-permute-done.12.refs_0_ = s16[2,528,128]{2,1,0:T(8,128)(2,1)S(1)} collective-permute-done((s16[2,528,128]{2,1,0:T(8,128)(2,1)}, s16[2,528,128]{2,1,0:T(8,128)(2,1)S(1)}, u32[]{:S(2)}, u32[]{:S(2)}) %collective-permute-start.12) | collective-permute-done | bytes 270368 | tf_op jit(solution)/shard_map/ppermute | solution.py:261
  51.6 2.1 %combine_message.16 = s16[2,528,128]{2,1,0:T(8,128)(2,1)} custom-call(f32[4,32,64,128]{3,2,1,0:T(8,128)} %get-tuple-element.11.own, s16[4,2,528,128]{3,2,1,0:T(8,128)(2,1)} %copy-done.3, s16[2,528,128]{2,1,0:T(8,128)(2,1)} %copy-done.11), custom_call_target="tpu_custom_call" | custom-call | tf_op jit(solution)/shard_map/combine_message/pallas_call | solution.py:227
  53.7 3.1 %collective-permute-start.13 = (s16[2,528,128]{2,1,0:T(8,128)(2,1)}, s16[2,528,128]{2,1,0:T(8,128)(2,1)S(1)}, u32[]{:S(2)}, u32[]{:S(2)}) collective-permute-start(s16[2,528,128]{2,1,0:T(8,128)(2,1)} %combine_message.16), channel_id=1, source_target_pairs={{0,2},{1,3},{6,4},{7,5},{2,6},{3,7},{4,0},{5,1},{8,10},{9,11},{14,... | collective-permute-start | bytes 811016 | tf_op jit(solution)/shard_map/ppermute | solution.py:263
  57.5 2.1 %combine_message.13 = s16[2,528,128]{2,1,0:T(8,128)(2,1)} custom-call(f32[4,32,64,128]{3,2,1,0:T(8,128)} %get-tuple-element.11.own, s16[4,2,528,128]{3,2,1,0:T(8,128)(2,1)} %copy-done.1, s16[2,528,128]{2,1,0:T(8,128)(2,1)} %copy-done.5), custom_call_target="tpu_custom_call" | custom-call | tf_op jit(solution)/shard_map/combine_message/pallas_call | solution.py:227
  59.6 2.6 %collective-permute-start.8 = (s16[2,528,128]{2,1,0:T(8,128)(2,1)}, s16[2,528,128]{2,1,0:T(8,128)(2,1)S(1)}, u32[]{:S(2)}, u32[]{:S(2)}) collective-permute-start(s16[2,528,128]{2,1,0:T(8,128)(2,1)} %combine_message.13), channel_id=1, source_target_pairs={{0,2},{1,3},{6,4},{7,5},{2,6},{3,7},{4,0},{5,1},{8,10},{9,11},{14,... | collective-permute-start | bytes 811016 | tf_op jit(solution)/shard_map/ppermute | solution.py:263
  63.2 2.1 %combine_message.17 = s16[2,528,128]{2,1,0:T(8,128)(2,1)} custom-call(f32[4,32,64,128]{3,2,1,0:T(8,128)} %get-tuple-element.11.own, s16[4,2,528,128]{3,2,1,0:T(8,128)(2,1)} %copy-done.3, s16[2,528,128]{2,1,0:T(8,128)(2,1)} %copy-done.12), custom_call_target="tpu_custom_call" | custom-call | tf_op jit(solution)/shard_map/combine_message/pallas_call | solution.py:227
  66.6 5.5 %collective-permute-start.15 = (s16[2,528,128]{2,1,0:T(8,128)(2,1)}, s16[2,528,128]{2,1,0:T(8,128)(2,1)S(1)}, u32[]{:S(2)}, u32[]{:S(2)}) collective-permute-start(s16[2,528,128]{2,1,0:T(8,128)(2,1)} %combine_message.17), channel_id=1, source_target_pairs={{2,4},{3,5},{4,2},{5,3},{10,12},{11,13},{12,10},{13,11},{18,20},{1... | collective-permute-start | bytes 811016 | tf_op jit(solution)/shard_map/ppermute | solution.py:266
  72.9 2.1 %combine_message.14 = s16[2,528,128]{2,1,0:T(8,128)(2,1)} custom-call(f32[4,32,64,128]{3,2,1,0:T(8,128)} %get-tuple-element.11.own, s16[4,2,528,128]{3,2,1,0:T(8,128)(2,1)} %copy-done.1, s16[2,528,128]{2,1,0:T(8,128)(2,1)} %copy-done.6), custom_call_target="tpu_custom_call" | custom-call | tf_op jit(solution)/shard_map/combine_message/pallas_call | solution.py:227
  74.9 1.9 collective-permute-start.10
  79.7 2.4 %combine_tiles.2.refs_4_ = bf16[32,64,128]{2,1,0:T(8,128)(2,1)} custom-call(f32[4,32,64,128]{3,2,1,0:T(8,128)} %get-tuple-element.11.own, s16[4,2,528,128]{3,2,1,0:T(8,128)(2,1)} %copy-done.3, s16[2,528,128]{2,1,0:T(8,128)(2,1)} %copy-done.11, s16[2,528,128]{2,1,0:T(8,128)(2,1)} %copy-done.12, s16[2,528,128]{2,1,0:T(8,128)(2,1)} %copy-done.23, ...), custom_call_target="tpu_custom_call" | custom-call | tf_op jit(solution)/shard_map/combine_tiles/pallas_call | solution.py:227
  83.5 1.9 collective-permute-done.9.refs_2_
  86.2 2.4 %combine_tiles.3 = bf16[32,64,128]{2,1,0:T(8,128)(2,1)} custom-call(f32[4,32,64,128]{3,2,1,0:T(8,128)} %get-tuple-element.11.own, s16[4,2,528,128]{3,2,1,0:T(8,128)(2,1)} %copy-done.1, s16[2,528,128]{2,1,0:T(8,128)(2,1)} %copy-done.5, s16[2,528,128]{2,1,0:T(8,128)(2,1)} %copy-done.6, s16[2,528,128]{2,1,0:T(8,128)(2,1)} %copy-done.18, ...), custom_call_target="tpu_custom_call", output_to_operand_aliasing={{}: (6, {})} | custom-call | tf_op jit(solution)/shard_map/combine_tiles/pallas_call | solution.py:227
  89.8 1.9 collective-permute-start.19
  91.7 3.7 %collective-permute-start.16 = (bf16[8,64,128]{2,1,0:T(8,128)(2,1)S(1)}, bf16[8,64,128]{2,1,0:T(8,128)(2,1)S(1)}, u32[]{:S(2)}, u32[]{:S(2)}) collective-permute-start(bf16[8,64,128]{2,1,0:T(8,128)(2,1)S(1)} %get-tuple-element.20), channel_id=1, source_target_pairs={{0,0},{1,8},{2,16},{3,24},{4,1},{5,9},{6,17},{7,25},{8,2},{9,10},{... | collective-permute-start | bytes 393224 | tf_op jit(solution)/shard_map/ppermute | solution.py:324
  96.5 10.2 %collective-permute-done.19 = bf16[8,64,128]{2,1,0:T(8,128)(2,1)S(1)} collective-permute-done((bf16[8,64,128]{2,1,0:T(8,128)(2,1)S(1)}, bf16[8,64,128]{2,1,0:T(8,128)(2,1)S(1)}, u32[]{:S(2)}, u32[]{:S(2)}) %collective-permute-start.19) | collective-permute-done | bytes 131104 | tf_op jit(solution)/shard_map/ppermute | solution.py:324
  106.7 2.1 %collective-permute-start.21 = (bf16[16,64,128]{2,1,0:T(8,128)(2,1)S(1)}, bf16[16,64,128]{2,1,0:T(8,128)(2,1)S(1)}, u32[]{:S(2)}, u32[]{:S(2)}) collective-permute-start(bf16[16,64,128]{2,1,0:T(8,128)(2,1)S(1)} %constant_dynamic-update-slice_fusion.2.refs_1_), channel_id=1, source_target_pairs={{0,8},{8,0},{16,24},{24,16},{1,9},{9,1},{17,25},{25,17},{2,10},{10... | collective-permute-start | bytes 786440 | tf_op jit(solution)/shard_map/ppermute | solution.py:287
  109.5 1.5 collective-permute-done.17
  111.1 5.5 %collective-permute-start.22 = (bf16[16,64,128]{2,1,0:T(8,128)(2,1)S(1)}, bf16[16,64,128]{2,1,0:T(8,128)(2,1)S(1)}, u32[]{:S(2)}, u32[]{:S(2)}) collective-permute-start(bf16[16,64,128]{2,1,0:T(8,128)(2,1)S(1)} %constant_dynamic-update-slice_fusion.refs_0_), channel_id=1, source_target_pairs={{0,16},{8,24},{16,0},{24,8},{1,17},{9,25},{17,1},{25,9},{2,18},{10... | collective-permute-start | bytes 786440 | tf_op jit(solution)/shard_map/ppermute | solution.py:286
  116.6 4.8 %collective-permute-start.20 = (bf16[16,64,128]{2,1,0:T(8,128)(2,1)S(1)}, bf16[16,64,128]{2,1,0:T(8,128)(2,1)S(1)}, u32[]{:S(2)}, u32[]{:S(2)}) collective-permute-start(bf16[16,64,128]{2,1,0:T(8,128)(2,1)S(1)} %constant_dynamic-update-slice_fusion.refs_0_), channel_id=1, source_target_pairs={{0,8},{8,0},{16,24},{24,16},{1,9},{9,1},{17,25},{25,17},{2,10},{10... | collective-permute-start | bytes 786440 | tf_op jit(solution)/shard_map/ppermute | solution.py:288
  121.4 1.9 collective-permute-start.25
  123.3 5.1 %collective-permute-start.24 = (bf16[16,64,128]{2,1,0:T(8,128)(2,1)S(1)}, bf16[16,64,128]{2,1,0:T(8,128)(2,1)S(1)}, u32[]{:S(2)}, u32[]{:S(2)}) collective-permute-start(bf16[16,64,128]{2,1,0:T(8,128)(2,1)S(1)} %collective-permute-done.22.refs_4_), channel_id=1, source_target_pairs={{0,8},{8,0},{16,24},{24,16},{1,9},{9,1},{17,25},{25,17},{2,10},{10... | collective-permute-start | bytes 786440 | tf_op jit(solution)/shard_map/ppermute | solution.py:290
  129.4 3.4 %collective-permute-done.24.refs_6_ = bf16[16,64,128]{2,1,0:T(8,128)(2,1)S(1)} collective-permute-done((bf16[16,64,128]{2,1,0:T(8,128)(2,1)S(1)}, bf16[16,64,128]{2,1,0:T(8,128)(2,1)S(1)}, u32[]{:S(2)}, u32[]{:S(2)}) %collective-permute-start.24) | collective-permute-done | bytes 262176 | tf_op jit(solution)/shard_map/ppermute | solution.py:290
  133.6 12.8 %block_product.3 = (f32[4,32,64,128]{3,2,1,0:T(8,128)}, s16[4,2,528,128]{3,2,1,0:T(8,128)(2,1)}, s16[4,2,528,128]{3,2,1,0:T(8,128)(2,1)}) custom-call(s32[1,512]{1,0:T(1,128)} %rows.3, s32[1,512]{1,0:T(1,128)} %cols.3, s32[1,1]{1,0:T(1,128)S(6)} %copy.15.count, bf16[16,64,128]{2,1,0:T(8,128)(2,1)} %copy-done.16, bf16[16,64,128]{2,1,0:T(8,128)(2,1)} %copy-done.15, ...), custom_call_target="tpu_custom_call" | custom-call | tf_op jit(solution)/shard_map/block_product/pallas_call | solution.py:139
  146.9 2.4 %collective-permute-done.31.sib = s16[4,2,528,128]{3,2,1,0:T(8,128)(2,1)S(1)} collective-permute-done((s16[4,2,528,128]{3,2,1,0:T(8,128)(2,1)}, s16[4,2,528,128]{3,2,1,0:T(8,128)(2,1)S(1)}, u32[]{:S(2)}, u32[]{:S(2)}) %collective-permute-start.31) | collective-permute-done | bytes 1081376 | tf_op jit(solution)/shard_map/ppermute | solution.py:258
  150.3 1.9 combine_message.21
  152.3 3.7 %collective-permute-start.32 = (s16[2,528,128]{2,1,0:T(8,128)(2,1)}, s16[2,528,128]{2,1,0:T(8,128)(2,1)S(1)}, u32[]{:S(2)}, u32[]{:S(2)}) collective-permute-start(s16[2,528,128]{2,1,0:T(8,128)(2,1)} %combine_message.21), channel_id=1, source_target_pairs={{0,2},{1,3},{2,0},{3,1},{4,6},{5,7},{6,4},{7,5},{8,10},{9,11},{10,... | collective-permute-start | bytes 811016 | tf_op jit(solution)/shard_map/ppermute | solution.py:261
  157.0 1.9 combine_message.18
  159.0 4.5 %collective-permute-done.32.refs_0_ = s16[2,528,128]{2,1,0:T(8,128)(2,1)S(1)} collective-permute-done((s16[2,528,128]{2,1,0:T(8,128)(2,1)}, s16[2,528,128]{2,1,0:T(8,128)(2,1)S(1)}, u32[]{:S(2)}, u32[]{:S(2)}) %collective-permute-start.32) | collective-permute-done | bytes 270368 | tf_op jit(solution)/shard_map/ppermute | solution.py:261
  164.2 2.1 %combine_message.22 = s16[2,528,128]{2,1,0:T(8,128)(2,1)} custom-call(f32[4,32,64,128]{3,2,1,0:T(8,128)} %get-tuple-element.14.own, s16[4,2,528,128]{3,2,1,0:T(8,128)(2,1)} %copy-done.2, s16[2,528,128]{2,1,0:T(8,128)(2,1)} %copy-done.7), custom_call_target="tpu_custom_call" | custom-call | tf_op jit(solution)/shard_map/combine_message/pallas_call | solution.py:227
  166.3 8.8 %collective-permute-start.33 = (s16[2,528,128]{2,1,0:T(8,128)(2,1)}, s16[2,528,128]{2,1,0:T(8,128)(2,1)S(1)}, u32[]{:S(2)}, u32[]{:S(2)}) collective-permute-start(s16[2,528,128]{2,1,0:T(8,128)(2,1)} %combine_message.22), channel_id=1, source_target_pairs={{0,2},{1,3},{6,4},{7,5},{2,6},{3,7},{4,0},{5,1},{8,10},{9,11},{14,... | collective-permute-start | bytes 811016 | tf_op jit(solution)/shard_map/ppermute | solution.py:263
  175.8 2.1 %combine_message.19 = s16[2,528,128]{2,1,0:T(8,128)(2,1)} custom-call(f32[4,32,64,128]{3,2,1,0:T(8,128)} %get-tuple-element.14.own, s16[4,2,528,128]{3,2,1,0:T(8,128)(2,1)} %copy-done.4, s16[2,528,128]{2,1,0:T(8,128)(2,1)} %copy-done.9), custom_call_target="tpu_custom_call" | custom-call | tf_op jit(solution)/shard_map/combine_message/pallas_call | solution.py:227
  177.9 2.6 %collective-permute-start.28 = (s16[2,528,128]{2,1,0:T(8,128)(2,1)}, s16[2,528,128]{2,1,0:T(8,128)(2,1)S(1)}, u32[]{:S(2)}, u32[]{:S(2)}) collective-permute-start(s16[2,528,128]{2,1,0:T(8,128)(2,1)} %combine_message.19), channel_id=1, source_target_pairs={{0,2},{1,3},{6,4},{7,5},{2,6},{3,7},{4,0},{5,1},{8,10},{9,11},{14,... | collective-permute-start | bytes 811016 | tf_op jit(solution)/shard_map/ppermute | solution.py:263
  181.3 2.1 %combine_message.23 = s16[2,528,128]{2,1,0:T(8,128)(2,1)} custom-call(f32[4,32,64,128]{3,2,1,0:T(8,128)} %get-tuple-element.14.own, s16[4,2,528,128]{3,2,1,0:T(8,128)(2,1)} %copy-done.2, s16[2,528,128]{2,1,0:T(8,128)(2,1)} %copy-done.8), custom_call_target="tpu_custom_call" | custom-call | tf_op jit(solution)/shard_map/combine_message/pallas_call | solution.py:227
  184.7 5.8 %collective-permute-start.35 = (s16[2,528,128]{2,1,0:T(8,128)(2,1)}, s16[2,528,128]{2,1,0:T(8,128)(2,1)S(1)}, u32[]{:S(2)}, u32[]{:S(2)}) collective-permute-start(s16[2,528,128]{2,1,0:T(8,128)(2,1)} %combine_message.23), channel_id=1, source_target_pairs={{2,4},{3,5},{4,2},{5,3},{10,12},{11,13},{12,10},{13,11},{18,20},{1... | collective-permute-start | bytes 811016 | tf_op jit(solution)/shard_map/ppermute | solution.py:266
  191.2 2.1 %combine_message.20 = s16[2,528,128]{2,1,0:T(8,128)(2,1)} custom-call(f32[4,32,64,128]{3,2,1,0:T(8,128)} %get-tuple-element.14.own, s16[4,2,528,128]{3,2,1,0:T(8,128)(2,1)} %copy-done.4, s16[2,528,128]{2,1,0:T(8,128)(2,1)} %copy-done.10), custom_call_target="tpu_custom_call" | custom-call | tf_op jit(solution)/shard_map/combine_message/pallas_call | solution.py:227
  194.6 1.9 collective-permute-start.30
  198.0 2.5 %combine_rows.2.refs_4_ = f32[64,4096]{1,0:T(8,128)} custom-call(f32[4,32,64,128]{3,2,1,0:T(8,128)} %get-tuple-element.14.own, s16[4,2,528,128]{3,2,1,0:T(8,128)(2,1)} %copy-done.2, s16[2,528,128]{2,1,0:T(8,128)(2,1)} %copy-done.7, s16[2,528,128]{2,1,0:T(8,128)(2,1)} %copy-done.8, s16[2,528,128]{2,1,0:T(8,128)(2,1)} %copy-done.19, s16[2,528,128]{2,1,0:T(8,128)(2,1)} %copy-done.20), custom_call_target="tpu_custom_call" | custom-call | tf_op jit(solution)/shard_map/combine_rows/pallas_call | solution.py:227
  203.9 2.5 %combine_rows.3 = f32[64,4096]{1,0:T(8,128)} custom-call(f32[4,32,64,128]{3,2,1,0:T(8,128)} %get-tuple-element.14.own, s16[4,2,528,128]{3,2,1,0:T(8,128)(2,1)} %copy-done.4, s16[2,528,128]{2,1,0:T(8,128)(2,1)} %copy-done.9, s16[2,528,128]{2,1,0:T(8,128)(2,1)} %copy-done.10, s16[2,528,128]{2,1,0:T(8,128)(2,1)} %copy-done.21, ...), custom_call_target="tpu_custom_call", output_to_operand_aliasing={{}: (6, {})} | custom-call | tf_op jit(solution)/shard_map/combine_rows/pallas_call | solution.py:227
  (123 shorter events, 34.8 us)
Async XLA Ops:
  1.2 19.6 %copy-start.13 = (bf16[16,64,128]{2,1,0:T(8,128)(2,1)}, bf16[16,64,128]{2,1,0:T(8,128)(2,1)S(1)}, u32[]{:S(2)}) copy-start(bf16[16,64,128]{2,1,0:T(8,128)(2,1)S(1)} %get-tuple-element.21.refs_1_) | copy-start | bytes 786436
  1.2 19.6 %copy-start.14 = (bf16[16,64,128]{2,1,0:T(8,128)(2,1)}, bf16[16,64,128]{2,1,0:T(8,128)(2,1)S(1)}, u32[]{:S(2)}) copy-start(bf16[16,64,128]{2,1,0:T(8,128)(2,1)S(1)} %get-tuple-element.22.refs_0_) | copy-start | bytes 786436
  1.2 9.2 %collective-permute-start.2 = (bf16[16,64,128]{2,1,0:T(8,128)(2,1)S(1)}, bf16[16,64,128]{2,1,0:T(8,128)(2,1)S(1)}, u32[]{:S(2)}, u32[]{:S(2)}) collective-permute-start(bf16[16,64,128]{2,1,0:T(8,128)(2,1)S(1)} %get-tuple-element.22.refs_0_), channel_id=1, source_target_pairs={{0,16},{8,24},{16,0},{24,8},{1,17},{9,25},{17,1},{25,9},{2,18},{10... | collective-permute-start | bytes 786440 | tf_op jit(solution)/shard_map/ppermute | solution.py:286
  1.8 9.2 %collective-permute-start.1 = (bf16[16,64,128]{2,1,0:T(8,128)(2,1)S(1)}, bf16[16,64,128]{2,1,0:T(8,128)(2,1)S(1)}, u32[]{:S(2)}, u32[]{:S(2)}) collective-permute-start(bf16[16,64,128]{2,1,0:T(8,128)(2,1)S(1)} %get-tuple-element.21.refs_1_), channel_id=1, source_target_pairs={{0,8},{8,0},{16,24},{24,16},{1,9},{9,1},{17,25},{25,17},{2,10},{10... | collective-permute-start | bytes 786440 | tf_op jit(solution)/shard_map/ppermute | solution.py:287
  2.4 14.3 %collective-permute-start = (bf16[16,64,128]{2,1,0:T(8,128)(2,1)S(1)}, bf16[16,64,128]{2,1,0:T(8,128)(2,1)S(1)}, u32[]{:S(2)}, u32[]{:S(2)}) collective-permute-start(bf16[16,64,128]{2,1,0:T(8,128)(2,1)S(1)} %get-tuple-element.22.refs_0_), channel_id=1, source_target_pairs={{0,8},{8,0},{16,24},{24,16},{1,9},{9,1},{17,25},{25,17},{2,10},{10... | collective-permute-start | bytes 786440 | tf_op jit(solution)/shard_map/ppermute | solution.py:288
  3.8 12.8 %collective-permute-start.3 = (bf16[16,64,128]{2,1,0:T(8,128)(2,1)S(1)}, bf16[16,64,128]{2,1,0:T(8,128)(2,1)S(1)}, u32[]{:S(2)}, u32[]{:S(2)}) collective-permute-start(bf16[16,64,128]{2,1,0:T(8,128)(2,1)S(1)} %get-tuple-element.21.refs_1_), channel_id=1, source_target_pairs={{0,16},{8,24},{16,0},{24,8},{1,17},{9,25},{17,1},{25,9},{2,18},{10... | collective-permute-start | bytes 786440 | tf_op jit(solution)/shard_map/ppermute | solution.py:289
  10.5 10.4 %copy-start.26 = (bf16[16,64,128]{2,1,0:T(8,128)(2,1)}, bf16[16,64,128]{2,1,0:T(8,128)(2,1)S(1)}, u32[]{:S(2)}) copy-start(bf16[16,64,128]{2,1,0:T(8,128)(2,1)S(1)} %collective-permute-done.2.refs_4_) | copy-start | bytes 786436
  10.5 10.3 %collective-permute-start.4 = (bf16[16,64,128]{2,1,0:T(8,128)(2,1)S(1)}, bf16[16,64,128]{2,1,0:T(8,128)(2,1)S(1)}, u32[]{:S(2)}, u32[]{:S(2)}) collective-permute-start(bf16[16,64,128]{2,1,0:T(8,128)(2,1)S(1)} %collective-permute-done.2.refs_4_), channel_id=1, source_target_pairs={{0,8},{8,0},{16,24},{24,16},{1,9},{9,1},{17,25},{25,17},{2,10},{10... | collective-permute-start | bytes 786440 | tf_op jit(solution)/shard_map/ppermute | solution.py:290
  11.0 9.8 %copy-start.27 = (bf16[16,64,128]{2,1,0:T(8,128)(2,1)}, bf16[16,64,128]{2,1,0:T(8,128)(2,1)S(1)}, u32[]{:S(2)}) copy-start(bf16[16,64,128]{2,1,0:T(8,128)(2,1)S(1)} %collective-permute-done.1.refs_3_) | copy-start | bytes 786436
  11.0 9.8 %collective-permute-start.5 = (bf16[16,64,128]{2,1,0:T(8,128)(2,1)S(1)}, bf16[16,64,128]{2,1,0:T(8,128)(2,1)S(1)}, u32[]{:S(2)}, u32[]{:S(2)}) collective-permute-start(bf16[16,64,128]{2,1,0:T(8,128)(2,1)S(1)} %collective-permute-done.1.refs_3_), channel_id=1, source_target_pairs={{0,16},{8,24},{16,0},{24,8},{1,17},{9,25},{17,1},{25,9},{2,18},{10... | collective-permute-start | bytes 786440 | tf_op jit(solution)/shard_map/ppermute | solution.py:291
  16.6 4.3 %copy-start.29 = (bf16[16,64,128]{2,1,0:T(8,128)(2,1)}, bf16[16,64,128]{2,1,0:T(8,128)(2,1)S(1)}, u32[]{:S(2)}) copy-start(bf16[16,64,128]{2,1,0:T(8,128)(2,1)S(1)} %collective-permute-done.refs_2_) | copy-start | bytes 786436
  16.6 4.3 %copy-start.31 = (bf16[16,64,128]{2,1,0:T(8,128)(2,1)}, bf16[16,64,128]{2,1,0:T(8,128)(2,1)S(1)}, u32[]{:S(2)}) copy-start(bf16[16,64,128]{2,1,0:T(8,128)(2,1)S(1)} %collective-permute-done.3.refs_5_) | copy-start | bytes 786436
  34.4 3.0 %collective-permute-start.11 = (s16[4,2,528,128]{3,2,1,0:T(8,128)(2,1)}, s16[4,2,528,128]{3,2,1,0:T(8,128)(2,1)S(1)}, u32[]{:S(2)}, u32[]{:S(2)}) collective-permute-start(s16[4,2,528,128]{3,2,1,0:T(8,128)(2,1)} %get-tuple-element.13), channel_id=1, source_target_pairs={{0,1},{1,0},{2,3},{3,2},{4,5},{5,4},{6,7},{7,6},{8,9},{9,8},{10,11... | collective-permute-start | bytes 3244040 | tf_op jit(solution)/shard_map/ppermute | solution.py:258
  34.7 8.7 %collective-permute-start.6 = (s16[4,2,528,128]{3,2,1,0:T(8,128)(2,1)}, s16[4,2,528,128]{3,2,1,0:T(8,128)(2,1)S(1)}, u32[]{:S(2)}, u32[]{:S(2)}) collective-permute-start(s16[4,2,528,128]{3,2,1,0:T(8,128)(2,1)} %get-tuple-element.12), channel_id=1, source_target_pairs={{0,1},{1,0},{2,3},{3,2},{4,5},{5,4},{6,7},{7,6},{8,9},{9,8},{10,11... | collective-permute-start | bytes 3244040 | tf_op jit(solution)/shard_map/ppermute | solution.py:258
  40.3 10.6 %collective-permute-start.12 = (s16[2,528,128]{2,1,0:T(8,128)(2,1)}, s16[2,528,128]{2,1,0:T(8,128)(2,1)S(1)}, u32[]{:S(2)}, u32[]{:S(2)}) collective-permute-start(s16[2,528,128]{2,1,0:T(8,128)(2,1)} %combine_message.15), channel_id=1, source_target_pairs={{0,2},{1,3},{2,0},{3,1},{4,6},{5,7},{6,4},{7,5},{8,10},{9,11},{10,... | collective-permute-start | bytes 811016 | tf_op jit(solution)/shard_map/ppermute | solution.py:261
  46.3 10.5 %collective-permute-start.7 = (s16[2,528,128]{2,1,0:T(8,128)(2,1)}, s16[2,528,128]{2,1,0:T(8,128)(2,1)S(1)}, u32[]{:S(2)}, u32[]{:S(2)}) collective-permute-start(s16[2,528,128]{2,1,0:T(8,128)(2,1)} %combine_message.12), channel_id=1, source_target_pairs={{0,2},{1,3},{2,0},{3,1},{4,6},{5,7},{6,4},{7,5},{8,10},{9,11},{10,... | collective-permute-start | bytes 811016 | tf_op jit(solution)/shard_map/ppermute | solution.py:261
  53.7 8.8 %collective-permute-start.13 = (s16[2,528,128]{2,1,0:T(8,128)(2,1)}, s16[2,528,128]{2,1,0:T(8,128)(2,1)S(1)}, u32[]{:S(2)}, u32[]{:S(2)}) collective-permute-start(s16[2,528,128]{2,1,0:T(8,128)(2,1)} %combine_message.16), channel_id=1, source_target_pairs={{0,2},{1,3},{6,4},{7,5},{2,6},{3,7},{4,0},{5,1},{8,10},{9,11},{14,... | collective-permute-start | bytes 811016 | tf_op jit(solution)/shard_map/ppermute | solution.py:263
  59.6 12.5 %collective-permute-start.8 = (s16[2,528,128]{2,1,0:T(8,128)(2,1)}, s16[2,528,128]{2,1,0:T(8,128)(2,1)S(1)}, u32[]{:S(2)}, u32[]{:S(2)}) collective-permute-start(s16[2,528,128]{2,1,0:T(8,128)(2,1)} %combine_message.13), channel_id=1, source_target_pairs={{0,2},{1,3},{6,4},{7,5},{2,6},{3,7},{4,0},{5,1},{8,10},{9,11},{14,... | collective-permute-start | bytes 811016 | tf_op jit(solution)/shard_map/ppermute | solution.py:263
  65.3 12.9 %collective-permute-start.14 = (s16[2,528,128]{2,1,0:T(8,128)(2,1)}, s16[2,528,128]{2,1,0:T(8,128)(2,1)S(1)}, u32[]{:S(2)}, u32[]{:S(2)}) collective-permute-start(s16[2,528,128]{2,1,0:T(8,128)(2,1)} %combine_message.17), channel_id=1, source_target_pairs={{0,2},{1,3},{6,4},{7,5},{8,10},{9,11},{14,12},{15,13},{16,18},{17,... | collective-permute-start | bytes 811016 | tf_op jit(solution)/shard_map/ppermute | solution.py:265
  66.6 11.6 %collective-permute-start.15 = (s16[2,528,128]{2,1,0:T(8,128)(2,1)}, s16[2,528,128]{2,1,0:T(8,128)(2,1)S(1)}, u32[]{:S(2)}, u32[]{:S(2)}) collective-permute-start(s16[2,528,128]{2,1,0:T(8,128)(2,1)} %combine_message.17), channel_id=1, source_target_pairs={{2,4},{3,5},{4,2},{5,3},{10,12},{11,13},{12,10},{13,11},{18,20},{1... | collective-permute-start | bytes 811016 | tf_op jit(solution)/shard_map/ppermute | solution.py:266
  74.9 8.6 %collective-permute-start.10 = (s16[2,528,128]{2,1,0:T(8,128)(2,1)}, s16[2,528,128]{2,1,0:T(8,128)(2,1)S(1)}, u32[]{:S(2)}, u32[]{:S(2)}) collective-permute-start(s16[2,528,128]{2,1,0:T(8,128)(2,1)} %combine_message.14), channel_id=1, source_target_pairs={{2,4},{3,5},{4,2},{5,3},{10,12},{11,13},{12,10},{13,11},{18,20},{1... | collective-permute-start | bytes 811016 | tf_op jit(solution)/shard_map/ppermute | solution.py:266
  76.9 8.6 %collective-permute-start.9 = (s16[2,528,128]{2,1,0:T(8,128)(2,1)}, s16[2,528,128]{2,1,0:T(8,128)(2,1)S(1)}, u32[]{:S(2)}, u32[]{:S(2)}) collective-permute-start(s16[2,528,128]{2,1,0:T(8,128)(2,1)} %combine_message.14), channel_id=1, source_target_pairs={{0,2},{1,3},{6,4},{7,5},{8,10},{9,11},{14,12},{15,13},{16,18},{17,... | collective-permute-start | bytes 811016 | tf_op jit(solution)/shard_map/ppermute | solution.py:265
  89.7 6.7 %collective-permute-start.18 = (bf16[8,64,128]{2,1,0:T(8,128)(2,1)S(1)}, bf16[8,64,128]{2,1,0:T(8,128)(2,1)S(1)}, u32[]{:S(2)}, u32[]{:S(2)}) collective-permute-start(bf16[8,64,128]{2,1,0:T(8,128)(2,1)S(1)} %get-tuple-element.18), channel_id=1, source_target_pairs={{0,16},{1,24},{2,0},{3,8},{4,17},{5,25},{6,1},{7,9},{8,18},{9,26},... | collective-permute-start | bytes 393224 | tf_op jit(solution)/shard_map/ppermute | solution.py:324
  89.8 16.9 %collective-permute-start.19 = (bf16[8,64,128]{2,1,0:T(8,128)(2,1)S(1)}, bf16[8,64,128]{2,1,0:T(8,128)(2,1)S(1)}, u32[]{:S(2)}, u32[]{:S(2)}) collective-permute-start(bf16[8,64,128]{2,1,0:T(8,128)(2,1)S(1)} %get-tuple-element.17), channel_id=1, source_target_pairs={{0,24},{1,16},{2,8},{3,0},{4,25},{5,17},{6,9},{7,1},{8,26},{9,18},... | collective-permute-start | bytes 393224 | tf_op jit(solution)/shard_map/ppermute | solution.py:324
  91.7 17.8 %collective-permute-start.16 = (bf16[8,64,128]{2,1,0:T(8,128)(2,1)S(1)}, bf16[8,64,128]{2,1,0:T(8,128)(2,1)S(1)}, u32[]{:S(2)}, u32[]{:S(2)}) collective-permute-start(bf16[8,64,128]{2,1,0:T(8,128)(2,1)S(1)} %get-tuple-element.20), channel_id=1, source_target_pairs={{0,0},{1,8},{2,16},{3,24},{4,1},{5,9},{6,17},{7,25},{8,2},{9,10},{... | collective-permute-start | bytes 393224 | tf_op jit(solution)/shard_map/ppermute | solution.py:324
  95.5 15.6 %collective-permute-start.17 = (bf16[8,64,128]{2,1,0:T(8,128)(2,1)S(1)}, bf16[8,64,128]{2,1,0:T(8,128)(2,1)S(1)}, u32[]{:S(2)}, u32[]{:S(2)}) collective-permute-start(bf16[8,64,128]{2,1,0:T(8,128)(2,1)S(1)} %get-tuple-element.19), channel_id=1, source_target_pairs={{0,8},{1,0},{2,24},{3,16},{4,9},{5,1},{6,25},{7,17},{8,10},{9,2},{... | collective-permute-start | bytes 393224 | tf_op jit(solution)/shard_map/ppermute | solution.py:324
  106.7 26.1 %copy-start.15 = (bf16[16,64,128]{2,1,0:T(8,128)(2,1)}, bf16[16,64,128]{2,1,0:T(8,128)(2,1)S(1)}, u32[]{:S(2)}) copy-start(bf16[16,64,128]{2,1,0:T(8,128)(2,1)S(1)} %constant_dynamic-update-slice_fusion.2.refs_1_) | copy-start | bytes 786436
  106.7 14.7 %collective-permute-start.21 = (bf16[16,64,128]{2,1,0:T(8,128)(2,1)S(1)}, bf16[16,64,128]{2,1,0:T(8,128)(2,1)S(1)}, u32[]{:S(2)}, u32[]{:S(2)}) collective-permute-start(bf16[16,64,128]{2,1,0:T(8,128)(2,1)S(1)} %constant_dynamic-update-slice_fusion.2.refs_1_), channel_id=1, source_target_pairs={{0,8},{8,0},{16,24},{24,16},{1,9},{9,1},{17,25},{25,17},{2,10},{10... | collective-permute-start | bytes 786440 | tf_op jit(solution)/shard_map/ppermute | solution.py:287
  111.1 21.8 %copy-start.16 = (bf16[16,64,128]{2,1,0:T(8,128)(2,1)}, bf16[16,64,128]{2,1,0:T(8,128)(2,1)S(1)}, u32[]{:S(2)}) copy-start(bf16[16,64,128]{2,1,0:T(8,128)(2,1)S(1)} %constant_dynamic-update-slice_fusion.refs_0_) | copy-start | bytes 786436
  111.1 12.3 %collective-permute-start.22 = (bf16[16,64,128]{2,1,0:T(8,128)(2,1)S(1)}, bf16[16,64,128]{2,1,0:T(8,128)(2,1)S(1)}, u32[]{:S(2)}, u32[]{:S(2)}) collective-permute-start(bf16[16,64,128]{2,1,0:T(8,128)(2,1)S(1)} %constant_dynamic-update-slice_fusion.refs_0_), channel_id=1, source_target_pairs={{0,16},{8,24},{16,0},{24,8},{1,17},{9,25},{17,1},{25,9},{2,18},{10... | collective-permute-start | bytes 786440 | tf_op jit(solution)/shard_map/ppermute | solution.py:286
  116.5 11.9 %collective-permute-start.23 = (bf16[16,64,128]{2,1,0:T(8,128)(2,1)S(1)}, bf16[16,64,128]{2,1,0:T(8,128)(2,1)S(1)}, u32[]{:S(2)}, u32[]{:S(2)}) collective-permute-start(bf16[16,64,128]{2,1,0:T(8,128)(2,1)S(1)} %constant_dynamic-update-slice_fusion.2.refs_1_), channel_id=1, source_target_pairs={{0,16},{8,24},{16,0},{24,8},{1,17},{9,25},{17,1},{25,9},{2,18},{10... | collective-permute-start | bytes 786440 | tf_op jit(solution)/shard_map/ppermute | solution.py:289
  116.6 11.8 %collective-permute-start.20 = (bf16[16,64,128]{2,1,0:T(8,128)(2,1)S(1)}, bf16[16,64,128]{2,1,0:T(8,128)(2,1)S(1)}, u32[]{:S(2)}, u32[]{:S(2)}) collective-permute-start(bf16[16,64,128]{2,1,0:T(8,128)(2,1)S(1)} %constant_dynamic-update-slice_fusion.refs_0_), channel_id=1, source_target_pairs={{0,8},{8,0},{16,24},{24,16},{1,9},{9,1},{17,25},{25,17},{2,10},{10... | collective-permute-start | bytes 786440 | tf_op jit(solution)/shard_map/ppermute | solution.py:288
  121.4 11.4 %copy-start.25 = (bf16[16,64,128]{2,1,0:T(8,128)(2,1)}, bf16[16,64,128]{2,1,0:T(8,128)(2,1)S(1)}, u32[]{:S(2)}) copy-start(bf16[16,64,128]{2,1,0:T(8,128)(2,1)S(1)} %collective-permute-done.21.refs_3_) | copy-start | bytes 786436
  121.4 8.0 %collective-permute-start.25 = (bf16[16,64,128]{2,1,0:T(8,128)(2,1)S(1)}, bf16[16,64,128]{2,1,0:T(8,128)(2,1)S(1)}, u32[]{:S(2)}, u32[]{:S(2)}) collective-permute-start(bf16[16,64,128]{2,1,0:T(8,128)(2,1)S(1)} %collective-permute-done.21.refs_3_), channel_id=1, source_target_pairs={{0,16},{8,24},{16,0},{24,8},{1,17},{9,25},{17,1},{25,9},{2,18},{10... | collective-permute-start | bytes 786440 | tf_op jit(solution)/shard_map/ppermute | solution.py:291
  123.3 9.5 %copy-start.28 = (bf16[16,64,128]{2,1,0:T(8,128)(2,1)}, bf16[16,64,128]{2,1,0:T(8,128)(2,1)S(1)}, u32[]{:S(2)}) copy-start(bf16[16,64,128]{2,1,0:T(8,128)(2,1)S(1)} %collective-permute-done.22.refs_4_) | copy-start | bytes 786436
  123.3 9.5 %collective-permute-start.24 = (bf16[16,64,128]{2,1,0:T(8,128)(2,1)S(1)}, bf16[16,64,128]{2,1,0:T(8,128)(2,1)S(1)}, u32[]{:S(2)}, u32[]{:S(2)}) collective-permute-start(bf16[16,64,128]{2,1,0:T(8,128)(2,1)S(1)} %collective-permute-done.22.refs_4_), channel_id=1, source_target_pairs={{0,8},{8,0},{16,24},{24,16},{1,9},{9,1},{17,25},{25,17},{2,10},{10... | collective-permute-start | bytes 786440 | tf_op jit(solution)/shard_map/ppermute | solution.py:290
  128.5 4.4 %copy-start.30 = (bf16[16,64,128]{2,1,0:T(8,128)(2,1)}, bf16[16,64,128]{2,1,0:T(8,128)(2,1)S(1)}, u32[]{:S(2)}) copy-start(bf16[16,64,128]{2,1,0:T(8,128)(2,1)S(1)} %collective-permute-done.23.refs_5_) | copy-start | bytes 786436
  128.5 4.4 %copy-start.32 = (bf16[16,64,128]{2,1,0:T(8,128)(2,1)}, bf16[16,64,128]{2,1,0:T(8,128)(2,1)S(1)}, u32[]{:S(2)}) copy-start(bf16[16,64,128]{2,1,0:T(8,128)(2,1)S(1)} %collective-permute-done.20.refs_2_) | copy-start | bytes 786436
  146.4 3.0 %collective-permute-start.31 = (s16[4,2,528,128]{3,2,1,0:T(8,128)(2,1)}, s16[4,2,528,128]{3,2,1,0:T(8,128)(2,1)S(1)}, u32[]{:S(2)}, u32[]{:S(2)}) collective-permute-start(s16[4,2,528,128]{3,2,1,0:T(8,128)(2,1)} %get-tuple-element.16), channel_id=1, source_target_pairs={{0,1},{1,0},{2,3},{3,2},{4,5},{5,4},{6,7},{7,6},{8,9},{9,8},{10,11... | collective-permute-start | bytes 3244040 | tf_op jit(solution)/shard_map/ppermute | solution.py:258
  146.4 9.5 %collective-permute-start.26 = (s16[4,2,528,128]{3,2,1,0:T(8,128)(2,1)}, s16[4,2,528,128]{3,2,1,0:T(8,128)(2,1)S(1)}, u32[]{:S(2)}, u32[]{:S(2)}) collective-permute-start(s16[4,2,528,128]{3,2,1,0:T(8,128)(2,1)} %get-tuple-element.15), channel_id=1, source_target_pairs={{0,1},{1,0},{2,3},{3,2},{4,5},{5,4},{6,7},{7,6},{8,9},{9,8},{10,11... | collective-permute-start | bytes 3244040 | tf_op jit(solution)/shard_map/ppermute | solution.py:258
  152.3 11.2 %collective-permute-start.32 = (s16[2,528,128]{2,1,0:T(8,128)(2,1)}, s16[2,528,128]{2,1,0:T(8,128)(2,1)S(1)}, u32[]{:S(2)}, u32[]{:S(2)}) collective-permute-start(s16[2,528,128]{2,1,0:T(8,128)(2,1)} %combine_message.21), channel_id=1, source_target_pairs={{0,2},{1,3},{2,0},{3,1},{4,6},{5,7},{6,4},{7,5},{8,10},{9,11},{10,... | collective-permute-start | bytes 811016 | tf_op jit(solution)/shard_map/ppermute | solution.py:261
  158.9 16.2 %collective-permute-start.27 = (s16[2,528,128]{2,1,0:T(8,128)(2,1)}, s16[2,528,128]{2,1,0:T(8,128)(2,1)S(1)}, u32[]{:S(2)}, u32[]{:S(2)}) collective-permute-start(s16[2,528,128]{2,1,0:T(8,128)(2,1)} %combine_message.18), channel_id=1, source_target_pairs={{0,2},{1,3},{2,0},{3,1},{4,6},{5,7},{6,4},{7,5},{8,10},{9,11},{10,... | collective-permute-start | bytes 811016 | tf_op jit(solution)/shard_map/ppermute | solution.py:261
  166.3 14.2 %collective-permute-start.33 = (s16[2,528,128]{2,1,0:T(8,128)(2,1)}, s16[2,528,128]{2,1,0:T(8,128)(2,1)S(1)}, u32[]{:S(2)}, u32[]{:S(2)}) collective-permute-start(s16[2,528,128]{2,1,0:T(8,128)(2,1)} %combine_message.22), channel_id=1, source_target_pairs={{0,2},{1,3},{6,4},{7,5},{2,6},{3,7},{4,0},{5,1},{8,10},{9,11},{14,... | collective-permute-start | bytes 811016 | tf_op jit(solution)/shard_map/ppermute | solution.py:263
  177.9 12.5 %collective-permute-start.28 = (s16[2,528,128]{2,1,0:T(8,128)(2,1)}, s16[2,528,128]{2,1,0:T(8,128)(2,1)S(1)}, u32[]{:S(2)}, u32[]{:S(2)}) collective-permute-start(s16[2,528,128]{2,1,0:T(8,128)(2,1)} %combine_message.19), channel_id=1, source_target_pairs={{0,2},{1,3},{6,4},{7,5},{2,6},{3,7},{4,0},{5,1},{8,10},{9,11},{14,... | collective-permute-start | bytes 811016 | tf_op jit(solution)/shard_map/ppermute | solution.py:263
  183.4 13.2 %collective-permute-start.34 = (s16[2,528,128]{2,1,0:T(8,128)(2,1)}, s16[2,528,128]{2,1,0:T(8,128)(2,1)S(1)}, u32[]{:S(2)}, u32[]{:S(2)}) collective-permute-start(s16[2,528,128]{2,1,0:T(8,128)(2,1)} %combine_message.23), channel_id=1, source_target_pairs={{0,2},{1,3},{6,4},{7,5},{8,10},{9,11},{14,12},{15,13},{16,18},{17,... | collective-permute-start | bytes 811016 | tf_op jit(solution)/shard_map/ppermute | solution.py:265
  184.7 11.9 %collective-permute-start.35 = (s16[2,528,128]{2,1,0:T(8,128)(2,1)}, s16[2,528,128]{2,1,0:T(8,128)(2,1)S(1)}, u32[]{:S(2)}, u32[]{:S(2)}) collective-permute-start(s16[2,528,128]{2,1,0:T(8,128)(2,1)} %combine_message.23), channel_id=1, source_target_pairs={{2,4},{3,5},{4,2},{5,3},{10,12},{11,13},{12,10},{13,11},{18,20},{1... | collective-permute-start | bytes 811016 | tf_op jit(solution)/shard_map/ppermute | solution.py:266
  193.3 8.6 %collective-permute-start.29 = (s16[2,528,128]{2,1,0:T(8,128)(2,1)}, s16[2,528,128]{2,1,0:T(8,128)(2,1)S(1)}, u32[]{:S(2)}, u32[]{:S(2)}) collective-permute-start(s16[2,528,128]{2,1,0:T(8,128)(2,1)} %combine_message.20), channel_id=1, source_target_pairs={{0,2},{1,3},{6,4},{7,5},{8,10},{9,11},{14,12},{15,13},{16,18},{17,... | collective-permute-start | bytes 811016 | tf_op jit(solution)/shard_map/ppermute | solution.py:265
  194.6 8.6 %collective-permute-start.30 = (s16[2,528,128]{2,1,0:T(8,128)(2,1)}, s16[2,528,128]{2,1,0:T(8,128)(2,1)S(1)}, u32[]{:S(2)}, u32[]{:S(2)}) collective-permute-start(s16[2,528,128]{2,1,0:T(8,128)(2,1)} %combine_message.20), channel_id=1, source_target_pairs={{2,4},{3,5},{4,2},{5,3},{10,12},{11,13},{12,10},{13,11},{18,20},{1... | collective-permute-start | bytes 811016 | tf_op jit(solution)/shard_map/ppermute | solution.py:266
  (25 other events, 24.2 us)

commit v2 on v1

v2 whole, which is shorter than its diff:
```python
import functools

import jax
import jax.numpy as jnp
from jax import lax
from jax.experimental import pallas as pl
from jax.experimental.pallas import tpu as pltpu
from jax.sharding import PartitionSpec as P

GROUP = 8
STEP = 32
TOP = 14.0
VMEM_LIMIT = 24 * 1024 * 1024

def message_rows(vec_width):
    return GROUP * vec_width + 16


def encode(tiles, ref):
    k = tiles[0].shape[0]
    exponents = []
    for i, tile in enumerate(tiles):
        peak = jnp.max(jnp.abs(tile), axis=0, keepdims=True)
        exponent = jnp.ceil(jnp.log2(jnp.maximum(peak, 1e-30)))
        scaled = jnp.round(tile * jnp.exp2(TOP - exponent))
        ref[i * k : (i + 1) * k, :] = scaled.astype(jnp.int32).astype(jnp.int16)
        exponents.append(exponent)
    rest = jnp.zeros((16 - len(tiles), tiles[0].shape[1]), jnp.float32)
    table = jnp.concatenate(exponents + [rest], axis=0)
    ref[len(tiles) * k :, :] = table.astype(jnp.int32).astype(jnp.int16)


def decoder(ref, k, factor=None):
    table = ref[GROUP * k :, :].astype(jnp.int32).astype(jnp.float32)
    scale = jnp.exp2(table - TOP)
    if factor is not None:
        scale = scale * factor

    def tile(i):
        codes = ref[i * k : (i + 1) * k, :].astype(jnp.int32).astype(jnp.float32)
        return codes * scale[i : i + 1, :]

    return tile


def near(x):
    return pltpu.with_memory_space_constraint(x, pltpu.VMEM)


NEAR = pl.BlockSpec(memory_space=pltpu.VMEM)
FAR = pl.BlockSpec(memory_space=pltpu.HBM)


def product_kernel(places, shard, rows, cols, count, *refs):
    total = len(refs) - 8
    pieces = refs[:total]
    blocks, acc, msg_low, msg_high, panel, held, piece_sem, block_sem = refs[total:]
    chips, groups = msg_low.shape[:2]
    k = panel.shape[1]
    row_total = acc.shape[0] - 1
    slots = blocks.shape[0]
    n = count[0, 0]
    row_owner, col_owner = lax.axis_index("row"), lax.axis_index("col")

    def piece_copy(i):
        piece, start, tiles, at = places[i]
        there = panel.at[pl.ds(at(row_owner, col_owner // 2), tiles)]
        return pltpu.make_async_copy(pieces[piece].at[pl.ds(start, tiles)], there, piece_sem.at[i])

    def block_copy(i):
        span = pl.ds(i * STEP, STEP)
        return pltpu.make_async_copy(blocks.at[span], held.at[span], block_sem.at[i])

    for i in range(len(places)):
        piece_copy(i).start()
    for i in range(slots // STEP):

        @pl.when(i * STEP < n)
        def _():
            block_copy(i).start()

    @pl.loop(0, row_total + 1)
    def _(i):
        acc[i] = jnp.zeros_like(acc[0])

    for i in range(len(places)):
        piece_copy(i).wait()

    @pl.loop(0, (n + STEP - 1) // STEP)
    def _(step):
        block_copy(step).wait()
        base = step * STEP
        nil = jnp.zeros(panel.shape[1:], panel.dtype)
        products = []
        for u in range(0, STEP, 2):
            upper = jnp.concatenate([panel[cols[0, base + u]], nil], axis=1)
            lower = jnp.concatenate([nil, panel[cols[0, base + u + 1]]], axis=1)
            both = lax.dot_general(
                jnp.concatenate([upper, lower], axis=0),
                jnp.concatenate([held[base + u], held[base + u + 1]], axis=1),
                (((1,), (1,)), ((), ())),
                preferred_element_type=jnp.float32,
            )
            products += [both[:k], both[k:]]
        for u in range(STEP):
            at = jnp.where(base + u < n, rows[0, base + u], row_total)
            acc[at] += products[u]

    other = 1 - col_owner % 2
    for half, msg in enumerate((msg_low, msg_high)):

        @pl.loop(0, chips * groups)
        def _(i):
            d, g = i // groups, i % groups
            base = (2 * d + other) * shard + (half * groups + g) * GROUP
            encode([acc[base + t] for t in range(GROUP)], msg.at[d, g])


def block_product(pieces, places, blocks, block_rows, block_cols, counts, shard, col_total):
    slots, order, _ = blocks.shape
    k = pieces[0].shape[1]
    panel_tiles = sum(place[2] for place in places)
    scalars = pl.BlockSpec(memory_space=pltpu.SMEM)
    message = pltpu.VMEM((col_total // 2, shard // GROUP // 2, message_rows(k), order), jnp.int16)
    return pl.pallas_call(
        functools.partial(product_kernel, places, shard),
        out_shape=(pltpu.VMEM((col_total * shard + 1, k, order), jnp.float32), message, message),
        in_specs=[scalars] * 3 + [NEAR] * len(pieces) + [FAR],
        out_specs=(NEAR, NEAR, NEAR),
        scratch_shapes=[
            pltpu.VMEM((panel_tiles, k, order), jnp.bfloat16),
            pltpu.VMEM((slots, order, order), jnp.bfloat16),
            pltpu.SemaphoreType.DMA((len(places),)),
            pltpu.SemaphoreType.DMA((slots // STEP,)),
        ],
        compiler_params=pltpu.CompilerParams(vmem_limit_bytes=VMEM_LIMIT),
        name="block_product",
    )(block_rows, block_cols, counts, *[near(p) for p in pieces], pltpu.with_memory_space_constraint(blocks, pltpu.HBM))


def combine_kernel(half, which, gates, form, acc, sib, *refs):
    arrived = refs[: len(gates)]
    chips, groups = sib.shape[:2]
    _, k, order = acc.shape
    shard = acc.shape[0] // (2 * chips)
    col_owner = lax.axis_index("col")
    chip = col_owner // 2
    d = which(chip)
    base = (2 * d + col_owner % 2) * shard + half * groups * GROUP
    if form == "rows":
        result, out, out_sem = refs[-3:]
    elif form == "message":
        result = refs[-1]
    results = refs[len(gates) :]
    step = results[0].shape[0]

    def out_copy(g):
        width = GROUP * order
        there = result.at[:, pl.ds((half * groups + g) * width, width)]
        return pltpu.make_async_copy(out.at[g], there, out_sem.at[g])

    for g in range(groups):
        parts = [decoder(sib.at[d, g], k)]
        for ref, gate in zip(arrived, gates):
            factor = None if gate is None else jnp.where(gate(chip), 1.0, 0.0)
            parts.append(decoder(ref.at[g], k, factor))
        sums = []
        for i in range(GROUP):
            tile = acc[base + g * GROUP + i]
            for part in parts:
                tile = tile + part(i)
            if form == "message":
                sums.append(tile)
            elif form == "tiles":
                at = g * GROUP + i
                results[at // step][at % step] = tile.astype(results[0].dtype)
            else:
                out[g, :, i * order : (i + 1) * order] = tile
        if form == "message":
            encode(sums, result.at[g])
        elif form == "rows":
            out_copy(g).start()
    if form == "rows":
        for g in range(groups):
            out_copy(g).wait()


def combine(half, which, acc, sib, arrived, gates, form, into=None):
    chips, groups, rows, order = sib.shape
    k = acc.shape[1]
    operands = [near(x) for x in (acc, sib, *arrived)]
    specs = [NEAR] * len(operands)
    aliases, scratch, out_spec = {}, [], NEAR
    if form == "message":
        out_shape = pltpu.VMEM((groups, rows, order), jnp.int16)
    elif form == "tiles":
        parts = 4 if groups * GROUP % 4 == 0 else 1
        out_shape = (pltpu.VMEM((groups * GROUP // parts, k, order), jnp.bfloat16),) * parts
        out_spec = (NEAR,) * parts
    else:
        shard = acc.shape[0] // (2 * chips)
        out_shape = jax.ShapeDtypeStruct((k, shard * order), jnp.float32)
        out_spec = FAR
        scratch = [pltpu.VMEM((groups, k, GROUP * order), jnp.float32), pltpu.SemaphoreType.DMA((groups,))]
        if into is not None:
            aliases = {len(operands): 0}
            operands.append(into)
            specs.append(FAR)
    return pl.pallas_call(
        functools.partial(combine_kernel, half, which, gates, form),
        out_shape=out_shape,
        in_specs=specs,
        out_specs=out_spec,
        input_output_aliases=aliases,
        scratch_shapes=scratch,
        compiler_params=pltpu.CompilerParams(vmem_limit_bytes=4 * 1024 * 1024),
        name="combine_" + form,
    )(*operands)


def chip_moves(moves):
    return [(2 * a + core, 2 * b + core) for a, b in moves for core in range(2)]


def is_end(chip):
    return (chip == 0) | (chip == 3)


def is_inner(chip):
    return (chip == 1) | (chip == 2)


def line_sum(half, acc, msg, form, into=None):
    chips = msg.shape[0]
    sib = lax.ppermute(msg, "col", [(c, c ^ 1) for c in range(2 * chips)])
    if chips == 4:
        send = combine(half, lambda z: 3 - 3 * (z % 2), acc, sib, (), (), "message")
        got_a = lax.ppermute(send, "col", chip_moves([(0, 1), (1, 0), (2, 3), (3, 2)]))
        send = combine(half, lambda z: z ^ 2, acc, sib, (got_a,), (is_inner,), "message")
        got_b = lax.ppermute(send, "col", chip_moves([(0, 1), (3, 2), (1, 3), (2, 0)]))
        send = combine(half, lambda z: 1 + z % 2, acc, sib, (got_b,), (is_inner,), "message")
        got_c = lax.ppermute(send, "col", chip_moves([(0, 1), (3, 2)]))
        got_d = lax.ppermute(send, "col", chip_moves([(1, 2), (2, 1)]))
        arrived, gates = (got_a, got_b, got_c, got_d), (is_end, is_end, None, None)
    else:
        arrived = ()
        for step in range(1, chips):
            send = combine(half, lambda z: (z + step) % chips, acc, sib, (), (), "message")
            moves = chip_moves([(a, (a + step) % chips) for a in range(chips)])
            arrived += (lax.ppermute(send, "col", moves),)
        gates = (None,) * len(arrived)
    return combine(half, lambda z: z, acc, sib, arrived, gates, form, into)


def across(x, flip):
    return lax.ppermute(x, "row", [(r, r ^ flip) for r in range(4)])


def gather_square(low, high):
    y_low = across(low, 2)
    x_high = across(high, 1)
    x_low = across(low, 1)
    y_high = across(high, 2)
    return low, high, x_low, x_high, y_low, y_high, across(y_low, 1), across(x_high, 2)


def vector_panel(tiles, row_total):
    shard = tiles.shape[0]
    if row_total != 4:
        whole = lax.all_gather(tiles, "row", axis=0, tiled=True)
        return (whole,), ((0, 0, row_total * shard, lambda r, z: 0),)
    half = shard // 2
    places = []
    for piece in range(8):
        at = lambda r, z, piece=piece: (r ^ (piece // 2)) * shard + piece % 2 * half
        places.append((piece, 0, half, at))
    return gather_square(tiles[:half], tiles[half:]), tuple(places)


def shuffle_kernel(pick, *refs):
    half = len(refs) // 2
    for i in range(half):
        wanted = pick(lax.axis_index("row"), lax.axis_index("col"), i)
        for j in range(half):

            @pl.when(wanted == j)
            def _():
                refs[half + i][...] = refs[j][...]


def shuffle(parts, pick):
    return pl.pallas_call(
        functools.partial(shuffle_kernel, pick),
        out_shape=tuple(pltpu.VMEM(x.shape, x.dtype) for x in parts),
        in_specs=[NEAR] * len(parts),
        out_specs=(NEAR,) * len(parts),
        compiler_params=pltpu.CompilerParams(vmem_limit_bytes=1024 * 1024),
        name="shuffle",
    )(*[near(x) for x in parts])


def join_kernel(*refs):
    step = refs[0].shape[0]
    for i, ref in enumerate(refs[:-1]):
        refs[-1][i * step : (i + 1) * step] = ref[...]


def join(parts):
    shape = (len(parts) * parts[0].shape[0],) + parts[0].shape[1:]
    return pl.pallas_call(
        join_kernel,
        out_shape=pltpu.VMEM(shape, parts[0].dtype),
        in_specs=[NEAR] * len(parts),
        out_specs=NEAR,
        compiler_params=pltpu.CompilerParams(vmem_limit_bytes=1024 * 1024),
        name="join",
    )(*[near(x) for x in parts])


def spread(quarters):
    parts = shuffle(quarters, lambda r, c, i: r ^ i)
    parts = parts[:1] + tuple(across(parts[f], f) for f in (1, 2, 3))
    parts = shuffle(parts, lambda r, c, i: r ^ (c % 4) ^ i)
    got = []
    for j in range(4):
        got.append(lax.ppermute(parts[j], "col", [(c, 2 * (c % 4 ^ j) + c // 4) for c in range(8)]))
    return join(got)


def first_panel(low, high, row_total, col_total):
    if (row_total, col_total) != (4, 8):
        moves = []
        for s in range(row_total * col_total):
            moves.append((s, (s % row_total) * col_total + s // row_total))
        tiles = lax.ppermute(jnp.concatenate(low + high, axis=0), ("row", "col"), moves)
        return vector_panel(tiles, row_total)
    quarter = low[0].shape[0]
    places = []
    for piece in range(8):
        for j in range(4):

            def at(r, z, flip=piece // 2, which=piece % 2, j=j):
                return (z ^ j) * 8 * quarter + which * 4 * quarter + (r ^ flip) * quarter

            places.append((piece, j * quarter, quarter, at))
    return gather_square(spread(low), spread(high)), tuple(places)


def shards(row_total, col_total, vectors, blocks, block_rows, block_cols, counts):
    k, width = vectors.shape
    order = blocks.shape[2]
    shard = width // order
    matrix = (blocks[0], block_rows, block_cols, counts, shard, col_total)
    tiles = vectors.reshape(k, shard, order).transpose(1, 0, 2)
    acc, low, high = block_product(*vector_panel(tiles, row_total), *matrix)
    firsts = line_sum(0, acc, low, "tiles"), line_sum(1, acc, high, "tiles")
    acc, low, high = block_product(*first_panel(*firsts, row_total, col_total), *matrix)
    return line_sum(1, acc, high, "rows", line_sum(0, acc, low, "rows"))


def solution(mesh):
    in_specs = (
        P(None, ("col", "row")),
        P("row", "col", None, None),
        P("row", "col"),
        P("row", "col"),
        P("row", "col"),
    )
    out_specs = P(None, ("row", "col"))
    body = functools.partial(shards, mesh.shape["row"], mesh.shape["col"])
    return jax.shard_map(body, mesh=mesh, in_specs=in_specs, out_specs=out_specs, check_vma=False)
```

time: 205 us -> 178 us (0.87)
  the two profiles are of different devices: /device:TPU:14 before, /device:TPU:18 now
where the time goes in v2:
time: 178 us; the launch traced here: 175 us
  waiting for transfers between devices  75.2 us (42%)
  starting transfers between devices  70 us (39%)
  Pallas kernels  27.7 us (16%)
    ppermute x4, waiting for transfers between devices, line_sum(): lax.ppermute(send, 'col', chip_moves([(0, 1), (1, 0), (2, 3), (3, 2)]))  30.7 us
    ppermute x18, waiting for transfers between devices, across(): return lax.ppermute(x, 'row', [(r, r ^ flip) for r in range(4)])  24.7 us
    pallas_call x2, Pallas kernels, block_product(): pl.pallas_call(functools.partial(product_kernel, places, shard), out_shap...  21.6 us
    ppermute x18, starting transfers between devices, across(): return lax.ppermute(x, 'row', [(r, r ^ flip) for r in range(4)])  20.1 us
    ppermute x8, starting transfers between devices, spread(): lax.ppermute(parts[j], 'col', [(c, 2 * (c % 4 ^ j) + c // 4) for c in ran...  15.5 us
    ppermute x4, starting transfers between devices, line_sum(): got_d = lax.ppermute(send, 'col', chip_moves([(1, 2), (2, 1)]))  14.3 us
    ppermute x4, starting transfers between devices, line_sum(): lax.ppermute(send, 'col', chip_moves([(0, 1), (1, 0), (2, 3), (3, 2)]))  9.42 us
    pallas_call x16, Pallas kernels, combine(): pl.pallas_call(functools.partial(combine_kernel, half, which, gates, form...  5.73 us
  transfers between devices with their start and end apart: 46, of which 23 were waited for; matrix products, arithmetic and copies ran while one was open for 0% of the time, Pallas kernels for 3%

profile of v2, /device:TPU:18, one launch (start us, length us, event | category | flops | bytes accessed | tf_op | source)
XLA Modules:
  0.0 175.0 jit_solution(14564350610916569080)
XLA Ops:
  1.2 1.6 collective-permute-start.2
  3.3 1.5 collective-permute-start
  5.3 5.1 %collective-permute-done.2.refs_4_ = bf16[16,64,128]{2,1,0:T(8,128)(2,1)S(1)} collective-permute-done((bf16[16,64,128]{2,1,0:T(8,128)(2,1)S(1)}, bf16[16,64,128]{2,1,0:T(8,128)(2,1)S(1)}, u32[]{:S(2)}, u32[]{:S(2)}) %collective-permute-start.2) | collective-permute-done | bytes 262176 | tf_op jit(solution)/shard_map/ppermute | solution.py:256
  13.2 4.4 %collective-permute-done.refs_2_ = bf16[16,64,128]{2,1,0:T(8,128)(2,1)S(1)} collective-permute-done((bf16[16,64,128]{2,1,0:T(8,128)(2,1)S(1)}, bf16[16,64,128]{2,1,0:T(8,128)(2,1)S(1)}, u32[]{:S(2)}, u32[]{:S(2)}) %collective-permute-start) | collective-permute-done | bytes 262176 | tf_op jit(solution)/shard_map/ppermute | solution.py:256
  17.6 4.2 %collective-permute-done.4.refs_6_ = bf16[16,64,128]{2,1,0:T(8,128)(2,1)S(1)} collective-permute-done((bf16[16,64,128]{2,1,0:T(8,128)(2,1)S(1)}, bf16[16,64,128]{2,1,0:T(8,128)(2,1)S(1)}, u32[]{:S(2)}, u32[]{:S(2)}) %collective-permute-start.4) | collective-permute-done | bytes 262176 | tf_op jit(solution)/shard_map/ppermute | solution.py:256
  21.8 9.3 %block_product.2 = (f32[257,64,128]{2,1,0:T(8,128)S(1)}, s16[4,2,528,128]{3,2,1,0:T(8,128)(2,1)S(1)}, s16[4,2,528,128]{3,2,1,0:T(8,128)(2,1)S(1)}) custom-call(s32[1,512]{1,0:T(1,128)S(1)} %copy-done.1, s32[1,512]{1,0:T(1,128)S(1)} %copy-done.2, s32[1,1]{1,0:T(1,128)S(6)} %copy.11.count, bf16[16,64,128]{2,1,0:T(8,128)(2,1)S(1)} %get-tuple-element.66.refs_0_, ...), custom_call_target="tpu_custom_call" | custom-call | tf_op jit(solution)/shard_map/block_product/pallas_call | solution.py:125
  31.7 2.2 %collective-permute-done.18.sib = s16[4,2,528,128]{3,2,1,0:T(8,128)(2,1)S(1)} collective-permute-done((s16[4,2,528,128]{3,2,1,0:T(8,128)(2,1)S(1)}, s16[4,2,528,128]{3,2,1,0:T(8,128)(2,1)S(1)}, u32[]{:S(2)}, u32[]{:S(2)}) %collective-permute-start.18) | collective-permute-done | bytes 1081376 | tf_op jit(solution)/shard_map/ppermute | solution.py:235
  36.5 7.1 %collective-permute-done.19.refs_0_ = s16[2,528,128]{2,1,0:T(8,128)(2,1)S(1)} collective-permute-done((s16[2,528,128]{2,1,0:T(8,128)(2,1)S(1)}, s16[2,528,128]{2,1,0:T(8,128)(2,1)S(1)}, u32[]{:S(2)}, u32[]{:S(2)}) %collective-permute-start.19) | collective-permute-done | bytes 270368 | tf_op jit(solution)/shard_map/ppermute | solution.py:238
  43.9 8.6 %collective-permute-done.7.refs_0_ = s16[2,528,128]{2,1,0:T(8,128)(2,1)S(1)} collective-permute-done((s16[2,528,128]{2,1,0:T(8,128)(2,1)S(1)}, s16[2,528,128]{2,1,0:T(8,128)(2,1)S(1)}, u32[]{:S(2)}, u32[]{:S(2)}) %collective-permute-start.7) | collective-permute-done | bytes 270368 | tf_op jit(solution)/shard_map/ppermute | solution.py:238
  52.7 2.0 %collective-permute-start.8 = (s16[2,528,128]{2,1,0:T(8,128)(2,1)S(1)}, s16[2,528,128]{2,1,0:T(8,128)(2,1)S(1)}, u32[]{:S(2)}, u32[]{:S(2)}) collective-permute-start(s16[2,528,128]{2,1,0:T(8,128)(2,1)S(1)} %combine_message.13), channel_id=1, source_target_pairs={{0,2},{1,3},{6,4},{7,5},{2,6},{3,7},{4,0},{5,1},{8,10},{9,11},{14,... | collective-permute-start | bytes 811016 | tf_op jit(solution)/shard_map/ppermute | solution.py:240
  55.0 1.3 collective-permute-start.21
  56.3 3.9 %collective-permute-start.22 = (s16[2,528,128]{2,1,0:T(8,128)(2,1)S(1)}, s16[2,528,128]{2,1,0:T(8,128)(2,1)S(1)}, u32[]{:S(2)}, u32[]{:S(2)}) collective-permute-start(s16[2,528,128]{2,1,0:T(8,128)(2,1)S(1)} %combine_message.17), channel_id=1, source_target_pairs={{2,4},{3,5},{4,2},{5,3},{10,12},{11,13},{12,10},{13,11},{18,20},{1... | collective-permute-start | bytes 811016 | tf_op jit(solution)/shard_map/ppermute | solution.py:243
  60.2 2.4 %collective-permute-done.8.refs_0_.refs_1_ = s16[2,528,128]{2,1,0:T(8,128)(2,1)S(1)} collective-permute-done((s16[2,528,128]{2,1,0:T(8,128)(2,1)S(1)}, s16[2,528,128]{2,1,0:T(8,128)(2,1)S(1)}, u32[]{:S(2)}, u32[]{:S(2)}) %collective-permute-start.8) | collective-permute-done | bytes 270368 | tf_op jit(solution)/shard_map/ppermute | solution.py:240
  62.9 2.9 %collective-permute-start.10 = (s16[2,528,128]{2,1,0:T(8,128)(2,1)S(1)}, s16[2,528,128]{2,1,0:T(8,128)(2,1)S(1)}, u32[]{:S(2)}, u32[]{:S(2)}) collective-permute-start(s16[2,528,128]{2,1,0:T(8,128)(2,1)S(1)} %combine_message.14), channel_id=1, source_target_pairs={{2,4},{3,5},{4,2},{5,3},{10,12},{11,13},{12,10},{13,11},{18,20},{1... | collective-permute-start | bytes 811016 | tf_op jit(solution)/shard_map/ppermute | solution.py:243
  65.8 1.3 collective-permute-start.9
  67.1 2.8 %collective-permute-done.22.refs_3_ = s16[2,528,128]{2,1,0:T(8,128)(2,1)S(1)} collective-permute-done((s16[2,528,128]{2,1,0:T(8,128)(2,1)S(1)}, s16[2,528,128]{2,1,0:T(8,128)(2,1)S(1)}, u32[]{:S(2)}, u32[]{:S(2)}) %collective-permute-start.22) | collective-permute-done | bytes 270368 | tf_op jit(solution)/shard_map/ppermute | solution.py:243
  70.4 2.8 %collective-permute-start.24 = (bf16[4,64,128]{2,1,0:T(8,128)(2,1)S(1)}, bf16[4,64,128]{2,1,0:T(8,128)(2,1)S(1)}, u32[]{:S(2)}, u32[]{:S(2)}) collective-permute-start(bf16[4,64,128]{2,1,0:T(8,128)(2,1)S(1)} %get-tuple-element.56), channel_id=1, source_target_pairs={{0,16},{8,24},{16,0},{24,8},{1,17},{9,25},{17,1},{25,9},{2,18},{10... | collective-permute-start | bytes 196616 | tf_op jit(solution)/shard_map/ppermute | solution.py:256
  73.2 1.4 collective-permute-start.25
  75.7 1.8 %collective-permute-start.12 = (bf16[4,64,128]{2,1,0:T(8,128)(2,1)S(1)}, bf16[4,64,128]{2,1,0:T(8,128)(2,1)S(1)}, u32[]{:S(2)}, u32[]{:S(2)}) collective-permute-start(bf16[4,64,128]{2,1,0:T(8,128)(2,1)S(1)} %get-tuple-element.43), channel_id=1, source_target_pairs={{0,16},{8,24},{16,0},{24,8},{1,17},{9,25},{17,1},{25,9},{2,18},{10... | collective-permute-start | bytes 196616 | tf_op jit(solution)/shard_map/ppermute | solution.py:256
  77.5 1.4 collective-permute-start.13
  79.1 1.9 %collective-permute-start.26 = (bf16[4,64,128]{2,1,0:T(8,128)(2,1)S(1)}, bf16[4,64,128]{2,1,0:T(8,128)(2,1)S(1)}, u32[]{:S(2)}, u32[]{:S(2)}) collective-permute-start(bf16[4,64,128]{2,1,0:T(8,128)(2,1)S(1)} %get-tuple-element.58), channel_id=1, source_target_pairs={{0,0},{1,2},{2,4},{3,6},{4,1},{5,3},{6,5},{7,7},{8,8},{9,10},{10,1... | collective-permute-start | bytes 196616 | tf_op jit(solution)/shard_map/ppermute | solution.py:326
  81.8 1.5 collective-permute-start.28
  83.3 2.7 %collective-permute-start.29 = (bf16[4,64,128]{2,1,0:T(8,128)(2,1)S(1)}, bf16[4,64,128]{2,1,0:T(8,128)(2,1)S(1)}, u32[]{:S(2)}, u32[]{:S(2)}) collective-permute-start(bf16[4,64,128]{2,1,0:T(8,128)(2,1)S(1)} %get-tuple-element.61), channel_id=1, source_target_pairs={{0,6},{1,4},{2,2},{3,0},{4,7},{5,5},{6,3},{7,1},{8,14},{9,12},{10,... | collective-permute-start | bytes 196616 | tf_op jit(solution)/shard_map/ppermute | solution.py:326
  86.1 3.8 %collective-permute-start.14 = (bf16[4,64,128]{2,1,0:T(8,128)(2,1)S(1)}, bf16[4,64,128]{2,1,0:T(8,128)(2,1)S(1)}, u32[]{:S(2)}, u32[]{:S(2)}) collective-permute-start(bf16[4,64,128]{2,1,0:T(8,128)(2,1)S(1)} %get-tuple-element.45), channel_id=1, source_target_pairs={{0,0},{1,2},{2,4},{3,6},{4,1},{5,3},{6,5},{7,7},{8,8},{9,10},{10,1... | collective-permute-start | bytes 196616 | tf_op jit(solution)/shard_map/ppermute | solution.py:326
  90.1 4.7 %collective-permute-start.17 = (bf16[4,64,128]{2,1,0:T(8,128)(2,1)S(1)}, bf16[4,64,128]{2,1,0:T(8,128)(2,1)S(1)}, u32[]{:S(2)}, u32[]{:S(2)}) collective-permute-start(bf16[4,64,128]{2,1,0:T(8,128)(2,1)S(1)} %get-tuple-element.48), channel_id=1, source_target_pairs={{0,6},{1,4},{2,2},{3,0},{4,7},{5,5},{6,3},{7,1},{8,14},{9,12},{10,... | collective-permute-start | bytes 196616 | tf_op jit(solution)/shard_map/ppermute | solution.py:326
  95.5 1.2 collective-permute-done.17.refs_3_
  96.7 2.1 %collective-permute-start.32 = (bf16[16,64,128]{2,1,0:T(8,128)(2,1)S(1)}, bf16[16,64,128]{2,1,0:T(8,128)(2,1)S(1)}, u32[]{:S(2)}, u32[]{:S(2)}) collective-permute-start(bf16[16,64,128]{2,1,0:T(8,128)(2,1)S(1)} %join.2.refs_0_), channel_id=1, source_target_pairs={{0,16},{8,24},{16,0},{24,8},{1,17},{9,25},{17,1},{25,9},{2,18},{10... | collective-permute-start | bytes 786440 | tf_op jit(solution)/shard_map/ppermute | solution.py:256
  99.9 4.2 %collective-permute-done.31.refs_3_ = bf16[16,64,128]{2,1,0:T(8,128)(2,1)S(1)} collective-permute-done((bf16[16,64,128]{2,1,0:T(8,128)(2,1)S(1)}, bf16[16,64,128]{2,1,0:T(8,128)(2,1)S(1)}, u32[]{:S(2)}, u32[]{:S(2)}) %collective-permute-start.31) | collective-permute-done | bytes 262176 | tf_op jit(solution)/shard_map/ppermute | solution.py:256
  104.1 2.0 %collective-permute-start.35 = (bf16[16,64,128]{2,1,0:T(8,128)(2,1)S(1)}, bf16[16,64,128]{2,1,0:T(8,128)(2,1)S(1)}, u32[]{:S(2)}, u32[]{:S(2)}) collective-permute-start(bf16[16,64,128]{2,1,0:T(8,128)(2,1)S(1)} %collective-permute-done.31.refs_3_), channel_id=1, source_target_pairs={{0,16},{8,24},{16,0},{24,8},{1,17},{9,25},{17,1},{25,9},{2,18},{10... | collective-permute-start | bytes 786440 | tf_op jit(solution)/shard_map/ppermute | solution.py:256
  107.0 2.7 %collective-permute-done.33.refs_5_ = bf16[16,64,128]{2,1,0:T(8,128)(2,1)S(1)} collective-permute-done((bf16[16,64,128]{2,1,0:T(8,128)(2,1)S(1)}, bf16[16,64,128]{2,1,0:T(8,128)(2,1)S(1)}, u32[]{:S(2)}, u32[]{:S(2)}) %collective-permute-start.33) | collective-permute-done | bytes 262176 | tf_op jit(solution)/shard_map/ppermute | solution.py:256
  109.8 2.8 %collective-permute-done.35.refs_7_ = bf16[16,64,128]{2,1,0:T(8,128)(2,1)S(1)} collective-permute-done((bf16[16,64,128]{2,1,0:T(8,128)(2,1)S(1)}, bf16[16,64,128]{2,1,0:T(8,128)(2,1)S(1)}, u32[]{:S(2)}, u32[]{:S(2)}) %collective-permute-start.35) | collective-permute-done | bytes 262176 | tf_op jit(solution)/shard_map/ppermute | solution.py:256
  112.6 12.3 %block_product.3 = (f32[257,64,128]{2,1,0:T(8,128)S(1)}, s16[4,2,528,128]{3,2,1,0:T(8,128)(2,1)S(1)}, s16[4,2,528,128]{3,2,1,0:T(8,128)(2,1)S(1)}) custom-call(s32[1,512]{1,0:T(1,128)S(1)} %copy-done.1, s32[1,512]{1,0:T(1,128)S(1)} %copy-done.2, s32[1,1]{1,0:T(1,128)S(6)} %copy.11.count, bf16[16,64,128]{2,1,0:T(8,128)(2,1)S(1)} %join.2.refs_0_, ...), custom_call_target="tpu_custom_call" | custom-call | tf_op jit(solution)/shard_map/block_product/pallas_call | solution.py:125
  125.4 2.2 %collective-permute-done.41.sib = s16[4,2,528,128]{3,2,1,0:T(8,128)(2,1)S(1)} collective-permute-done((s16[4,2,528,128]{3,2,1,0:T(8,128)(2,1)S(1)}, s16[4,2,528,128]{3,2,1,0:T(8,128)(2,1)S(1)}, u32[]{:S(2)}, u32[]{:S(2)}) %collective-permute-start.41) | collective-permute-done | bytes 1081376 | tf_op jit(solution)/shard_map/ppermute | solution.py:235
  127.8 6.5 %collective-permute-start.42 = (s16[2,528,128]{2,1,0:T(8,128)(2,1)S(1)}, s16[2,528,128]{2,1,0:T(8,128)(2,1)S(1)}, u32[]{:S(2)}, u32[]{:S(2)}) collective-permute-start(s16[2,528,128]{2,1,0:T(8,128)(2,1)S(1)} %combine_message.21), channel_id=1, source_target_pairs={{0,2},{1,3},{2,0},{3,1},{4,6},{5,7},{6,4},{7,5},{8,10},{9,11},{10,... | collective-permute-start | bytes 811016 | tf_op jit(solution)/shard_map/ppermute | solution.py:238
  134.5 1.4 collective-permute-start.37
  135.9 5.8 %collective-permute-done.42.refs_0_ = s16[2,528,128]{2,1,0:T(8,128)(2,1)S(1)} collective-permute-done((s16[2,528,128]{2,1,0:T(8,128)(2,1)S(1)}, s16[2,528,128]{2,1,0:T(8,128)(2,1)S(1)}, u32[]{:S(2)}, u32[]{:S(2)}) %collective-permute-start.42) | collective-permute-done | bytes 270368 | tf_op jit(solution)/shard_map/ppermute | solution.py:238
  142.9 9.3 %collective-permute-done.37.refs_0_ = s16[2,528,128]{2,1,0:T(8,128)(2,1)S(1)} collective-permute-done((s16[2,528,128]{2,1,0:T(8,128)(2,1)S(1)}, s16[2,528,128]{2,1,0:T(8,128)(2,1)S(1)}, u32[]{:S(2)}, u32[]{:S(2)}) %collective-permute-start.37) | collective-permute-done | bytes 270368 | tf_op jit(solution)/shard_map/ppermute | solution.py:238
  152.5 1.2 collective-permute-start.38
  154.0 1.3 collective-permute-start.44
  155.3 4.7 %collective-permute-start.45 = (s16[2,528,128]{2,1,0:T(8,128)(2,1)S(1)}, s16[2,528,128]{2,1,0:T(8,128)(2,1)S(1)}, u32[]{:S(2)}, u32[]{:S(2)}) collective-permute-start(s16[2,528,128]{2,1,0:T(8,128)(2,1)S(1)} %combine_message.23), channel_id=1, source_target_pairs={{2,4},{3,5},{4,2},{5,3},{10,12},{11,13},{12,10},{13,11},{18,20},{1... | collective-permute-start | bytes 811016 | tf_op jit(solution)/shard_map/ppermute | solution.py:243
  159.9 2.4 %collective-permute-done.38.refs_0_.refs_1_ = s16[2,528,128]{2,1,0:T(8,128)(2,1)S(1)} collective-permute-done((s16[2,528,128]{2,1,0:T(8,128)(2,1)S(1)}, s16[2,528,128]{2,1,0:T(8,128)(2,1)S(1)}, u32[]{:S(2)}, u32[]{:S(2)}) %collective-permute-start.38) | collective-permute-done | bytes 270368 | tf_op jit(solution)/shard_map/ppermute | solution.py:240
  162.6 1.3 collective-permute-start.39
  163.9 2.9 %collective-permute-start.40 = (s16[2,528,128]{2,1,0:T(8,128)(2,1)S(1)}, s16[2,528,128]{2,1,0:T(8,128)(2,1)S(1)}, u32[]{:S(2)}, u32[]{:S(2)}) collective-permute-start(s16[2,528,128]{2,1,0:T(8,128)(2,1)S(1)} %combine_message.20), channel_id=1, source_target_pairs={{2,4},{3,5},{4,2},{5,3},{10,12},{11,13},{12,10},{13,11},{18,20},{1... | collective-permute-start | bytes 811016 | tf_op jit(solution)/shard_map/ppermute | solution.py:243
  166.8 1.3 collective-permute-done.44.refs_2_
  168.1 1.5 collective-permute-done.45.refs_3_
  169.6 1.1 combine_rows.2.refs_4_
  170.7 2.1 %collective-permute-done.39.refs_2_ = s16[2,528,128]{2,1,0:T(8,128)(2,1)S(1)} collective-permute-done((s16[2,528,128]{2,1,0:T(8,128)(2,1)S(1)}, s16[2,528,128]{2,1,0:T(8,128)(2,1)S(1)}, u32[]{:S(2)}, u32[]{:S(2)}) %collective-permute-start.39) | collective-permute-done | bytes 270368 | tf_op jit(solution)/shard_map/ppermute | solution.py:242
  172.7 1.2 collective-permute-done.40.refs_3_
  (76 shorter events, 18.2 us)
Async XLA Ops:
  0.0 21.8 %copy-start.1 = (s32[1,512]{1,0:T(1,128)S(1)}, s32[1,512]{1,0:T(1,128)}, u32[]{:S(2)}) copy-start(s32[1,512]{1,0:T(1,128)} %rows.3) | copy-start | bytes 6148
  1.0 20.8 %copy-start.2 = (s32[1,512]{1,0:T(1,128)S(1)}, s32[1,512]{1,0:T(1,128)}, u32[]{:S(2)}) copy-start(s32[1,512]{1,0:T(1,128)} %cols.3) | copy-start | bytes 6148
  1.2 9.2 %collective-permute-start.2 = (bf16[16,64,128]{2,1,0:T(8,128)(2,1)S(1)}, bf16[16,64,128]{2,1,0:T(8,128)(2,1)S(1)}, u32[]{:S(2)}, u32[]{:S(2)}) collective-permute-start(bf16[16,64,128]{2,1,0:T(8,128)(2,1)S(1)} %get-tuple-element.66.refs_0_), channel_id=1, source_target_pairs={{0,16},{8,24},{16,0},{24,8},{1,17},{9,25},{17,1},{25,9},{2,18},{10... | collective-permute-start | bytes 786440 | tf_op jit(solution)/shard_map/ppermute | solution.py:256
  2.8 9.2 %collective-permute-start.1 = (bf16[16,64,128]{2,1,0:T(8,128)(2,1)S(1)}, bf16[16,64,128]{2,1,0:T(8,128)(2,1)S(1)}, u32[]{:S(2)}, u32[]{:S(2)}) collective-permute-start(bf16[16,64,128]{2,1,0:T(8,128)(2,1)S(1)} %get-tuple-element.65.refs_1_), channel_id=1, source_target_pairs={{0,8},{8,0},{16,24},{24,16},{1,9},{9,1},{17,25},{25,17},{2,10},{10... | collective-permute-start | bytes 786440 | tf_op jit(solution)/shard_map/ppermute | solution.py:256
  3.3 14.3 %collective-permute-start = (bf16[16,64,128]{2,1,0:T(8,128)(2,1)S(1)}, bf16[16,64,128]{2,1,0:T(8,128)(2,1)S(1)}, u32[]{:S(2)}, u32[]{:S(2)}) collective-permute-start(bf16[16,64,128]{2,1,0:T(8,128)(2,1)S(1)} %get-tuple-element.66.refs_0_), channel_id=1, source_target_pairs={{0,8},{8,0},{16,24},{24,16},{1,9},{9,1},{17,25},{25,17},{2,10},{10... | collective-permute-start | bytes 786440 | tf_op jit(solution)/shard_map/ppermute | solution.py:256
  4.8 12.8 %collective-permute-start.3 = (bf16[16,64,128]{2,1,0:T(8,128)(2,1)S(1)}, bf16[16,64,128]{2,1,0:T(8,128)(2,1)S(1)}, u32[]{:S(2)}, u32[]{:S(2)}) collective-permute-start(bf16[16,64,128]{2,1,0:T(8,128)(2,1)S(1)} %get-tuple-element.65.refs_1_), channel_id=1, source_target_pairs={{0,16},{8,24},{16,0},{24,8},{1,17},{9,25},{17,1},{25,9},{2,18},{10... | collective-permute-start | bytes 786440 | tf_op jit(solution)/shard_map/ppermute | solution.py:256
  10.5 11.3 %collective-permute-start.4 = (bf16[16,64,128]{2,1,0:T(8,128)(2,1)S(1)}, bf16[16,64,128]{2,1,0:T(8,128)(2,1)S(1)}, u32[]{:S(2)}, u32[]{:S(2)}) collective-permute-start(bf16[16,64,128]{2,1,0:T(8,128)(2,1)S(1)} %collective-permute-done.2.refs_4_), channel_id=1, source_target_pairs={{0,8},{8,0},{16,24},{24,16},{1,9},{9,1},{17,25},{25,17},{2,10},{10... | collective-permute-start | bytes 786440 | tf_op jit(solution)/shard_map/ppermute | solution.py:256
  12.0 9.8 %collective-permute-start.5 = (bf16[16,64,128]{2,1,0:T(8,128)(2,1)S(1)}, bf16[16,64,128]{2,1,0:T(8,128)(2,1)S(1)}, u32[]{:S(2)}, u32[]{:S(2)}) collective-permute-start(bf16[16,64,128]{2,1,0:T(8,128)(2,1)S(1)} %collective-permute-done.1.refs_3_), channel_id=1, source_target_pairs={{0,16},{8,24},{16,0},{24,8},{1,17},{9,25},{17,1},{25,9},{2,18},{10... | collective-permute-start | bytes 786440 | tf_op jit(solution)/shard_map/ppermute | solution.py:256
  31.2 2.8 %collective-permute-start.18 = (s16[4,2,528,128]{3,2,1,0:T(8,128)(2,1)S(1)}, s16[4,2,528,128]{3,2,1,0:T(8,128)(2,1)S(1)}, u32[]{:S(2)}, u32[]{:S(2)}) collective-permute-start(s16[4,2,528,128]{3,2,1,0:T(8,128)(2,1)S(1)} %get-tuple-element.49), channel_id=1, source_target_pairs={{0,1},{1,0},{2,3},{3,2},{4,5},{5,4},{6,7},{7,6},{8,9},{9,8},{10,11... | collective-permute-start | bytes 3244040 | tf_op jit(solution)/shard_map/ppermute | solution.py:235
  31.2 4.2 %collective-permute-start.6 = (s16[4,2,528,128]{3,2,1,0:T(8,128)(2,1)S(1)}, s16[4,2,528,128]{3,2,1,0:T(8,128)(2,1)S(1)}, u32[]{:S(2)}, u32[]{:S(2)}) collective-permute-start(s16[4,2,528,128]{3,2,1,0:T(8,128)(2,1)S(1)} %get-tuple-element.36), channel_id=1, source_target_pairs={{0,1},{1,0},{2,3},{3,2},{4,5},{5,4},{6,7},{7,6},{8,9},{9,8},{10,11... | collective-permute-start | bytes 3244040 | tf_op jit(solution)/shard_map/ppermute | solution.py:235
  34.1 9.4 %collective-permute-start.19 = (s16[2,528,128]{2,1,0:T(8,128)(2,1)S(1)}, s16[2,528,128]{2,1,0:T(8,128)(2,1)S(1)}, u32[]{:S(2)}, u32[]{:S(2)}) collective-permute-start(s16[2,528,128]{2,1,0:T(8,128)(2,1)S(1)} %combine_message.15), channel_id=1, source_target_pairs={{0,2},{1,3},{2,0},{3,1},{4,6},{5,7},{6,4},{7,5},{8,10},{9,11},{10,... | collective-permute-start | bytes 811016 | tf_op jit(solution)/shard_map/ppermute | solution.py:238
  35.7 16.8 %collective-permute-start.7 = (s16[2,528,128]{2,1,0:T(8,128)(2,1)S(1)}, s16[2,528,128]{2,1,0:T(8,128)(2,1)S(1)}, u32[]{:S(2)}, u32[]{:S(2)}) collective-permute-start(s16[2,528,128]{2,1,0:T(8,128)(2,1)S(1)} %combine_message.12), channel_id=1, source_target_pairs={{0,2},{1,3},{2,0},{3,1},{4,6},{5,7},{6,4},{7,5},{8,10},{9,11},{10,... | collective-permute-start | bytes 811016 | tf_op jit(solution)/shard_map/ppermute | solution.py:238
  43.8 11.0 %collective-permute-start.20 = (s16[2,528,128]{2,1,0:T(8,128)(2,1)S(1)}, s16[2,528,128]{2,1,0:T(8,128)(2,1)S(1)}, u32[]{:S(2)}, u32[]{:S(2)}) collective-permute-start(s16[2,528,128]{2,1,0:T(8,128)(2,1)S(1)} %combine_message.16), channel_id=1, source_target_pairs={{0,2},{1,3},{6,4},{7,5},{2,6},{3,7},{4,0},{5,1},{8,10},{9,11},{14,... | collective-permute-start | bytes 811016 | tf_op jit(solution)/shard_map/ppermute | solution.py:240
  52.7 9.9 %collective-permute-start.8 = (s16[2,528,128]{2,1,0:T(8,128)(2,1)S(1)}, s16[2,528,128]{2,1,0:T(8,128)(2,1)S(1)}, u32[]{:S(2)}, u32[]{:S(2)}) collective-permute-start(s16[2,528,128]{2,1,0:T(8,128)(2,1)S(1)} %combine_message.13), channel_id=1, source_target_pairs={{0,2},{1,3},{6,4},{7,5},{2,6},{3,7},{4,0},{5,1},{8,10},{9,11},{14,... | collective-permute-start | bytes 811016 | tf_op jit(solution)/shard_map/ppermute | solution.py:240
  55.0 12.0 %collective-permute-start.21 = (s16[2,528,128]{2,1,0:T(8,128)(2,1)S(1)}, s16[2,528,128]{2,1,0:T(8,128)(2,1)S(1)}, u32[]{:S(2)}, u32[]{:S(2)}) collective-permute-start(s16[2,528,128]{2,1,0:T(8,128)(2,1)S(1)} %combine_message.17), channel_id=1, source_target_pairs={{0,2},{1,3},{6,4},{7,5},{8,10},{9,11},{14,12},{15,13},{16,18},{17,... | collective-permute-start | bytes 811016 | tf_op jit(solution)/shard_map/ppermute | solution.py:242
  56.3 13.5 %collective-permute-start.22 = (s16[2,528,128]{2,1,0:T(8,128)(2,1)S(1)}, s16[2,528,128]{2,1,0:T(8,128)(2,1)S(1)}, u32[]{:S(2)}, u32[]{:S(2)}) collective-permute-start(s16[2,528,128]{2,1,0:T(8,128)(2,1)S(1)} %combine_message.17), channel_id=1, source_target_pairs={{2,4},{3,5},{4,2},{5,3},{10,12},{11,13},{12,10},{13,11},{18,20},{1... | collective-permute-start | bytes 811016 | tf_op jit(solution)/shard_map/ppermute | solution.py:243
  62.9 11.8 %collective-permute-start.10 = (s16[2,528,128]{2,1,0:T(8,128)(2,1)S(1)}, s16[2,528,128]{2,1,0:T(8,128)(2,1)S(1)}, u32[]{:S(2)}, u32[]{:S(2)}) collective-permute-start(s16[2,528,128]{2,1,0:T(8,128)(2,1)S(1)} %combine_message.14), channel_id=1, source_target_pairs={{2,4},{3,5},{4,2},{5,3},{10,12},{11,13},{12,10},{13,11},{18,20},{1... | collective-permute-start | bytes 811016 | tf_op jit(solution)/shard_map/ppermute | solution.py:243
  65.8 8.8 %collective-permute-start.9 = (s16[2,528,128]{2,1,0:T(8,128)(2,1)S(1)}, s16[2,528,128]{2,1,0:T(8,128)(2,1)S(1)}, u32[]{:S(2)}, u32[]{:S(2)}) collective-permute-start(s16[2,528,128]{2,1,0:T(8,128)(2,1)S(1)} %combine_message.14), channel_id=1, source_target_pairs={{0,2},{1,3},{6,4},{7,5},{8,10},{9,11},{14,12},{15,13},{16,18},{17,... | collective-permute-start | bytes 811016 | tf_op jit(solution)/shard_map/ppermute | solution.py:242
  70.3 7.2 %collective-permute-start.23 = (bf16[4,64,128]{2,1,0:T(8,128)(2,1)S(1)}, bf16[4,64,128]{2,1,0:T(8,128)(2,1)S(1)}, u32[]{:S(2)}, u32[]{:S(2)}) collective-permute-start(bf16[4,64,128]{2,1,0:T(8,128)(2,1)S(1)} %get-tuple-element.55), channel_id=1, source_target_pairs={{0,8},{8,0},{16,24},{24,16},{1,9},{9,1},{17,25},{25,17},{2,10},{10... | collective-permute-start | bytes 196616 | tf_op jit(solution)/shard_map/ppermute | solution.py:256
  70.4 8.5 %collective-permute-start.24 = (bf16[4,64,128]{2,1,0:T(8,128)(2,1)S(1)}, bf16[4,64,128]{2,1,0:T(8,128)(2,1)S(1)}, u32[]{:S(2)}, u32[]{:S(2)}) collective-permute-start(bf16[4,64,128]{2,1,0:T(8,128)(2,1)S(1)} %get-tuple-element.56), channel_id=1, source_target_pairs={{0,16},{8,24},{16,0},{24,8},{1,17},{9,25},{17,1},{25,9},{2,18},{10... | collective-permute-start | bytes 196616 | tf_op jit(solution)/shard_map/ppermute | solution.py:256
  73.2 5.8 %collective-permute-start.25 = (bf16[4,64,128]{2,1,0:T(8,128)(2,1)S(1)}, bf16[4,64,128]{2,1,0:T(8,128)(2,1)S(1)}, u32[]{:S(2)}, u32[]{:S(2)}) collective-permute-start(bf16[4,64,128]{2,1,0:T(8,128)(2,1)S(1)} %get-tuple-element.57), channel_id=1, source_target_pairs={{0,24},{8,16},{16,8},{24,0},{1,25},{9,17},{17,9},{25,1},{2,26},{10... | collective-permute-start | bytes 196616 | tf_op jit(solution)/shard_map/ppermute | solution.py:256
  75.1 6.7 %collective-permute-start.11 = (bf16[4,64,128]{2,1,0:T(8,128)(2,1)S(1)}, bf16[4,64,128]{2,1,0:T(8,128)(2,1)S(1)}, u32[]{:S(2)}, u32[]{:S(2)}) collective-permute-start(bf16[4,64,128]{2,1,0:T(8,128)(2,1)S(1)} %get-tuple-element.42), channel_id=1, source_target_pairs={{0,8},{8,0},{16,24},{24,16},{1,9},{9,1},{17,25},{25,17},{2,10},{10... | collective-permute-start | bytes 196616 | tf_op jit(solution)/shard_map/ppermute | solution.py:256
  75.7 7.6 %collective-permute-start.12 = (bf16[4,64,128]{2,1,0:T(8,128)(2,1)S(1)}, bf16[4,64,128]{2,1,0:T(8,128)(2,1)S(1)}, u32[]{:S(2)}, u32[]{:S(2)}) collective-permute-start(bf16[4,64,128]{2,1,0:T(8,128)(2,1)S(1)} %get-tuple-element.43), channel_id=1, source_target_pairs={{0,16},{8,24},{16,0},{24,8},{1,17},{9,25},{17,1},{25,9},{2,18},{10... | collective-permute-start | bytes 196616 | tf_op jit(solution)/shard_map/ppermute | solution.py:256
  77.5 8.5 %collective-permute-start.13 = (bf16[4,64,128]{2,1,0:T(8,128)(2,1)S(1)}, bf16[4,64,128]{2,1,0:T(8,128)(2,1)S(1)}, u32[]{:S(2)}, u32[]{:S(2)}) collective-permute-start(bf16[4,64,128]{2,1,0:T(8,128)(2,1)S(1)} %get-tuple-element.44), channel_id=1, source_target_pairs={{0,24},{8,16},{16,8},{24,0},{1,25},{9,17},{17,9},{25,1},{2,26},{10... | collective-permute-start | bytes 196616 | tf_op jit(solution)/shard_map/ppermute | solution.py:256
  79.1 10.7 %collective-permute-start.26 = (bf16[4,64,128]{2,1,0:T(8,128)(2,1)S(1)}, bf16[4,64,128]{2,1,0:T(8,128)(2,1)S(1)}, u32[]{:S(2)}, u32[]{:S(2)}) collective-permute-start(bf16[4,64,128]{2,1,0:T(8,128)(2,1)S(1)} %get-tuple-element.58), channel_id=1, source_target_pairs={{0,0},{1,2},{2,4},{3,6},{4,1},{5,3},{6,5},{7,7},{8,8},{9,10},{10,1... | collective-permute-start | bytes 196616 | tf_op jit(solution)/shard_map/ppermute | solution.py:326
  81.1 8.9 %collective-permute-start.27 = (bf16[4,64,128]{2,1,0:T(8,128)(2,1)S(1)}, bf16[4,64,128]{2,1,0:T(8,128)(2,1)S(1)}, u32[]{:S(2)}, u32[]{:S(2)}) collective-permute-start(bf16[4,64,128]{2,1,0:T(8,128)(2,1)S(1)} %get-tuple-element.59), channel_id=1, source_target_pairs={{0,2},{1,0},{2,6},{3,4},{4,3},{5,1},{6,7},{7,5},{8,10},{9,8},{10,1... | collective-permute-start | bytes 196616 | tf_op jit(solution)/shard_map/ppermute | solution.py:326
  81.8 8.3 %collective-permute-start.28 = (bf16[4,64,128]{2,1,0:T(8,128)(2,1)S(1)}, bf16[4,64,128]{2,1,0:T(8,128)(2,1)S(1)}, u32[]{:S(2)}, u32[]{:S(2)}) collective-permute-start(bf16[4,64,128]{2,1,0:T(8,128)(2,1)S(1)} %get-tuple-element.60), channel_id=1, source_target_pairs={{0,4},{1,6},{2,0},{3,2},{4,5},{5,7},{6,1},{7,3},{8,12},{9,14},{10,... | collective-permute-start | bytes 196616 | tf_op jit(solution)/shard_map/ppermute | solution.py:326
  83.3 11.5 %collective-permute-start.29 = (bf16[4,64,128]{2,1,0:T(8,128)(2,1)S(1)}, bf16[4,64,128]{2,1,0:T(8,128)(2,1)S(1)}, u32[]{:S(2)}, u32[]{:S(2)}) collective-permute-start(bf16[4,64,128]{2,1,0:T(8,128)(2,1)S(1)} %get-tuple-element.61), channel_id=1, source_target_pairs={{0,6},{1,4},{2,2},{3,0},{4,7},{5,5},{6,3},{7,1},{8,14},{9,12},{10,... | collective-permute-start | bytes 196616 | tf_op jit(solution)/shard_map/ppermute | solution.py:326
  86.1 9.4 %collective-permute-start.14 = (bf16[4,64,128]{2,1,0:T(8,128)(2,1)S(1)}, bf16[4,64,128]{2,1,0:T(8,128)(2,1)S(1)}, u32[]{:S(2)}, u32[]{:S(2)}) collective-permute-start(bf16[4,64,128]{2,1,0:T(8,128)(2,1)S(1)} %get-tuple-element.45), channel_id=1, source_target_pairs={{0,0},{1,2},{2,4},{3,6},{4,1},{5,3},{6,5},{7,7},{8,8},{9,10},{10,1... | collective-permute-start | bytes 196616 | tf_op jit(solution)/shard_map/ppermute | solution.py:326
  89.9 5.6 %collective-permute-start.15 = (bf16[4,64,128]{2,1,0:T(8,128)(2,1)S(1)}, bf16[4,64,128]{2,1,0:T(8,128)(2,1)S(1)}, u32[]{:S(2)}, u32[]{:S(2)}) collective-permute-start(bf16[4,64,128]{2,1,0:T(8,128)(2,1)S(1)} %get-tuple-element.46), channel_id=1, source_target_pairs={{0,2},{1,0},{2,6},{3,4},{4,3},{5,1},{6,7},{7,5},{8,10},{9,8},{10,1... | collective-permute-start | bytes 196616 | tf_op jit(solution)/shard_map/ppermute | solution.py:326
  90.0 5.5 %collective-permute-start.16 = (bf16[4,64,128]{2,1,0:T(8,128)(2,1)S(1)}, bf16[4,64,128]{2,1,0:T(8,128)(2,1)S(1)}, u32[]{:S(2)}, u32[]{:S(2)}) collective-permute-start(bf16[4,64,128]{2,1,0:T(8,128)(2,1)S(1)} %get-tuple-element.47), channel_id=1, source_target_pairs={{0,4},{1,6},{2,0},{3,2},{4,5},{5,7},{6,1},{7,3},{8,12},{9,14},{10,... | collective-permute-start | bytes 196616 | tf_op jit(solution)/shard_map/ppermute | solution.py:326
  90.1 6.6 %collective-permute-start.17 = (bf16[4,64,128]{2,1,0:T(8,128)(2,1)S(1)}, bf16[4,64,128]{2,1,0:T(8,128)(2,1)S(1)}, u32[]{:S(2)}, u32[]{:S(2)}) collective-permute-start(bf16[4,64,128]{2,1,0:T(8,128)(2,1)S(1)} %get-tuple-element.48), channel_id=1, source_target_pairs={{0,6},{1,4},{2,2},{3,0},{4,7},{5,5},{6,3},{7,1},{8,14},{9,12},{10,... | collective-permute-start | bytes 196616 | tf_op jit(solution)/shard_map/ppermute | solution.py:326
  94.8 9.2 %collective-permute-start.31 = (bf16[16,64,128]{2,1,0:T(8,128)(2,1)S(1)}, bf16[16,64,128]{2,1,0:T(8,128)(2,1)S(1)}, u32[]{:S(2)}, u32[]{:S(2)}) collective-permute-start(bf16[16,64,128]{2,1,0:T(8,128)(2,1)S(1)} %join.3.refs_1_), channel_id=1, source_target_pairs={{0,8},{8,0},{16,24},{24,16},{1,9},{9,1},{17,25},{25,17},{2,10},{10... | collective-permute-start | bytes 786440 | tf_op jit(solution)/shard_map/ppermute | solution.py:256
  96.7 9.4 %collective-permute-start.32 = (bf16[16,64,128]{2,1,0:T(8,128)(2,1)S(1)}, bf16[16,64,128]{2,1,0:T(8,128)(2,1)S(1)}, u32[]{:S(2)}, u32[]{:S(2)}) collective-permute-start(bf16[16,64,128]{2,1,0:T(8,128)(2,1)S(1)} %join.2.refs_0_), channel_id=1, source_target_pairs={{0,16},{8,24},{16,0},{24,8},{1,17},{9,25},{17,1},{25,9},{2,18},{10... | collective-permute-start | bytes 786440 | tf_op jit(solution)/shard_map/ppermute | solution.py:256
  98.8 11.0 %collective-permute-start.33 = (bf16[16,64,128]{2,1,0:T(8,128)(2,1)S(1)}, bf16[16,64,128]{2,1,0:T(8,128)(2,1)S(1)}, u32[]{:S(2)}, u32[]{:S(2)}) collective-permute-start(bf16[16,64,128]{2,1,0:T(8,128)(2,1)S(1)} %join.3.refs_1_), channel_id=1, source_target_pairs={{0,16},{8,24},{16,0},{24,8},{1,17},{9,25},{17,1},{25,9},{2,18},{10... | collective-permute-start | bytes 786440 | tf_op jit(solution)/shard_map/ppermute | solution.py:256
  98.9 10.9 %collective-permute-start.30 = (bf16[16,64,128]{2,1,0:T(8,128)(2,1)S(1)}, bf16[16,64,128]{2,1,0:T(8,128)(2,1)S(1)}, u32[]{:S(2)}, u32[]{:S(2)}) collective-permute-start(bf16[16,64,128]{2,1,0:T(8,128)(2,1)S(1)} %join.2.refs_0_), channel_id=1, source_target_pairs={{0,8},{8,0},{16,24},{24,16},{1,9},{9,1},{17,25},{25,17},{2,10},{10... | collective-permute-start | bytes 786440 | tf_op jit(solution)/shard_map/ppermute | solution.py:256
  104.1 8.5 %collective-permute-start.35 = (bf16[16,64,128]{2,1,0:T(8,128)(2,1)S(1)}, bf16[16,64,128]{2,1,0:T(8,128)(2,1)S(1)}, u32[]{:S(2)}, u32[]{:S(2)}) collective-permute-start(bf16[16,64,128]{2,1,0:T(8,128)(2,1)S(1)} %collective-permute-done.31.refs_3_), channel_id=1, source_target_pairs={{0,16},{8,24},{16,0},{24,8},{1,17},{9,25},{17,1},{25,9},{2,18},{10... | collective-permute-start | bytes 786440 | tf_op jit(solution)/shard_map/ppermute | solution.py:256
  106.1 6.5 %collective-permute-start.34 = (bf16[16,64,128]{2,1,0:T(8,128)(2,1)S(1)}, bf16[16,64,128]{2,1,0:T(8,128)(2,1)S(1)}, u32[]{:S(2)}, u32[]{:S(2)}) collective-permute-start(bf16[16,64,128]{2,1,0:T(8,128)(2,1)S(1)} %collective-permute-done.32.refs_4_), channel_id=1, source_target_pairs={{0,8},{8,0},{16,24},{24,16},{1,9},{9,1},{17,25},{25,17},{2,10},{10... | collective-permute-start | bytes 786440 | tf_op jit(solution)/shard_map/ppermute | solution.py:256
  124.9 2.8 %collective-permute-start.41 = (s16[4,2,528,128]{3,2,1,0:T(8,128)(2,1)S(1)}, s16[4,2,528,128]{3,2,1,0:T(8,128)(2,1)S(1)}, u32[]{:S(2)}, u32[]{:S(2)}) collective-permute-start(s16[4,2,528,128]{3,2,1,0:T(8,128)(2,1)S(1)} %get-tuple-element.64), channel_id=1, source_target_pairs={{0,1},{1,0},{2,3},{3,2},{4,5},{5,4},{6,7},{7,6},{8,9},{9,8},{10,11... | collective-permute-start | bytes 3244040 | tf_op jit(solution)/shard_map/ppermute | solution.py:235
  124.9 9.4 %collective-permute-start.36 = (s16[4,2,528,128]{3,2,1,0:T(8,128)(2,1)S(1)}, s16[4,2,528,128]{3,2,1,0:T(8,128)(2,1)S(1)}, u32[]{:S(2)}, u32[]{:S(2)}) collective-permute-start(s16[4,2,528,128]{3,2,1,0:T(8,128)(2,1)S(1)} %get-tuple-element.63), channel_id=1, source_target_pairs={{0,1},{1,0},{2,3},{3,2},{4,5},{5,4},{6,7},{7,6},{8,9},{9,8},{10,11... | collective-permute-start | bytes 3244040 | tf_op jit(solution)/shard_map/ppermute | solution.py:235
  127.8 13.9 %collective-permute-start.42 = (s16[2,528,128]{2,1,0:T(8,128)(2,1)S(1)}, s16[2,528,128]{2,1,0:T(8,128)(2,1)S(1)}, u32[]{:S(2)}, u32[]{:S(2)}) collective-permute-start(s16[2,528,128]{2,1,0:T(8,128)(2,1)S(1)} %combine_message.21), channel_id=1, source_target_pairs={{0,2},{1,3},{2,0},{3,1},{4,6},{5,7},{6,4},{7,5},{8,10},{9,11},{10,... | collective-permute-start | bytes 811016 | tf_op jit(solution)/shard_map/ppermute | solution.py:238
  134.5 17.7 %collective-permute-start.37 = (s16[2,528,128]{2,1,0:T(8,128)(2,1)S(1)}, s16[2,528,128]{2,1,0:T(8,128)(2,1)S(1)}, u32[]{:S(2)}, u32[]{:S(2)}) collective-permute-start(s16[2,528,128]{2,1,0:T(8,128)(2,1)S(1)} %combine_message.18), channel_id=1, source_target_pairs={{0,2},{1,3},{2,0},{3,1},{4,6},{5,7},{6,4},{7,5},{8,10},{9,11},{10,... | collective-permute-start | bytes 811016 | tf_op jit(solution)/shard_map/ppermute | solution.py:238
  141.9 11.8 %collective-permute-start.43 = (s16[2,528,128]{2,1,0:T(8,128)(2,1)S(1)}, s16[2,528,128]{2,1,0:T(8,128)(2,1)S(1)}, u32[]{:S(2)}, u32[]{:S(2)}) collective-permute-start(s16[2,528,128]{2,1,0:T(8,128)(2,1)S(1)} %combine_message.22), channel_id=1, source_target_pairs={{0,2},{1,3},{6,4},{7,5},{2,6},{3,7},{4,0},{5,1},{8,10},{9,11},{14,... | collective-permute-start | bytes 811016 | tf_op jit(solution)/shard_map/ppermute | solution.py:240
  152.5 9.9 %collective-permute-start.38 = (s16[2,528,128]{2,1,0:T(8,128)(2,1)S(1)}, s16[2,528,128]{2,1,0:T(8,128)(2,1)S(1)}, u32[]{:S(2)}, u32[]{:S(2)}) collective-permute-start(s16[2,528,128]{2,1,0:T(8,128)(2,1)S(1)} %combine_message.19), channel_id=1, source_target_pairs={{0,2},{1,3},{6,4},{7,5},{2,6},{3,7},{4,0},{5,1},{8,10},{9,11},{14,... | collective-permute-start | bytes 811016 | tf_op jit(solution)/shard_map/ppermute | solution.py:240
  154.0 14.2 %collective-permute-start.44 = (s16[2,528,128]{2,1,0:T(8,128)(2,1)S(1)}, s16[2,528,128]{2,1,0:T(8,128)(2,1)S(1)}, u32[]{:S(2)}, u32[]{:S(2)}) collective-permute-start(s16[2,528,128]{2,1,0:T(8,128)(2,1)S(1)} %combine_message.23), channel_id=1, source_target_pairs={{0,2},{1,3},{6,4},{7,5},{8,10},{9,11},{14,12},{15,13},{16,18},{17,... | collective-permute-start | bytes 811016 | tf_op jit(solution)/shard_map/ppermute | solution.py:242
  155.3 14.3 %collective-permute-start.45 = (s16[2,528,128]{2,1,0:T(8,128)(2,1)S(1)}, s16[2,528,128]{2,1,0:T(8,128)(2,1)S(1)}, u32[]{:S(2)}, u32[]{:S(2)}) collective-permute-start(s16[2,528,128]{2,1,0:T(8,128)(2,1)S(1)} %combine_message.23), channel_id=1, source_target_pairs={{2,4},{3,5},{4,2},{5,3},{10,12},{11,13},{12,10},{13,11},{18,20},{1... | collective-permute-start | bytes 811016 | tf_op jit(solution)/shard_map/ppermute | solution.py:243
  162.6 10.2 %collective-permute-start.39 = (s16[2,528,128]{2,1,0:T(8,128)(2,1)S(1)}, s16[2,528,128]{2,1,0:T(8,128)(2,1)S(1)}, u32[]{:S(2)}, u32[]{:S(2)}) collective-permute-start(s16[2,528,128]{2,1,0:T(8,128)(2,1)S(1)} %combine_message.20), channel_id=1, source_target_pairs={{0,2},{1,3},{6,4},{7,5},{8,10},{9,11},{14,12},{15,13},{16,18},{17,... | collective-permute-start | bytes 811016 | tf_op jit(solution)/shard_map/ppermute | solution.py:242
  163.9 10.0 %collective-permute-start.40 = (s16[2,528,128]{2,1,0:T(8,128)(2,1)S(1)}, s16[2,528,128]{2,1,0:T(8,128)(2,1)S(1)}, u32[]{:S(2)}, u32[]{:S(2)}) collective-permute-start(s16[2,528,128]{2,1,0:T(8,128)(2,1)S(1)} %combine_message.20), channel_id=1, source_target_pairs={{2,4},{3,5},{4,2},{5,3},{10,12},{11,13},{12,10},{13,11},{18,20},{1... | collective-permute-start | bytes 811016 | tf_op jit(solution)/shard_map/ppermute | solution.py:243
  (1 other events, 1.0 us)

commit v3 on v2

--- a/solution.py
+++ b/solution.py
@@ -10,7 +10,7 @@
 GROUP = 8
 STEP = 32
 TOP = 14.0
-VMEM_LIMIT = 24 * 1024 * 1024
+SMALL = 4 * 1024 * 1024
 
 def message_rows(vec_width):
     return GROUP * vec_width + 16
@@ -51,50 +51,103 @@
 FAR = pl.BlockSpec(memory_space=pltpu.HBM)
 
 
-def product_kernel(places, shard, rows, cols, count, *refs):
-    total = len(refs) - 8
+def prepare_kernel(load, count, *refs):
+    total = len(refs) - (5 if load else 3)
     pieces = refs[:total]
-    blocks, acc, msg_low, msg_high, panel, held, piece_sem, block_sem = refs[total:]
+    if load:
+        blocks, panel, acc, held, sem = refs[total:]
+        slots = blocks.shape[0]
+        n = count[0, 0]
+
+        def block_copy(i):
+            span = pl.ds(i * STEP, STEP)
+            return pltpu.make_async_copy(blocks.at[span], held.at[span], sem.at[i])
+
+        for i in range(slots // STEP):
+
+            @pl.when(i * STEP < n)
+            def _():
+                block_copy(i).start()
+    else:
+        panel, acc, sem = refs[total:]
+
+    def piece_copy(i):
+        tiles = pieces[i].shape[0]
+        return pltpu.make_async_copy(pieces[i], panel.at[pl.ds(i * tiles, tiles)], sem.at[sem.shape[0] - 1 - i])
+
+    for i in range(total):
+        piece_copy(i).start()
+
+    @pl.loop(0, acc.shape[0])
+    def _(i):
+        acc[i] = jnp.zeros_like(acc[0])
+
+    for i in range(total):
+        piece_copy(i).wait()
+    if load:
+        for i in range(slots // STEP):
+
+            @pl.when(i * STEP < n)
+            def _():
+                block_copy(i).wait()
+
+
+def prepare(pieces, panel_tiles, acc_tiles, k, order, counts, blocks=None):
+    operands = [near(p) for p in pieces]
+    specs = [pl.BlockSpec(memory_space=pltpu.SMEM)] + [NEAR] * len(pieces)
+    out_shape = [
+        pltpu.VMEM((panel_tiles, k, order), jnp.bfloat16),
+        pltpu.VMEM((acc_tiles, k, order), jnp.float32),
+    ]
+    copies = len(pieces)
+    if blocks is not None:
+        operands.append(pltpu.with_memory_space_constraint(blocks, pltpu.HBM))
+        specs.append(FAR)
+        out_shape.append(pltpu.VMEM(blocks.shape, blocks.dtype))
+        copies += blocks.shape[0] // STEP
+    return pl.pallas_call(
+        functools.partial(prepare_kernel, blocks is not None),
+        out_shape=tuple(out_shape),
+        in_specs=specs,
+        out_specs=(NEAR,) * len(out_shape),
+        scratch_shapes=[pltpu.SemaphoreType.DMA((max(copies, 1),))],
+        compiler_params=pltpu.CompilerParams(vmem_limit_bytes=SMALL),
+        name="prepare",
+    )(counts, *operands)
+
+
+def product_kernel(place, shard, rows, cols, count, panel_in, acc_in, held, *refs):
+    total = len(refs) - 5
+    pieces = refs[:total]
+    panel, acc, msg_low, msg_high, sem = refs[total:]
     chips, groups = msg_low.shape[:2]
     k = panel.shape[1]
     row_total = acc.shape[0] - 1
-    slots = blocks.shape[0]
     n = count[0, 0]
     row_owner, col_owner = lax.axis_index("row"), lax.axis_index("col")
 
     def piece_copy(i):
-        piece, start, tiles, at = places[i]
-        there = panel.at[pl.ds(at(row_owner, col_owner // 2), tiles)]
-        return pltpu.make_async_copy(pieces[piece].at[pl.ds(start, tiles)], there, piece_sem.at[i])
-
-    def block_copy(i):
-        span = pl.ds(i * STEP, STEP)
-        return pltpu.make_async_copy(blocks.at[span], held.at[span], block_sem.at[i])
-
-    for i in range(len(places)):
+        tiles = pieces[i].shape[0]
+        start = panel.shape[0] - (total - i) * tiles
+        return pltpu.make_async_copy(pieces[i], panel.at[pl.ds(start, tiles)], sem.at[i])
+
+    for i in range(total):
         piece_copy(i).start()
-    for i in range(slots // STEP):
-
-        @pl.when(i * STEP < n)
-        def _():
-            block_copy(i).start()
-
-    @pl.loop(0, row_total + 1)
-    def _(i):
-        acc[i] = jnp.zeros_like(acc[0])
-
-    for i in range(len(places)):
+    for i in range(total):
         piece_copy(i).wait()
 
     @pl.loop(0, (n + STEP - 1) // STEP)
     def _(step):
-        block_copy(step).wait()
         base = step * STEP
         nil = jnp.zeros(panel.shape[1:], panel.dtype)
+
+        def entry(u):
+            return panel[place(cols[0, base + u], row_owner, col_owner // 2)]
+
         products = []
         for u in range(0, STEP, 2):
-            upper = jnp.concatenate([panel[cols[0, base + u]], nil], axis=1)
-            lower = jnp.concatenate([nil, panel[cols[0, base + u + 1]]], axis=1)
+            upper = jnp.concatenate([entry(u), nil], axis=1)
+            lower = jnp.concatenate([nil, entry(u + 1)], axis=1)
             both = lax.dot_general(
                 jnp.concatenate([upper, lower], axis=0),
                 jnp.concatenate([held[base + u], held[base + u + 1]], axis=1),
@@ -116,26 +169,20 @@
             encode([acc[base + t] for t in range(GROUP)], msg.at[d, g])
 
 
-def block_product(pieces, places, blocks, block_rows, block_cols, counts, shard, col_total):
-    slots, order, _ = blocks.shape
-    k = pieces[0].shape[1]
-    panel_tiles = sum(place[2] for place in places)
+def block_product(late, place, panel, acc, held, block_rows, block_cols, counts, shard, col_total):
+    _, k, order = panel.shape
     scalars = pl.BlockSpec(memory_space=pltpu.SMEM)
     message = pltpu.VMEM((col_total // 2, shard // GROUP // 2, message_rows(k), order), jnp.int16)
     return pl.pallas_call(
-        functools.partial(product_kernel, places, shard),
-        out_shape=(pltpu.VMEM((col_total * shard + 1, k, order), jnp.float32), message, message),
-        in_specs=[scalars] * 3 + [NEAR] * len(pieces) + [FAR],
-        out_specs=(NEAR, NEAR, NEAR),
-        scratch_shapes=[
-            pltpu.VMEM((panel_tiles, k, order), jnp.bfloat16),
-            pltpu.VMEM((slots, order, order), jnp.bfloat16),
-            pltpu.SemaphoreType.DMA((len(places),)),
-            pltpu.SemaphoreType.DMA((slots // STEP,)),
-        ],
-        compiler_params=pltpu.CompilerParams(vmem_limit_bytes=VMEM_LIMIT),
+        functools.partial(product_kernel, place, shard),
+        out_shape=(pltpu.VMEM(panel.shape, panel.dtype), pltpu.VMEM(acc.shape, acc.dtype), message, message),
+        in_specs=[scalars] * 3 + [NEAR] * (3 + len(late)),
+        out_specs=(NEAR,) * 4,
+        input_output_aliases={3: 0, 4: 1},
+        scratch_shapes=[pltpu.SemaphoreType.DMA((max(len(late), 1),))],
+        compiler_params=pltpu.CompilerParams(vmem_limit_bytes=SMALL),
         name="block_product",
-    )(block_rows, block_cols, counts, *[near(p) for p in pieces], pltpu.with_memory_space_constraint(blocks, pltpu.HBM))
+    )(block_rows, block_cols, counts, near(panel), near(acc), near(held), *[near(p) for p in late])[1:]
 
 
 def combine_kernel(half, which, gates, form, acc, sib, *refs):
@@ -213,7 +260,7 @@
         out_specs=out_spec,
         input_output_aliases=aliases,
         scratch_shapes=scratch,
-        compiler_params=pltpu.CompilerParams(vmem_limit_bytes=4 * 1024 * 1024),
+        compiler_params=pltpu.CompilerParams(vmem_limit_bytes=SMALL),
         name="combine_" + form,
     )(*operands)
 
@@ -267,64 +314,50 @@
 def vector_panel(tiles, row_total):
     shard = tiles.shape[0]
     if row_total != 4:
-        whole = lax.all_gather(tiles, "row", axis=0, tiled=True)
-        return (whole,), ((0, 0, row_total * shard, lambda r, z: 0),)
+        return (lax.all_gather(tiles, "row", axis=0, tiled=True),), lambda c, r, z: c
     half = shard // 2
-    places = []
-    for piece in range(8):
-        at = lambda r, z, piece=piece: (r ^ (piece // 2)) * shard + piece % 2 * half
-        places.append((piece, 0, half, at))
-    return gather_square(tiles[:half], tiles[half:]), tuple(places)
-
-
-def shuffle_kernel(pick, *refs):
-    half = len(refs) // 2
-    for i in range(half):
+    return gather_square(tiles[:half], tiles[half:]), lambda c, r, z: c ^ (r * shard)
+
+
+def shuffle_kernel(pick, merge, *refs):
+    total = len(refs) * merge // (merge + 1)
+    step = refs[0].shape[0]
+    for i in range(total):
         wanted = pick(lax.axis_index("row"), lax.axis_index("col"), i)
-        for j in range(half):
+        for j in range(total):
 
             @pl.when(wanted == j)
             def _():
-                refs[half + i][...] = refs[j][...]
-
-
-def shuffle(parts, pick):
+                refs[total + i // merge][i % merge * step : (i % merge + 1) * step] = refs[j][...]
+
+
+def shuffle(parts, pick, merge=1):
+    shape = (merge * parts[0].shape[0],) + parts[0].shape[1:]
     return pl.pallas_call(
-        functools.partial(shuffle_kernel, pick),
-        out_shape=tuple(pltpu.VMEM(x.shape, x.dtype) for x in parts),
+        functools.partial(shuffle_kernel, pick, merge),
+        out_shape=(pltpu.VMEM(shape, parts[0].dtype),) * (len(parts) // merge),
         in_specs=[NEAR] * len(parts),
-        out_specs=(NEAR,) * len(parts),
-        compiler_params=pltpu.CompilerParams(vmem_limit_bytes=1024 * 1024),
+        out_specs=(NEAR,) * (len(parts) // merge),
+        compiler_params=pltpu.CompilerParams(vmem_limit_bytes=SMALL),
         name="shuffle",
     )(*[near(x) for x in parts])
 
 
-def join_kernel(*refs):
-    step = refs[0].shape[0]
-    for i, ref in enumerate(refs[:-1]):
-        refs[-1][i * step : (i + 1) * step] = ref[...]
-
-
-def join(parts):
-    shape = (len(parts) * parts[0].shape[0],) + parts[0].shape[1:]
-    return pl.pallas_call(
-        join_kernel,
-        out_shape=pltpu.VMEM(shape, parts[0].dtype),
-        in_specs=[NEAR] * len(parts),
-        out_specs=NEAR,
-        compiler_params=pltpu.CompilerParams(vmem_limit_bytes=1024 * 1024),
-        name="join",
-    )(*[near(x) for x in parts])
-
-
 def spread(quarters):
-    parts = shuffle(quarters, lambda r, c, i: r ^ i)
-    parts = parts[:1] + tuple(across(parts[f], f) for f in (1, 2, 3))
-    parts = shuffle(parts, lambda r, c, i: r ^ (c % 4) ^ i)
+    parts = shuffle(quarters, lambda r, c, i: (r // 2 * 2 + c % 2) ^ i)
     got = []
-    for j in range(4):
-        got.append(lax.ppermute(parts[j], "col", [(c, 2 * (c % 4 ^ j) + c // 4) for c in range(8)]))
-    return join(got)
+    for i in range(4):
+        moves = []
+        for r in range(4):
+            for c in range(8):
+                moves.append((r * 8 + c, ((r // 2 * 2 + c % 2) ^ i) * 8 + c // 2 * 2 + r % 2))
+        got.append(lax.ppermute(parts[i], ("row", "col"), moves))
+    pairs = shuffle(tuple(got), lambda r, c, i: r ^ (c // 2 % 2 * 2 ^ i), merge=2)
+    got = []
+    for i in range(2):
+        moves = [(c, 2 * (c % 2 + 2 * (c // 2 % 2 ^ i)) + c // 4) for c in range(8)]
+        got.append(lax.ppermute(pairs[i], "col", moves))
+    return shuffle(tuple(got), lambda r, c, i: c // 4 ^ i, merge=2)[0]
 
 
 def first_panel(low, high, row_total, col_total):
@@ -335,26 +368,30 @@
         tiles = lax.ppermute(jnp.concatenate(low + high, axis=0), ("row", "col"), moves)
         return vector_panel(tiles, row_total)
     quarter = low[0].shape[0]
-    places = []
-    for piece in range(8):
-        for j in range(4):
-
-            def at(r, z, flip=piece // 2, which=piece % 2, j=j):
-                return (z ^ j) * 8 * quarter + which * 4 * quarter + (r ^ flip) * quarter
-
-            places.append((piece, j * quarter, quarter, at))
-    return gather_square(spread(low), spread(high)), tuple(places)
+
+    def place(c, r, z):
+        block, tile = lax.div(c, quarter), lax.rem(c, quarter)
+        part, which, owner = block >> 3, (block >> 2) & 1, block & 3
+        return ((((owner ^ r) * 2 + which) * 4) + part) * quarter + tile
+
+    return gather_square(spread(low), spread(high)), place
 
 
 def shards(row_total, col_total, vectors, blocks, block_rows, block_cols, counts):
     k, width = vectors.shape
     order = blocks.shape[2]
     shard = width // order
-    matrix = (blocks[0], block_rows, block_cols, counts, shard, col_total)
+    sizes = (row_total * shard, col_total * shard + 1, k, order)
+    index = (block_rows, block_cols, counts, shard, col_total)
     tiles = vectors.reshape(k, shard, order).transpose(1, 0, 2)
-    acc, low, high = block_product(*vector_panel(tiles, row_total), *matrix)
+    pieces, place = vector_panel(tiles, row_total)
+    early = len(pieces) * 3 // 4
+    panel, acc, held = prepare(pieces[:early], *sizes, counts, blocks[0])
+    acc, low, high = block_product(pieces[early:], place, panel, acc, held, *index)
     firsts = line_sum(0, acc, low, "tiles"), line_sum(1, acc, high, "tiles")
-    acc, low, high = block_product(*first_panel(*firsts, row_total, col_total), *matrix)
+    pieces, place = first_panel(*firsts, row_total, col_total)
+    panel, acc = prepare(pieces[:early], *sizes, counts)
+    acc, low, high = block_product(pieces[early:], place, panel, acc, held, *index)
     return line_sum(1, acc, high, "rows", line_sum(0, acc, low, "rows"))
 
 

time: 178 us -> 169 us (0.949)
  the two profiles are of different devices: /device:TPU:18 before, /device:TPU:12 now
where the time goes in v3:
time: 169 us; the launch traced here: 168 us
  waiting for transfers between devices  80.2 us (47%)
  starting transfers between devices  53.5 us (32%)
  Pallas kernels  31.6 us (19%)
    ppermute x4, waiting for transfers between devices, line_sum(): lax.ppermute(send, 'col', chip_moves([(0, 1), (1, 0), (2, 3), (3, 2)]))  30.3 us
    ppermute x12, waiting for transfers between devices, across(): return lax.ppermute(x, 'row', [(r, r ^ flip) for r in range(4)])  21.6 us
    pallas_call x2, Pallas kernels, block_product(): pl.pallas_call(functools.partial(product_kernel, place, shard), out_shape...  17.9 us
    ppermute x12, starting transfers between devices, across(): return lax.ppermute(x, 'row', [(r, r ^ flip) for r in range(4)])  15.1 us
    ppermute x4, starting transfers between devices, line_sum(): got_d = lax.ppermute(send, 'col', chip_moves([(1, 2), (2, 1)]))  14.6 us
    ppermute x4, waiting for transfers between devices, line_sum(): got_d = lax.ppermute(send, 'col', chip_moves([(1, 2), (2, 1)]))  11.9 us
    pallas_call x2, Pallas kernels, prepare(): pl.pallas_call(functools.partial(prepare_kernel, blocks is not None), out...  7.53 us
    ppermute x4, waiting for transfers between devices, line_sum(): sib = lax.ppermute(msg, 'col', [(c, c ^ 1) for c in range(2 * chips)])  6.95 us
  transfers between devices with their start and end apart: 44, of which 25 were waited for; matrix products, arithmetic and copies ran while one was open for 0% of the time, Pallas kernels for 8%

profile of v3, /device:TPU:12, one launch (start us, length us, event | category | flops | bytes accessed | tf_op | source)
XLA Modules:
  0.0 167.6 jit_solution(17932208312156278605)
XLA Ops:
  0.0 1.0 copy-done
  1.2 1.6 collective-permute-start.1
  3.3 1.5 collective-permute-start.3
  5.3 5.1 %collective-permute-done.1.refs_3_ = bf16[16,64,128]{2,1,0:T(8,128)(2,1)S(1)} collective-permute-done((bf16[16,64,128]{2,1,0:T(8,128)(2,1)S(1)}, bf16[16,64,128]{2,1,0:T(8,128)(2,1)S(1)}, u32[]{:S(2)}, u32[]{:S(2)}) %collective-permute-start.1) | collective-permute-done | bytes 262176 | tf_op jit(solution)/shard_map/ppermute | solution.py:303
  13.2 4.4 %collective-permute-done.3.refs_5_ = bf16[16,64,128]{2,1,0:T(8,128)(2,1)S(1)} collective-permute-done((bf16[16,64,128]{2,1,0:T(8,128)(2,1)S(1)}, bf16[16,64,128]{2,1,0:T(8,128)(2,1)S(1)}, u32[]{:S(2)}, u32[]{:S(2)}) %collective-permute-start.3) | collective-permute-done | bytes 262176 | tf_op jit(solution)/shard_map/ppermute | solution.py:303
  17.6 6.0 %prepare.2 = (bf16[128,64,128]{2,1,0:T(8,128)(2,1)S(1)}, f32[257,64,128]{2,1,0:T(8,128)S(1)}, bf16[512,128,128]{2,1,0:T(8,128)(2,1)S(1)}) custom-call(s32[1,1]{1,0:T(1,128)S(6)} %copy.19.count, bf16[16,64,128]{2,1,0:T(8,128)(2,1)S(1)} %get-tuple-element.68.refs_0_, bf16[16,64,128]{2,1,0:T(8,128)(2,1)S(1)} %get-tuple-element.67.refs_1_, ...), custom_call_target="tpu_custom_call" | custom-call | tf_op jit(solution)/shard_map/prepare/pallas_call | solution.py:108
  23.6 9.0 %block_product.2 = (bf16[128,64,128]{2,1,0:T(8,128)(2,1)S(1)}, f32[257,64,128]{2,1,0:T(8,128)S(1)}, s16[4,2,528,128]{3,2,1,0:T(8,128)(2,1)S(1)}, s16[4,2,528,128]{3,2,1,0:T(8,128)(2,1)S(1)}) custom-call(s32[1,512]{1,0:T(1,128)S(1)} %copy-done.2, s32[1,512]{1,0:T(1,128)S(1)} %copy-done.3, ...), custom_call_target="tpu_custom_call", output_to_operand_aliasing={{0}: (3, {}), {1}: (4, {})} | custom-call | tf_op jit(solution)/shard_map/block_product/pallas_call | solution.py:176
  33.2 2.2 %collective-permute-done.6.sib = s16[4,2,528,128]{3,2,1,0:T(8,128)(2,1)S(1)} collective-permute-done((s16[4,2,528,128]{3,2,1,0:T(8,128)(2,1)S(1)}, s16[4,2,528,128]{3,2,1,0:T(8,128)(2,1)S(1)}, u32[]{:S(2)}, u32[]{:S(2)}) %collective-permute-start.6) | collective-permute-done | bytes 1081376 | tf_op jit(solution)/shard_map/ppermute | solution.py:282
  35.7 1.3 collective-permute-done.17.sib
  38.0 7.1 %collective-permute-done.7.refs_0_ = s16[2,528,128]{2,1,0:T(8,128)(2,1)S(1)} collective-permute-done((s16[2,528,128]{2,1,0:T(8,128)(2,1)S(1)}, s16[2,528,128]{2,1,0:T(8,128)(2,1)S(1)}, u32[]{:S(2)}, u32[]{:S(2)}) %collective-permute-start.7) | collective-permute-done | bytes 270368 | tf_op jit(solution)/shard_map/ppermute | solution.py:285
  45.7 7.9 %collective-permute-done.18.refs_0_ = s16[2,528,128]{2,1,0:T(8,128)(2,1)S(1)} collective-permute-done((s16[2,528,128]{2,1,0:T(8,128)(2,1)S(1)}, s16[2,528,128]{2,1,0:T(8,128)(2,1)S(1)}, u32[]{:S(2)}, u32[]{:S(2)}) %collective-permute-start.18) | collective-permute-done | bytes 270368 | tf_op jit(solution)/shard_map/ppermute | solution.py:285
  53.9 2.6 %collective-permute-start.19 = (s16[2,528,128]{2,1,0:T(8,128)(2,1)S(1)}, s16[2,528,128]{2,1,0:T(8,128)(2,1)S(1)}, u32[]{:S(2)}, u32[]{:S(2)}) collective-permute-start(s16[2,528,128]{2,1,0:T(8,128)(2,1)S(1)} %combine_message.16), channel_id=1, source_target_pairs={{0,2},{1,3},{6,4},{7,5},{2,6},{3,7},{4,0},{5,1},{8,10},{9,11},{14,... | collective-permute-start | bytes 811016 | tf_op jit(solution)/shard_map/ppermute | solution.py:287
  56.7 3.3 %collective-permute-start.10 = (s16[2,528,128]{2,1,0:T(8,128)(2,1)S(1)}, s16[2,528,128]{2,1,0:T(8,128)(2,1)S(1)}, u32[]{:S(2)}, u32[]{:S(2)}) collective-permute-start(s16[2,528,128]{2,1,0:T(8,128)(2,1)S(1)} %combine_message.14), channel_id=1, source_target_pairs={{2,4},{3,5},{4,2},{5,3},{10,12},{11,13},{12,10},{13,11},{18,20},{1... | collective-permute-start | bytes 811016 | tf_op jit(solution)/shard_map/ppermute | solution.py:290
  60.0 1.3 collective-permute-start.9
  61.3 2.0 %collective-permute-done.19.refs_0_.refs_1_ = s16[2,528,128]{2,1,0:T(8,128)(2,1)S(1)} collective-permute-done((s16[2,528,128]{2,1,0:T(8,128)(2,1)S(1)}, s16[2,528,128]{2,1,0:T(8,128)(2,1)S(1)}, u32[]{:S(2)}, u32[]{:S(2)}) %collective-permute-start.19) | collective-permute-done | bytes 270368 | tf_op jit(solution)/shard_map/ppermute | solution.py:287
  63.6 3.3 %collective-permute-start.21 = (s16[2,528,128]{2,1,0:T(8,128)(2,1)S(1)}, s16[2,528,128]{2,1,0:T(8,128)(2,1)S(1)}, u32[]{:S(2)}, u32[]{:S(2)}) collective-permute-start(s16[2,528,128]{2,1,0:T(8,128)(2,1)S(1)} %combine_message.17), channel_id=1, source_target_pairs={{2,4},{3,5},{4,2},{5,3},{10,12},{11,13},{12,10},{13,11},{18,20},{1... | collective-permute-start | bytes 811016 | tf_op jit(solution)/shard_map/ppermute | solution.py:290
  66.9 1.3 collective-permute-start.20
  68.2 2.8 %collective-permute-done.10.refs_3_ = s16[2,528,128]{2,1,0:T(8,128)(2,1)S(1)} collective-permute-done((s16[2,528,128]{2,1,0:T(8,128)(2,1)S(1)}, s16[2,528,128]{2,1,0:T(8,128)(2,1)S(1)}, u32[]{:S(2)}, u32[]{:S(2)}) %collective-permute-start.10) | collective-permute-done | bytes 270368 | tf_op jit(solution)/shard_map/ppermute | solution.py:290
  72.3 3.0 %collective-permute-done.21.refs_3_ = s16[2,528,128]{2,1,0:T(8,128)(2,1)S(1)} collective-permute-done((s16[2,528,128]{2,1,0:T(8,128)(2,1)S(1)}, s16[2,528,128]{2,1,0:T(8,128)(2,1)S(1)}, u32[]{:S(2)}, u32[]{:S(2)}) %collective-permute-start.21) | collective-permute-done | bytes 270368 | tf_op jit(solution)/shard_map/ppermute | solution.py:290
  76.5 2.0 %collective-permute-start.23 = (bf16[4,64,128]{2,1,0:T(8,128)(2,1)S(1)}, bf16[4,64,128]{2,1,0:T(8,128)(2,1)S(1)}, u32[]{:S(2)}, u32[]{:S(2)}) collective-permute-start(bf16[4,64,128]{2,1,0:T(8,128)(2,1)S(1)} %get-tuple-element.57), channel_id=1, source_target_pairs={{0,8},{1,0},{2,10},{3,2},{4,12},{5,4},{6,14},{7,6},{8,9},{9,1},{10... | collective-permute-start | bytes 196616 | tf_op jit(solution)/shard_map/ppermute | solution.py:354
  78.5 3.0 %collective-permute-start.24 = (bf16[4,64,128]{2,1,0:T(8,128)(2,1)S(1)}, bf16[4,64,128]{2,1,0:T(8,128)(2,1)S(1)}, u32[]{:S(2)}, u32[]{:S(2)}) collective-permute-start(bf16[4,64,128]{2,1,0:T(8,128)(2,1)S(1)} %get-tuple-element.58), channel_id=1, source_target_pairs={{0,16},{1,24},{2,18},{3,26},{4,20},{5,28},{6,22},{7,30},{8,17},{9,... | collective-permute-start | bytes 196616 | tf_op jit(solution)/shard_map/ppermute | solution.py:354
  81.7 2.2 %collective-permute-start.15 = (bf16[8,64,128]{2,1,0:T(8,128)(2,1)S(1)}, bf16[8,64,128]{2,1,0:T(8,128)(2,1)S(1)}, u32[]{:S(2)}, u32[]{:S(2)}) collective-permute-start(bf16[8,64,128]{2,1,0:T(8,128)(2,1)S(1)} %get-tuple-element.49), channel_id=1, source_target_pairs={{0,0},{1,2},{2,4},{3,6},{4,1},{5,3},{6,5},{7,7},{8,8},{9,10},{10,1... | collective-permute-start | bytes 393224 | tf_op jit(solution)/shard_map/ppermute | solution.py:359
  84.5 1.5 collective-permute-done.25.refs_3_
  86.0 2.2 %collective-permute-start.26 = (bf16[8,64,128]{2,1,0:T(8,128)(2,1)S(1)}, bf16[8,64,128]{2,1,0:T(8,128)(2,1)S(1)}, u32[]{:S(2)}, u32[]{:S(2)}) collective-permute-start(bf16[8,64,128]{2,1,0:T(8,128)(2,1)S(1)} %get-tuple-element.60), channel_id=1, source_target_pairs={{0,0},{1,2},{2,4},{3,6},{4,1},{5,3},{6,5},{7,7},{8,8},{9,10},{10,1... | collective-permute-start | bytes 393224 | tf_op jit(solution)/shard_map/ppermute | solution.py:359
  89.0 2.5 %collective-permute-start.30 = (bf16[16,64,128]{2,1,0:T(8,128)(2,1)S(1)}, bf16[16,64,128]{2,1,0:T(8,128)(2,1)S(1)}, u32[]{:S(2)}, u32[]{:S(2)}) collective-permute-start(bf16[16,64,128]{2,1,0:T(8,128)(2,1)S(1)} %shuffle.8.refs_0_), channel_id=1, source_target_pairs={{0,16},{8,24},{16,0},{24,8},{1,17},{9,25},{17,1},{25,9},{2,18},{10... | collective-permute-start | bytes 786440 | tf_op jit(solution)/shard_map/ppermute | solution.py:303
  91.4 3.3 %collective-permute-done.26.refs_0_ = bf16[8,64,128]{2,1,0:T(8,128)(2,1)S(1)} collective-permute-done((bf16[8,64,128]{2,1,0:T(8,128)(2,1)S(1)}, bf16[8,64,128]{2,1,0:T(8,128)(2,1)S(1)}, u32[]{:S(2)}, u32[]{:S(2)}) %collective-permute-start.26) | collective-permute-done | bytes 131104 | tf_op jit(solution)/shard_map/ppermute | solution.py:359
  94.8 2.0 %collective-permute-start.28 = (bf16[16,64,128]{2,1,0:T(8,128)(2,1)S(1)}, bf16[16,64,128]{2,1,0:T(8,128)(2,1)S(1)}, u32[]{:S(2)}, u32[]{:S(2)}) collective-permute-start(bf16[16,64,128]{2,1,0:T(8,128)(2,1)S(1)} %shuffle.8.refs_0_), channel_id=1, source_target_pairs={{0,8},{8,0},{16,24},{24,16},{1,9},{9,1},{17,25},{25,17},{2,10},{10... | collective-permute-start | bytes 786440 | tf_op jit(solution)/shard_map/ppermute | solution.py:303
  96.8 2.4 %collective-permute-start.31 = (bf16[16,64,128]{2,1,0:T(8,128)(2,1)S(1)}, bf16[16,64,128]{2,1,0:T(8,128)(2,1)S(1)}, u32[]{:S(2)}, u32[]{:S(2)}) collective-permute-start(bf16[16,64,128]{2,1,0:T(8,128)(2,1)S(1)} %shuffle.11.refs_1_), channel_id=1, source_target_pairs={{0,16},{8,24},{16,0},{24,8},{1,17},{9,25},{17,1},{25,9},{2,18},{10... | collective-permute-start | bytes 786440 | tf_op jit(solution)/shard_map/ppermute | solution.py:303
  99.5 4.1 %collective-permute-done.29.refs_3_ = bf16[16,64,128]{2,1,0:T(8,128)(2,1)S(1)} collective-permute-done((bf16[16,64,128]{2,1,0:T(8,128)(2,1)S(1)}, bf16[16,64,128]{2,1,0:T(8,128)(2,1)S(1)}, u32[]{:S(2)}, u32[]{:S(2)}) %collective-permute-start.29) | collective-permute-done | bytes 262176 | tf_op jit(solution)/shard_map/ppermute | solution.py:303
  103.6 2.8 %collective-permute-start.33 = (bf16[16,64,128]{2,1,0:T(8,128)(2,1)S(1)}, bf16[16,64,128]{2,1,0:T(8,128)(2,1)S(1)}, u32[]{:S(2)}, u32[]{:S(2)}) collective-permute-start(bf16[16,64,128]{2,1,0:T(8,128)(2,1)S(1)} %collective-permute-done.29.refs_3_), channel_id=1, source_target_pairs={{0,16},{8,24},{16,0},{24,8},{1,17},{9,25},{17,1},{25,9},{2,18},{10... | collective-permute-start | bytes 786440 | tf_op jit(solution)/shard_map/ppermute | solution.py:303
  106.4 2.8 %collective-permute-done.28.refs_2_ = bf16[16,64,128]{2,1,0:T(8,128)(2,1)S(1)} collective-permute-done((bf16[16,64,128]{2,1,0:T(8,128)(2,1)S(1)}, bf16[16,64,128]{2,1,0:T(8,128)(2,1)S(1)}, u32[]{:S(2)}, u32[]{:S(2)}) %collective-permute-start.28) | collective-permute-done | bytes 262176 | tf_op jit(solution)/shard_map/ppermute | solution.py:303
  109.2 1.5 prepare.3
  110.8 4.1 %collective-permute-done.32.refs_0_ = bf16[16,64,128]{2,1,0:T(8,128)(2,1)S(1)} collective-permute-done((bf16[16,64,128]{2,1,0:T(8,128)(2,1)S(1)}, bf16[16,64,128]{2,1,0:T(8,128)(2,1)S(1)}, u32[]{:S(2)}, u32[]{:S(2)}) %collective-permute-start.32) | collective-permute-done | bytes 262176 | tf_op jit(solution)/shard_map/ppermute | solution.py:303
  114.8 8.9 %block_product.3 = (bf16[128,64,128]{2,1,0:T(8,128)(2,1)S(1)}, f32[257,64,128]{2,1,0:T(8,128)S(1)}, s16[4,2,528,128]{3,2,1,0:T(8,128)(2,1)S(1)}, s16[4,2,528,128]{3,2,1,0:T(8,128)(2,1)S(1)}) custom-call(s32[1,512]{1,0:T(1,128)S(1)} %copy-done.2, s32[1,512]{1,0:T(1,128)S(1)} %copy-done.3, ...), custom_call_target="tpu_custom_call", output_to_operand_aliasing={{0}: (3, {}), {1}: (4, {})} | custom-call | tf_op jit(solution)/shard_map/block_product/pallas_call | solution.py:176
  124.3 2.2 %collective-permute-done.39.sib = s16[4,2,528,128]{3,2,1,0:T(8,128)(2,1)S(1)} collective-permute-done((s16[4,2,528,128]{3,2,1,0:T(8,128)(2,1)S(1)}, s16[4,2,528,128]{3,2,1,0:T(8,128)(2,1)S(1)}, u32[]{:S(2)}, u32[]{:S(2)}) %collective-permute-start.39) | collective-permute-done | bytes 1081376 | tf_op jit(solution)/shard_map/ppermute | solution.py:282
  126.8 1.3 collective-permute-done.34.sib
  129.1 7.1 %collective-permute-done.40.refs_0_ = s16[2,528,128]{2,1,0:T(8,128)(2,1)S(1)} collective-permute-done((s16[2,528,128]{2,1,0:T(8,128)(2,1)S(1)}, s16[2,528,128]{2,1,0:T(8,128)(2,1)S(1)}, u32[]{:S(2)}, u32[]{:S(2)}) %collective-permute-start.40) | collective-permute-done | bytes 270368 | tf_op jit(solution)/shard_map/ppermute | solution.py:285
  136.5 8.2 %collective-permute-done.35.refs_0_ = s16[2,528,128]{2,1,0:T(8,128)(2,1)S(1)} collective-permute-done((s16[2,528,128]{2,1,0:T(8,128)(2,1)S(1)}, s16[2,528,128]{2,1,0:T(8,128)(2,1)S(1)}, u32[]{:S(2)}, u32[]{:S(2)}) %collective-permute-start.35) | collective-permute-done | bytes 270368 | tf_op jit(solution)/shard_map/ppermute | solution.py:285
  145.0 1.5 collective-permute-start.36
  147.2 4.0 %collective-permute-start.43 = (s16[2,528,128]{2,1,0:T(8,128)(2,1)S(1)}, s16[2,528,128]{2,1,0:T(8,128)(2,1)S(1)}, u32[]{:S(2)}, u32[]{:S(2)}) collective-permute-start(s16[2,528,128]{2,1,0:T(8,128)(2,1)S(1)} %combine_message.23), channel_id=1, source_target_pairs={{2,4},{3,5},{4,2},{5,3},{10,12},{11,13},{12,10},{13,11},{18,20},{1... | collective-permute-start | bytes 811016 | tf_op jit(solution)/shard_map/ppermute | solution.py:290
  151.2 1.3 collective-permute-start.42
  152.5 1.3 collective-permute-done.36.refs_0_.refs_1_
  154.0 4.0 %collective-permute-start.38 = (s16[2,528,128]{2,1,0:T(8,128)(2,1)S(1)}, s16[2,528,128]{2,1,0:T(8,128)(2,1)S(1)}, u32[]{:S(2)}, u32[]{:S(2)}) collective-permute-start(s16[2,528,128]{2,1,0:T(8,128)(2,1)S(1)} %combine_message.20), channel_id=1, source_target_pairs={{2,4},{3,5},{4,2},{5,3},{10,12},{11,13},{12,10},{13,11},{18,20},{1... | collective-permute-start | bytes 811016 | tf_op jit(solution)/shard_map/ppermute | solution.py:290
  158.0 1.3 collective-permute-start.37
  159.3 2.8 %collective-permute-done.43.refs_3_ = s16[2,528,128]{2,1,0:T(8,128)(2,1)S(1)} collective-permute-done((s16[2,528,128]{2,1,0:T(8,128)(2,1)S(1)}, s16[2,528,128]{2,1,0:T(8,128)(2,1)S(1)}, u32[]{:S(2)}, u32[]{:S(2)}) %collective-permute-start.43) | collective-permute-done | bytes 270368 | tf_op jit(solution)/shard_map/ppermute | solution.py:290
  162.1 1.1 combine_rows.2.refs_4_
  163.2 3.3 %collective-permute-done.38.refs_3_ = s16[2,528,128]{2,1,0:T(8,128)(2,1)S(1)} collective-permute-done((s16[2,528,128]{2,1,0:T(8,128)(2,1)S(1)}, s16[2,528,128]{2,1,0:T(8,128)(2,1)S(1)}, u32[]{:S(2)}, u32[]{:S(2)}) %collective-permute-start.38) | collective-permute-done | bytes 270368 | tf_op jit(solution)/shard_map/ppermute | solution.py:290
  166.5 1.1 combine_rows.3
  (76 shorter events, 14.1 us)
Async XLA Ops:
  0.0 1.0 copy-start
  1.2 9.2 %collective-permute-start.1 = (bf16[16,64,128]{2,1,0:T(8,128)(2,1)S(1)}, bf16[16,64,128]{2,1,0:T(8,128)(2,1)S(1)}, u32[]{:S(2)}, u32[]{:S(2)}) collective-permute-start(bf16[16,64,128]{2,1,0:T(8,128)(2,1)S(1)} %get-tuple-element.67.refs_1_), channel_id=1, source_target_pairs={{0,8},{8,0},{16,24},{24,16},{1,9},{9,1},{17,25},{25,17},{2,10},{10... | collective-permute-start | bytes 786440 | tf_op jit(solution)/shard_map/ppermute | solution.py:303
  2.8 9.2 %collective-permute-start.2 = (bf16[16,64,128]{2,1,0:T(8,128)(2,1)S(1)}, bf16[16,64,128]{2,1,0:T(8,128)(2,1)S(1)}, u32[]{:S(2)}, u32[]{:S(2)}) collective-permute-start(bf16[16,64,128]{2,1,0:T(8,128)(2,1)S(1)} %get-tuple-element.68.refs_0_), channel_id=1, source_target_pairs={{0,16},{8,24},{16,0},{24,8},{1,17},{9,25},{17,1},{25,9},{2,18},{10... | collective-permute-start | bytes 786440 | tf_op jit(solution)/shard_map/ppermute | solution.py:303
  3.3 14.3 %collective-permute-start.3 = (bf16[16,64,128]{2,1,0:T(8,128)(2,1)S(1)}, bf16[16,64,128]{2,1,0:T(8,128)(2,1)S(1)}, u32[]{:S(2)}, u32[]{:S(2)}) collective-permute-start(bf16[16,64,128]{2,1,0:T(8,128)(2,1)S(1)} %get-tuple-element.67.refs_1_), channel_id=1, source_target_pairs={{0,16},{8,24},{16,0},{24,8},{1,17},{9,25},{17,1},{25,9},{2,18},{10... | collective-permute-start | bytes 786440 | tf_op jit(solution)/shard_map/ppermute | solution.py:303
  4.8 12.8 %collective-permute-start = (bf16[16,64,128]{2,1,0:T(8,128)(2,1)S(1)}, bf16[16,64,128]{2,1,0:T(8,128)(2,1)S(1)}, u32[]{:S(2)}, u32[]{:S(2)}) collective-permute-start(bf16[16,64,128]{2,1,0:T(8,128)(2,1)S(1)} %get-tuple-element.68.refs_0_), channel_id=1, source_target_pairs={{0,8},{8,0},{16,24},{24,16},{1,9},{9,1},{17,25},{25,17},{2,10},{10... | collective-permute-start | bytes 786440 | tf_op jit(solution)/shard_map/ppermute | solution.py:303
  10.5 13.1 %collective-permute-start.5 = (bf16[16,64,128]{2,1,0:T(8,128)(2,1)S(1)}, bf16[16,64,128]{2,1,0:T(8,128)(2,1)S(1)}, u32[]{:S(2)}, u32[]{:S(2)}) collective-permute-start(bf16[16,64,128]{2,1,0:T(8,128)(2,1)S(1)} %collective-permute-done.1.refs_3_), channel_id=1, source_target_pairs={{0,16},{8,24},{16,0},{24,8},{1,17},{9,25},{17,1},{25,9},{2,18},{10... | collective-permute-start | bytes 786440 | tf_op jit(solution)/shard_map/ppermute | solution.py:303
  12.0 11.7 %collective-permute-start.4 = (bf16[16,64,128]{2,1,0:T(8,128)(2,1)S(1)}, bf16[16,64,128]{2,1,0:T(8,128)(2,1)S(1)}, u32[]{:S(2)}, u32[]{:S(2)}) collective-permute-start(bf16[16,64,128]{2,1,0:T(8,128)(2,1)S(1)} %collective-permute-done.2.refs_4_), channel_id=1, source_target_pairs={{0,8},{8,0},{16,24},{24,16},{1,9},{9,1},{17,25},{25,17},{2,10},{10... | collective-permute-start | bytes 786440 | tf_op jit(solution)/shard_map/ppermute | solution.py:303
  17.6 6.0 %copy-start.2 = (s32[1,512]{1,0:T(1,128)S(1)}, s32[1,512]{1,0:T(1,128)}, u32[]{:S(2)}) copy-start(s32[1,512]{1,0:T(1,128)} %rows.3) | copy-start | bytes 6148
  17.6 6.1 %copy-start.3 = (s32[1,512]{1,0:T(1,128)S(1)}, s32[1,512]{1,0:T(1,128)}, u32[]{:S(2)}) copy-start(s32[1,512]{1,0:T(1,128)} %cols.3) | copy-start | bytes 6148
  32.7 2.8 %collective-permute-start.6 = (s16[4,2,528,128]{3,2,1,0:T(8,128)(2,1)S(1)}, s16[4,2,528,128]{3,2,1,0:T(8,128)(2,1)S(1)}, u32[]{:S(2)}, u32[]{:S(2)}) collective-permute-start(s16[4,2,528,128]{3,2,1,0:T(8,128)(2,1)S(1)} %get-tuple-element.40), channel_id=1, source_target_pairs={{0,1},{1,0},{2,3},{3,2},{4,5},{5,4},{6,7},{7,6},{8,9},{9,8},{10,11... | collective-permute-start | bytes 3244040 | tf_op jit(solution)/shard_map/ppermute | solution.py:282
  32.7 4.2 %collective-permute-start.17 = (s16[4,2,528,128]{3,2,1,0:T(8,128)(2,1)S(1)}, s16[4,2,528,128]{3,2,1,0:T(8,128)(2,1)S(1)}, u32[]{:S(2)}, u32[]{:S(2)}) collective-permute-start(s16[4,2,528,128]{3,2,1,0:T(8,128)(2,1)S(1)} %get-tuple-element.51), channel_id=1, source_target_pairs={{0,1},{1,0},{2,3},{3,2},{4,5},{5,4},{6,7},{7,6},{8,9},{9,8},{10,11... | collective-permute-start | bytes 3244040 | tf_op jit(solution)/shard_map/ppermute | solution.py:282
  35.6 9.4 %collective-permute-start.7 = (s16[2,528,128]{2,1,0:T(8,128)(2,1)S(1)}, s16[2,528,128]{2,1,0:T(8,128)(2,1)S(1)}, u32[]{:S(2)}, u32[]{:S(2)}) collective-permute-start(s16[2,528,128]{2,1,0:T(8,128)(2,1)S(1)} %combine_message.12), channel_id=1, source_target_pairs={{0,2},{1,3},{2,0},{3,1},{4,6},{5,7},{6,4},{7,5},{8,10},{9,11},{10,... | collective-permute-start | bytes 811016 | tf_op jit(solution)/shard_map/ppermute | solution.py:285
  37.2 16.4 %collective-permute-start.18 = (s16[2,528,128]{2,1,0:T(8,128)(2,1)S(1)}, s16[2,528,128]{2,1,0:T(8,128)(2,1)S(1)}, u32[]{:S(2)}, u32[]{:S(2)}) collective-permute-start(s16[2,528,128]{2,1,0:T(8,128)(2,1)S(1)} %combine_message.15), channel_id=1, source_target_pairs={{0,2},{1,3},{2,0},{3,1},{4,6},{5,7},{6,4},{7,5},{8,10},{9,11},{10,... | collective-permute-start | bytes 811016 | tf_op jit(solution)/shard_map/ppermute | solution.py:285
  45.3 11.2 %collective-permute-start.8 = (s16[2,528,128]{2,1,0:T(8,128)(2,1)S(1)}, s16[2,528,128]{2,1,0:T(8,128)(2,1)S(1)}, u32[]{:S(2)}, u32[]{:S(2)}) collective-permute-start(s16[2,528,128]{2,1,0:T(8,128)(2,1)S(1)} %combine_message.13), channel_id=1, source_target_pairs={{0,2},{1,3},{6,4},{7,5},{2,6},{3,7},{4,0},{5,1},{8,10},{9,11},{14,... | collective-permute-start | bytes 811016 | tf_op jit(solution)/shard_map/ppermute | solution.py:287
  53.9 9.5 %collective-permute-start.19 = (s16[2,528,128]{2,1,0:T(8,128)(2,1)S(1)}, s16[2,528,128]{2,1,0:T(8,128)(2,1)S(1)}, u32[]{:S(2)}, u32[]{:S(2)}) collective-permute-start(s16[2,528,128]{2,1,0:T(8,128)(2,1)S(1)} %combine_message.16), channel_id=1, source_target_pairs={{0,2},{1,3},{6,4},{7,5},{2,6},{3,7},{4,0},{5,1},{8,10},{9,11},{14,... | collective-permute-start | bytes 811016 | tf_op jit(solution)/shard_map/ppermute | solution.py:287
  56.7 14.3 %collective-permute-start.10 = (s16[2,528,128]{2,1,0:T(8,128)(2,1)S(1)}, s16[2,528,128]{2,1,0:T(8,128)(2,1)S(1)}, u32[]{:S(2)}, u32[]{:S(2)}) collective-permute-start(s16[2,528,128]{2,1,0:T(8,128)(2,1)S(1)} %combine_message.14), channel_id=1, source_target_pairs={{2,4},{3,5},{4,2},{5,3},{10,12},{11,13},{12,10},{13,11},{18,20},{1... | collective-permute-start | bytes 811016 | tf_op jit(solution)/shard_map/ppermute | solution.py:290
  60.0 10.9 %collective-permute-start.9 = (s16[2,528,128]{2,1,0:T(8,128)(2,1)S(1)}, s16[2,528,128]{2,1,0:T(8,128)(2,1)S(1)}, u32[]{:S(2)}, u32[]{:S(2)}) collective-permute-start(s16[2,528,128]{2,1,0:T(8,128)(2,1)S(1)} %combine_message.14), channel_id=1, source_target_pairs={{0,2},{1,3},{6,4},{7,5},{8,10},{9,11},{14,12},{15,13},{16,18},{17,... | collective-permute-start | bytes 811016 | tf_op jit(solution)/shard_map/ppermute | solution.py:289
  63.6 11.8 %collective-permute-start.21 = (s16[2,528,128]{2,1,0:T(8,128)(2,1)S(1)}, s16[2,528,128]{2,1,0:T(8,128)(2,1)S(1)}, u32[]{:S(2)}, u32[]{:S(2)}) collective-permute-start(s16[2,528,128]{2,1,0:T(8,128)(2,1)S(1)} %combine_message.17), channel_id=1, source_target_pairs={{2,4},{3,5},{4,2},{5,3},{10,12},{11,13},{12,10},{13,11},{18,20},{1... | collective-permute-start | bytes 811016 | tf_op jit(solution)/shard_map/ppermute | solution.py:290
  66.9 8.5 %collective-permute-start.20 = (s16[2,528,128]{2,1,0:T(8,128)(2,1)S(1)}, s16[2,528,128]{2,1,0:T(8,128)(2,1)S(1)}, u32[]{:S(2)}, u32[]{:S(2)}) collective-permute-start(s16[2,528,128]{2,1,0:T(8,128)(2,1)S(1)} %combine_message.17), channel_id=1, source_target_pairs={{0,2},{1,3},{6,4},{7,5},{8,10},{9,11},{14,12},{15,13},{16,18},{17,... | collective-permute-start | bytes 811016 | tf_op jit(solution)/shard_map/ppermute | solution.py:289
  71.5 5.1 %collective-permute-start.11 = (bf16[4,64,128]{2,1,0:T(8,128)(2,1)S(1)}, bf16[4,64,128]{2,1,0:T(8,128)(2,1)S(1)}, u32[]{:S(2)}, u32[]{:S(2)}) collective-permute-start(bf16[4,64,128]{2,1,0:T(8,128)(2,1)S(1)} %get-tuple-element.45), channel_id=1, source_target_pairs={{0,0},{1,8},{2,2},{3,10},{4,4},{5,12},{6,6},{7,14},{8,1},{9,9},{10... | collective-permute-start | bytes 196616 | tf_op jit(solution)/shard_map/ppermute | solution.py:354
  72.1 6.4 %collective-permute-start.12 = (bf16[4,64,128]{2,1,0:T(8,128)(2,1)S(1)}, bf16[4,64,128]{2,1,0:T(8,128)(2,1)S(1)}, u32[]{:S(2)}, u32[]{:S(2)}) collective-permute-start(bf16[4,64,128]{2,1,0:T(8,128)(2,1)S(1)} %get-tuple-element.46), channel_id=1, source_target_pairs={{0,8},{1,0},{2,10},{3,2},{4,12},{5,4},{6,14},{7,6},{8,9},{9,1},{10... | collective-permute-start | bytes 196616 | tf_op jit(solution)/shard_map/ppermute | solution.py:354
  72.3 9.2 %collective-permute-start.13 = (bf16[4,64,128]{2,1,0:T(8,128)(2,1)S(1)}, bf16[4,64,128]{2,1,0:T(8,128)(2,1)S(1)}, u32[]{:S(2)}, u32[]{:S(2)}) collective-permute-start(bf16[4,64,128]{2,1,0:T(8,128)(2,1)S(1)} %get-tuple-element.47), channel_id=1, source_target_pairs={{0,16},{1,24},{2,18},{3,26},{4,20},{5,28},{6,22},{7,30},{8,17},{9,... | collective-permute-start | bytes 196616 | tf_op jit(solution)/shard_map/ppermute | solution.py:354
  75.4 6.2 %collective-permute-start.14 = (bf16[4,64,128]{2,1,0:T(8,128)(2,1)S(1)}, bf16[4,64,128]{2,1,0:T(8,128)(2,1)S(1)}, u32[]{:S(2)}, u32[]{:S(2)}) collective-permute-start(bf16[4,64,128]{2,1,0:T(8,128)(2,1)S(1)} %get-tuple-element.48), channel_id=1, source_target_pairs={{0,24},{1,16},{2,26},{3,18},{4,28},{5,20},{6,30},{7,22},{8,25},{9,... | collective-permute-start | bytes 196616 | tf_op jit(solution)/shard_map/ppermute | solution.py:354
  75.9 8.1 %collective-permute-start.22 = (bf16[4,64,128]{2,1,0:T(8,128)(2,1)S(1)}, bf16[4,64,128]{2,1,0:T(8,128)(2,1)S(1)}, u32[]{:S(2)}, u32[]{:S(2)}) collective-permute-start(bf16[4,64,128]{2,1,0:T(8,128)(2,1)S(1)} %get-tuple-element.56), channel_id=1, source_target_pairs={{0,0},{1,8},{2,2},{3,10},{4,4},{5,12},{6,6},{7,14},{8,1},{9,9},{10... | collective-permute-start | bytes 196616 | tf_op jit(solution)/shard_map/ppermute | solution.py:354
  76.5 7.5 %collective-permute-start.23 = (bf16[4,64,128]{2,1,0:T(8,128)(2,1)S(1)}, bf16[4,64,128]{2,1,0:T(8,128)(2,1)S(1)}, u32[]{:S(2)}, u32[]{:S(2)}) collective-permute-start(bf16[4,64,128]{2,1,0:T(8,128)(2,1)S(1)} %get-tuple-element.57), channel_id=1, source_target_pairs={{0,8},{1,0},{2,10},{3,2},{4,12},{5,4},{6,14},{7,6},{8,9},{9,1},{10... | collective-permute-start | bytes 196616 | tf_op jit(solution)/shard_map/ppermute | solution.py:354
  78.5 6.0 %collective-permute-start.24 = (bf16[4,64,128]{2,1,0:T(8,128)(2,1)S(1)}, bf16[4,64,128]{2,1,0:T(8,128)(2,1)S(1)}, u32[]{:S(2)}, u32[]{:S(2)}) collective-permute-start(bf16[4,64,128]{2,1,0:T(8,128)(2,1)S(1)} %get-tuple-element.58), channel_id=1, source_target_pairs={{0,16},{1,24},{2,18},{3,26},{4,20},{5,28},{6,22},{7,30},{8,17},{9,... | collective-permute-start | bytes 196616 | tf_op jit(solution)/shard_map/ppermute | solution.py:354
  81.6 4.4 %collective-permute-start.25 = (bf16[4,64,128]{2,1,0:T(8,128)(2,1)S(1)}, bf16[4,64,128]{2,1,0:T(8,128)(2,1)S(1)}, u32[]{:S(2)}, u32[]{:S(2)}) collective-permute-start(bf16[4,64,128]{2,1,0:T(8,128)(2,1)S(1)} %get-tuple-element.59), channel_id=1, source_target_pairs={{0,24},{1,16},{2,26},{3,18},{4,28},{5,20},{6,30},{7,22},{8,25},{9,... | collective-permute-start | bytes 196616 | tf_op jit(solution)/shard_map/ppermute | solution.py:354
  81.7 7.2 %collective-permute-start.15 = (bf16[8,64,128]{2,1,0:T(8,128)(2,1)S(1)}, bf16[8,64,128]{2,1,0:T(8,128)(2,1)S(1)}, u32[]{:S(2)}, u32[]{:S(2)}) collective-permute-start(bf16[8,64,128]{2,1,0:T(8,128)(2,1)S(1)} %get-tuple-element.49), channel_id=1, source_target_pairs={{0,0},{1,2},{2,4},{3,6},{4,1},{5,3},{6,5},{7,7},{8,8},{9,10},{10,1... | collective-permute-start | bytes 393224 | tf_op jit(solution)/shard_map/ppermute | solution.py:359
  84.0 5.0 %collective-permute-start.16 = (bf16[8,64,128]{2,1,0:T(8,128)(2,1)S(1)}, bf16[8,64,128]{2,1,0:T(8,128)(2,1)S(1)}, u32[]{:S(2)}, u32[]{:S(2)}) collective-permute-start(bf16[8,64,128]{2,1,0:T(8,128)(2,1)S(1)} %get-tuple-element.50), channel_id=1, source_target_pairs={{0,4},{1,6},{2,0},{3,2},{4,5},{5,7},{6,1},{7,3},{8,12},{9,14},{10,... | collective-permute-start | bytes 393224 | tf_op jit(solution)/shard_map/ppermute | solution.py:359
  86.0 8.7 %collective-permute-start.26 = (bf16[8,64,128]{2,1,0:T(8,128)(2,1)S(1)}, bf16[8,64,128]{2,1,0:T(8,128)(2,1)S(1)}, u32[]{:S(2)}, u32[]{:S(2)}) collective-permute-start(bf16[8,64,128]{2,1,0:T(8,128)(2,1)S(1)} %get-tuple-element.60), channel_id=1, source_target_pairs={{0,0},{1,2},{2,4},{3,6},{4,1},{5,3},{6,5},{7,7},{8,8},{9,10},{10,1... | collective-permute-start | bytes 393224 | tf_op jit(solution)/shard_map/ppermute | solution.py:359
  88.3 6.4 %collective-permute-start.27 = (bf16[8,64,128]{2,1,0:T(8,128)(2,1)S(1)}, bf16[8,64,128]{2,1,0:T(8,128)(2,1)S(1)}, u32[]{:S(2)}, u32[]{:S(2)}) collective-permute-start(bf16[8,64,128]{2,1,0:T(8,128)(2,1)S(1)} %get-tuple-element.61), channel_id=1, source_target_pairs={{0,4},{1,6},{2,0},{3,2},{4,5},{5,7},{6,1},{7,3},{8,12},{9,14},{10,... | collective-permute-start | bytes 393224 | tf_op jit(solution)/shard_map/ppermute | solution.py:359
  89.0 10.3 %collective-permute-start.30 = (bf16[16,64,128]{2,1,0:T(8,128)(2,1)S(1)}, bf16[16,64,128]{2,1,0:T(8,128)(2,1)S(1)}, u32[]{:S(2)}, u32[]{:S(2)}) collective-permute-start(bf16[16,64,128]{2,1,0:T(8,128)(2,1)S(1)} %shuffle.8.refs_0_), channel_id=1, source_target_pairs={{0,16},{8,24},{16,0},{24,8},{1,17},{9,25},{17,1},{25,9},{2,18},{10... | collective-permute-start | bytes 786440 | tf_op jit(solution)/shard_map/ppermute | solution.py:303
  94.7 8.9 %collective-permute-start.29 = (bf16[16,64,128]{2,1,0:T(8,128)(2,1)S(1)}, bf16[16,64,128]{2,1,0:T(8,128)(2,1)S(1)}, u32[]{:S(2)}, u32[]{:S(2)}) collective-permute-start(bf16[16,64,128]{2,1,0:T(8,128)(2,1)S(1)} %shuffle.11.refs_1_), channel_id=1, source_target_pairs={{0,8},{8,0},{16,24},{24,16},{1,9},{9,1},{17,25},{25,17},{2,10},{10... | collective-permute-start | bytes 786440 | tf_op jit(solution)/shard_map/ppermute | solution.py:303
  94.8 14.4 %collective-permute-start.28 = (bf16[16,64,128]{2,1,0:T(8,128)(2,1)S(1)}, bf16[16,64,128]{2,1,0:T(8,128)(2,1)S(1)}, u32[]{:S(2)}, u32[]{:S(2)}) collective-permute-start(bf16[16,64,128]{2,1,0:T(8,128)(2,1)S(1)} %shuffle.8.refs_0_), channel_id=1, source_target_pairs={{0,8},{8,0},{16,24},{24,16},{1,9},{9,1},{17,25},{25,17},{2,10},{10... | collective-permute-start | bytes 786440 | tf_op jit(solution)/shard_map/ppermute | solution.py:303
  96.8 12.4 %collective-permute-start.31 = (bf16[16,64,128]{2,1,0:T(8,128)(2,1)S(1)}, bf16[16,64,128]{2,1,0:T(8,128)(2,1)S(1)}, u32[]{:S(2)}, u32[]{:S(2)}) collective-permute-start(bf16[16,64,128]{2,1,0:T(8,128)(2,1)S(1)} %shuffle.11.refs_1_), channel_id=1, source_target_pairs={{0,16},{8,24},{16,0},{24,8},{1,17},{9,25},{17,1},{25,9},{2,18},{10... | collective-permute-start | bytes 786440 | tf_op jit(solution)/shard_map/ppermute | solution.py:303
  99.2 15.6 %collective-permute-start.32 = (bf16[16,64,128]{2,1,0:T(8,128)(2,1)S(1)}, bf16[16,64,128]{2,1,0:T(8,128)(2,1)S(1)}, u32[]{:S(2)}, u32[]{:S(2)}) collective-permute-start(bf16[16,64,128]{2,1,0:T(8,128)(2,1)S(1)} %collective-permute-done.30.refs_4_), channel_id=1, source_target_pairs={{0,8},{8,0},{16,24},{24,16},{1,9},{9,1},{17,25},{25,17},{2,10},{10... | collective-permute-start | bytes 786440 | tf_op jit(solution)/shard_map/ppermute | solution.py:303
  103.6 11.2 %collective-permute-start.33 = (bf16[16,64,128]{2,1,0:T(8,128)(2,1)S(1)}, bf16[16,64,128]{2,1,0:T(8,128)(2,1)S(1)}, u32[]{:S(2)}, u32[]{:S(2)}) collective-permute-start(bf16[16,64,128]{2,1,0:T(8,128)(2,1)S(1)} %collective-permute-done.29.refs_3_), channel_id=1, source_target_pairs={{0,16},{8,24},{16,0},{24,8},{1,17},{9,25},{17,1},{25,9},{2,18},{10... | collective-permute-start | bytes 786440 | tf_op jit(solution)/shard_map/ppermute | solution.py:303
  123.8 2.8 %collective-permute-start.39 = (s16[4,2,528,128]{3,2,1,0:T(8,128)(2,1)S(1)}, s16[4,2,528,128]{3,2,1,0:T(8,128)(2,1)S(1)}, u32[]{:S(2)}, u32[]{:S(2)}) collective-permute-start(s16[4,2,528,128]{3,2,1,0:T(8,128)(2,1)S(1)} %get-tuple-element.66), channel_id=1, source_target_pairs={{0,1},{1,0},{2,3},{3,2},{4,5},{5,4},{6,7},{7,6},{8,9},{9,8},{10,11... | collective-permute-start | bytes 3244040 | tf_op jit(solution)/shard_map/ppermute | solution.py:282
  123.8 4.2 %collective-permute-start.34 = (s16[4,2,528,128]{3,2,1,0:T(8,128)(2,1)S(1)}, s16[4,2,528,128]{3,2,1,0:T(8,128)(2,1)S(1)}, u32[]{:S(2)}, u32[]{:S(2)}) collective-permute-start(s16[4,2,528,128]{3,2,1,0:T(8,128)(2,1)S(1)} %get-tuple-element.65), channel_id=1, source_target_pairs={{0,1},{1,0},{2,3},{3,2},{4,5},{5,4},{6,7},{7,6},{8,9},{9,8},{10,11... | collective-permute-start | bytes 3244040 | tf_op jit(solution)/shard_map/ppermute | solution.py:282
  126.7 9.4 %collective-permute-start.40 = (s16[2,528,128]{2,1,0:T(8,128)(2,1)S(1)}, s16[2,528,128]{2,1,0:T(8,128)(2,1)S(1)}, u32[]{:S(2)}, u32[]{:S(2)}) collective-permute-start(s16[2,528,128]{2,1,0:T(8,128)(2,1)S(1)} %combine_message.21), channel_id=1, source_target_pairs={{0,2},{1,3},{2,0},{3,1},{4,6},{5,7},{6,4},{7,5},{8,10},{9,11},{10,... | collective-permute-start | bytes 811016 | tf_op jit(solution)/shard_map/ppermute | solution.py:285
  128.3 16.4 %collective-permute-start.35 = (s16[2,528,128]{2,1,0:T(8,128)(2,1)S(1)}, s16[2,528,128]{2,1,0:T(8,128)(2,1)S(1)}, u32[]{:S(2)}, u32[]{:S(2)}) collective-permute-start(s16[2,528,128]{2,1,0:T(8,128)(2,1)S(1)} %combine_message.18), channel_id=1, source_target_pairs={{0,2},{1,3},{2,0},{3,1},{4,6},{5,7},{6,4},{7,5},{8,10},{9,11},{10,... | collective-permute-start | bytes 811016 | tf_op jit(solution)/shard_map/ppermute | solution.py:285
  136.4 10.5 %collective-permute-start.41 = (s16[2,528,128]{2,1,0:T(8,128)(2,1)S(1)}, s16[2,528,128]{2,1,0:T(8,128)(2,1)S(1)}, u32[]{:S(2)}, u32[]{:S(2)}) collective-permute-start(s16[2,528,128]{2,1,0:T(8,128)(2,1)S(1)} %combine_message.22), channel_id=1, source_target_pairs={{0,2},{1,3},{6,4},{7,5},{2,6},{3,7},{4,0},{5,1},{8,10},{9,11},{14,... | collective-permute-start | bytes 811016 | tf_op jit(solution)/shard_map/ppermute | solution.py:287
  145.0 8.7 %collective-permute-start.36 = (s16[2,528,128]{2,1,0:T(8,128)(2,1)S(1)}, s16[2,528,128]{2,1,0:T(8,128)(2,1)S(1)}, u32[]{:S(2)}, u32[]{:S(2)}) collective-permute-start(s16[2,528,128]{2,1,0:T(8,128)(2,1)S(1)} %combine_message.19), channel_id=1, source_target_pairs={{0,2},{1,3},{6,4},{7,5},{2,6},{3,7},{4,0},{5,1},{8,10},{9,11},{14,... | collective-permute-start | bytes 811016 | tf_op jit(solution)/shard_map/ppermute | solution.py:287
  147.2 14.9 %collective-permute-start.43 = (s16[2,528,128]{2,1,0:T(8,128)(2,1)S(1)}, s16[2,528,128]{2,1,0:T(8,128)(2,1)S(1)}, u32[]{:S(2)}, u32[]{:S(2)}) collective-permute-start(s16[2,528,128]{2,1,0:T(8,128)(2,1)S(1)} %combine_message.23), channel_id=1, source_target_pairs={{2,4},{3,5},{4,2},{5,3},{10,12},{11,13},{12,10},{13,11},{18,20},{1... | collective-permute-start | bytes 811016 | tf_op jit(solution)/shard_map/ppermute | solution.py:290
  151.2 10.9 %collective-permute-start.42 = (s16[2,528,128]{2,1,0:T(8,128)(2,1)S(1)}, s16[2,528,128]{2,1,0:T(8,128)(2,1)S(1)}, u32[]{:S(2)}, u32[]{:S(2)}) collective-permute-start(s16[2,528,128]{2,1,0:T(8,128)(2,1)S(1)} %combine_message.23), channel_id=1, source_target_pairs={{0,2},{1,3},{6,4},{7,5},{8,10},{9,11},{14,12},{15,13},{16,18},{17,... | collective-permute-start | bytes 811016 | tf_op jit(solution)/shard_map/ppermute | solution.py:289
  154.0 12.5 %collective-permute-start.38 = (s16[2,528,128]{2,1,0:T(8,128)(2,1)S(1)}, s16[2,528,128]{2,1,0:T(8,128)(2,1)S(1)}, u32[]{:S(2)}, u32[]{:S(2)}) collective-permute-start(s16[2,528,128]{2,1,0:T(8,128)(2,1)S(1)} %combine_message.20), channel_id=1, source_target_pairs={{2,4},{3,5},{4,2},{5,3},{10,12},{11,13},{12,10},{13,11},{18,20},{1... | collective-permute-start | bytes 811016 | tf_op jit(solution)/shard_map/ppermute | solution.py:290
  158.0 8.5 %collective-permute-start.37 = (s16[2,528,128]{2,1,0:T(8,128)(2,1)S(1)}, s16[2,528,128]{2,1,0:T(8,128)(2,1)S(1)}, u32[]{:S(2)}, u32[]{:S(2)}) collective-permute-start(s16[2,528,128]{2,1,0:T(8,128)(2,1)S(1)} %combine_message.20), channel_id=1, source_target_pairs={{0,2},{1,3},{6,4},{7,5},{8,10},{9,11},{14,12},{15,13},{16,18},{17,... | collective-permute-start | bytes 811016 | tf_op jit(solution)/shard_map/ppermute | solution.py:289
  166.5 1.1 copy-start.1

commit v4 on v3

--- a/solution.py
+++ b/solution.py
@@ -116,7 +116,7 @@
     )(counts, *operands)
 
 
-def product_kernel(place, shard, rows, cols, count, panel_in, acc_in, held, *refs):
+def product_kernel(place, halves, shard, rows, cols, count, panel_in, acc_in, held, *refs):
     total = len(refs) - 5
     pieces = refs[:total]
     panel, acc, msg_low, msg_high, sem = refs[total:]
@@ -142,7 +142,7 @@
         nil = jnp.zeros(panel.shape[1:], panel.dtype)
 
         def entry(u):
-            return panel[place(cols[0, base + u], row_owner, col_owner // 2)]
+            return panel[place(cols[0, base + u], row_owner)]
 
         products = []
         for u in range(0, STEP, 2):
@@ -165,16 +165,17 @@
         @pl.loop(0, chips * groups)
         def _(i):
             d, g = i // groups, i % groups
-            base = (2 * d + other) * shard + (half * groups + g) * GROUP
+            owner = other * chips + d if halves else 2 * d + other
+            base = owner * shard + (half * groups + g) * GROUP
             encode([acc[base + t] for t in range(GROUP)], msg.at[d, g])
 
 
-def block_product(late, place, panel, acc, held, block_rows, block_cols, counts, shard, col_total):
+def block_product(late, place, halves, panel, acc, held, block_rows, block_cols, counts, shard, col_total):
     _, k, order = panel.shape
     scalars = pl.BlockSpec(memory_space=pltpu.SMEM)
     message = pltpu.VMEM((col_total // 2, shard // GROUP // 2, message_rows(k), order), jnp.int16)
     return pl.pallas_call(
-        functools.partial(product_kernel, place, shard),
+        functools.partial(product_kernel, place, halves, shard),
         out_shape=(pltpu.VMEM(panel.shape, panel.dtype), pltpu.VMEM(acc.shape, acc.dtype), message, message),
         in_specs=[scalars] * 3 + [NEAR] * (3 + len(late)),
         out_specs=(NEAR,) * 4,
@@ -196,10 +197,8 @@
     base = (2 * d + col_owner % 2) * shard + half * groups * GROUP
     if form == "rows":
         result, out, out_sem = refs[-3:]
-    elif form == "message":
+    else:
         result = refs[-1]
-    results = refs[len(gates) :]
-    step = results[0].shape[0]
 
     def out_copy(g):
         width = GROUP * order
@@ -219,8 +218,7 @@
             if form == "message":
                 sums.append(tile)
             elif form == "tiles":
-                at = g * GROUP + i
-                results[at // step][at % step] = tile.astype(results[0].dtype)
+                result[g * GROUP + i] = tile.astype(result.dtype)
             else:
                 out[g, :, i * order : (i + 1) * order] = tile
         if form == "message":
@@ -241,9 +239,7 @@
     if form == "message":
         out_shape = pltpu.VMEM((groups, rows, order), jnp.int16)
     elif form == "tiles":
-        parts = 4 if groups * GROUP % 4 == 0 else 1
-        out_shape = (pltpu.VMEM((groups * GROUP // parts, k, order), jnp.bfloat16),) * parts
-        out_spec = (NEAR,) * parts
+        out_shape = pltpu.VMEM((groups * GROUP, k, order), jnp.bfloat16)
     else:
         shard = acc.shape[0] // (2 * chips)
         out_shape = jax.ShapeDtypeStruct((k, shard * order), jnp.float32)
@@ -277,26 +273,111 @@
     return (chip == 1) | (chip == 2)
 
 
+END_MOVES = [(0, 1), (3, 2)]
+MOVES_A = [(0, 1), (1, 0), (2, 3), (3, 2)]
+MOVES_B = END_MOVES + [(1, 3), (2, 0)]
+MOVES_D = [(1, 2), (2, 1)]
+ARRIVED_GATES = (is_end, is_end, None, None)
+
+
+def move(x, moves):
+    return lax.ppermute(x, "col", chip_moves(moves))
+
+
+def walk_line(summed, form):
+    got_a = move(summed(lambda z: 3 - 3 * (z % 2), (), (), "message"), MOVES_A)
+    got_b = move(summed(lambda z: z ^ 2, (got_a,), (is_inner,), "message"), MOVES_B)
+    send = summed(lambda z: 1 + z % 2, (got_b,), (is_inner,), "message")
+    return summed(lambda z: z, (got_a, got_b, move(send, END_MOVES), move(send, MOVES_D)), ARRIVED_GATES, form)
+
+
+def swap_cores(msg):
+    return lax.ppermute(msg, "col", [(c, c ^ 1) for c in range(2 * msg.shape[0])])
+
+
 def line_sum(half, acc, msg, form, into=None):
     chips = msg.shape[0]
-    sib = lax.ppermute(msg, "col", [(c, c ^ 1) for c in range(2 * chips)])
+    sib = swap_cores(msg)
+
+    def summed(which, arrived, gates, form):
+        return combine(half, which, acc, sib, arrived, gates, form, into if form == "rows" else None)
+
     if chips == 4:
-        send = combine(half, lambda z: 3 - 3 * (z % 2), acc, sib, (), (), "message")
-        got_a = lax.ppermute(send, "col", chip_moves([(0, 1), (1, 0), (2, 3), (3, 2)]))
-        send = combine(half, lambda z: z ^ 2, acc, sib, (got_a,), (is_inner,), "message")
-        got_b = lax.ppermute(send, "col", chip_moves([(0, 1), (3, 2), (1, 3), (2, 0)]))
-        send = combine(half, lambda z: 1 + z % 2, acc, sib, (got_b,), (is_inner,), "message")
-        got_c = lax.ppermute(send, "col", chip_moves([(0, 1), (3, 2)]))
-        got_d = lax.ppermute(send, "col", chip_moves([(1, 2), (2, 1)]))
-        arrived, gates = (got_a, got_b, got_c, got_d), (is_end, is_end, None, None)
-    else:
-        arrived = ()
-        for step in range(1, chips):
-            send = combine(half, lambda z: (z + step) % chips, acc, sib, (), (), "message")
-            moves = chip_moves([(a, (a + step) % chips) for a in range(chips)])
-            arrived += (lax.ppermute(send, "col", moves),)
-        gates = (None,) * len(arrived)
-    return combine(half, lambda z: z, acc, sib, arrived, gates, form, into)
+        return walk_line(summed, form)
+    arrived = ()
+    for step in range(1, chips):
+        send = summed(lambda z: (z + step) % chips, (), (), "message")
+        arrived += (move(send, [(a, (a + step) % chips) for a in range(chips)]),)
+    return summed(lambda z: z, arrived, (None,) * len(arrived), form)
+
+
+def spread_kernel(half, acc, sib, *results):
+    groups = sib.shape[1]
+    k = acc.shape[1]
+    shard = acc.shape[0] // 8
+    row_owner, core = lax.axis_index("row"), lax.axis_index("col") % 2
+    for flip, result in enumerate(results):
+        part = row_owner ^ flip
+
+        @pl.loop(0, groups)
+        def _(g):
+            base = (core * 4 + part) * shard + (half * groups + g) * GROUP
+            other = decoder(sib.at[part, g], k)
+            encode([acc[base + i] + other(i) for i in range(GROUP)], result.at[g])
+
+
+def relay_kernel(which, gates, form, *refs):
+    parts, arrived, result = refs[:4], refs[4:-1], refs[-1]
+    groups, rows, _ = parts[0].shape
+    k = (rows - 16) // GROUP
+    chip = lax.axis_index("col") // 2
+    wanted = lax.axis_index("row") ^ which(chip)
+    for flip, part in enumerate(parts):
+
+        @pl.when(wanted == flip)
+        def _():
+            if form == "message" and not arrived:
+                result[...] = part[...]
+                return
+
+            @pl.loop(0, groups)
+            def _(g):
+                terms = [decoder(part.at[g], k)]
+                for ref, gate in zip(arrived, gates):
+                    factor = None if gate is None else jnp.where(gate(chip), 1.0, 0.0)
+                    terms.append(decoder(ref.at[g], k, factor))
+                sums = [functools.reduce(jnp.add, [term(i) for term in terms]) for i in range(GROUP)]
+                if form == "message":
+                    encode(sums, result.at[g])
+                else:
+                    for i in range(GROUP):
+                        result[g * GROUP + i] = sums[i].astype(result.dtype)
+
+
+def small_call(kernel, name, out_shape, operands):
+    many = isinstance(out_shape, tuple)
+    return pl.pallas_call(
+        kernel,
+        out_shape=out_shape,
+        in_specs=[NEAR] * len(operands),
+        out_specs=(NEAR,) * len(out_shape) if many else NEAR,
+        compiler_params=pltpu.CompilerParams(vmem_limit_bytes=SMALL),
+        name=name,
+    )(*[near(x) for x in operands])
+
+
+def plane_sum(half, acc, msg):
+    _, groups, rows, order = msg.shape
+    message = pltpu.VMEM((groups, rows, order), jnp.int16)
+    tiles = pltpu.VMEM((groups * GROUP, acc.shape[1], order), jnp.bfloat16)
+    sent = small_call(functools.partial(spread_kernel, half), "spread", (message,) * 4, (acc, swap_cores(msg)))
+    parts = sent[:1] + tuple(across(sent[flip], flip) for flip in (1, 2, 3))
+
+    def summed(which, arrived, gates, form):
+        kernel = functools.partial(relay_kernel, which, gates, form)
+        return small_call(kernel, "relay_" + form, message if form == "message" else tiles, parts + arrived)
+
+    return walk_line(summed, "tiles")
 
 
 def across(x, flip):
@@ -311,87 +392,37 @@
     return low, high, x_low, x_high, y_low, y_high, across(y_low, 1), across(x_high, 2)
 
 
-def vector_panel(tiles, row_total):
-    shard = tiles.shape[0]
+def gather_panel(low, high, row_total):
+    shard = 2 * low.shape[0]
     if row_total != 4:
-        return (lax.all_gather(tiles, "row", axis=0, tiled=True),), lambda c, r, z: c
-    half = shard // 2
-    return gather_square(tiles[:half], tiles[half:]), lambda c, r, z: c ^ (r * shard)
-
-
-def shuffle_kernel(pick, merge, *refs):
-    total = len(refs) * merge // (merge + 1)
-    step = refs[0].shape[0]
-    for i in range(total):
-        wanted = pick(lax.axis_index("row"), lax.axis_index("col"), i)
-        for j in range(total):
-
-            @pl.when(wanted == j)
-            def _():
-                refs[total + i // merge][i % merge * step : (i % merge + 1) * step] = refs[j][...]
-
-
-def shuffle(parts, pick, merge=1):
-    shape = (merge * parts[0].shape[0],) + parts[0].shape[1:]
-    return pl.pallas_call(
-        functools.partial(shuffle_kernel, pick, merge),
-        out_shape=(pltpu.VMEM(shape, parts[0].dtype),) * (len(parts) // merge),
-        in_specs=[NEAR] * len(parts),
-        out_specs=(NEAR,) * (len(parts) // merge),
-        compiler_params=pltpu.CompilerParams(vmem_limit_bytes=SMALL),
-        name="shuffle",
-    )(*[near(x) for x in parts])
-
-
-def spread(quarters):
-    parts = shuffle(quarters, lambda r, c, i: (r // 2 * 2 + c % 2) ^ i)
-    got = []
-    for i in range(4):
-        moves = []
-        for r in range(4):
-            for c in range(8):
-                moves.append((r * 8 + c, ((r // 2 * 2 + c % 2) ^ i) * 8 + c // 2 * 2 + r % 2))
-        got.append(lax.ppermute(parts[i], ("row", "col"), moves))
-    pairs = shuffle(tuple(got), lambda r, c, i: r ^ (c // 2 % 2 * 2 ^ i), merge=2)
-    got = []
-    for i in range(2):
-        moves = [(c, 2 * (c % 2 + 2 * (c // 2 % 2 ^ i)) + c // 4) for c in range(8)]
-        got.append(lax.ppermute(pairs[i], "col", moves))
-    return shuffle(tuple(got), lambda r, c, i: c // 4 ^ i, merge=2)[0]
-
-
-def first_panel(low, high, row_total, col_total):
-    if (row_total, col_total) != (4, 8):
-        moves = []
-        for s in range(row_total * col_total):
-            moves.append((s, (s % row_total) * col_total + s // row_total))
-        tiles = lax.ppermute(jnp.concatenate(low + high, axis=0), ("row", "col"), moves)
-        return vector_panel(tiles, row_total)
-    quarter = low[0].shape[0]
-
-    def place(c, r, z):
-        block, tile = lax.div(c, quarter), lax.rem(c, quarter)
-        part, which, owner = block >> 3, (block >> 2) & 1, block & 3
-        return ((((owner ^ r) * 2 + which) * 4) + part) * quarter + tile
-
-    return gather_square(spread(low), spread(high)), place
+        tiles = jnp.concatenate([low, high], axis=0)
+        return (lax.all_gather(tiles, "row", axis=0, tiled=True),), lambda c, r: c
+    return gather_square(low, high), lambda c, r: c ^ (r * shard)
 
 
 def shards(row_total, col_total, vectors, blocks, block_rows, block_cols, counts):
     k, width = vectors.shape
     order = blocks.shape[2]
     shard = width // order
+    square = (row_total, col_total) == (4, 8)
     sizes = (row_total * shard, col_total * shard + 1, k, order)
     index = (block_rows, block_cols, counts, shard, col_total)
     tiles = vectors.reshape(k, shard, order).transpose(1, 0, 2)
-    pieces, place = vector_panel(tiles, row_total)
+    pieces, place = gather_panel(tiles[: shard // 2], tiles[shard // 2 :], row_total)
     early = len(pieces) * 3 // 4
     panel, acc, held = prepare(pieces[:early], *sizes, counts, blocks[0])
-    acc, low, high = block_product(pieces[early:], place, panel, acc, held, *index)
-    firsts = line_sum(0, acc, low, "tiles"), line_sum(1, acc, high, "tiles")
-    pieces, place = first_panel(*firsts, row_total, col_total)
+    acc, low, high = block_product(pieces[early:], place, square, panel, acc, held, *index)
+    if square:
+        low, high = plane_sum(0, acc, low), plane_sum(1, acc, high)
+    else:
+        moves = []
+        for s in range(row_total * col_total):
+            moves.append((s, (s % row_total) * col_total + s // row_total))
+        low, high = line_sum(0, acc, low, "tiles"), line_sum(1, acc, high, "tiles")
+        low, high = (lax.ppermute(x, ("row", "col"), moves) for x in (low, high))
+    pieces, place = gather_panel(low, high, row_total)
     panel, acc = prepare(pieces[:early], *sizes, counts)
-    acc, low, high = block_product(pieces[early:], place, panel, acc, held, *index)
+    acc, low, high = block_product(pieces[early:], place, False, panel, acc, held, *index)
     return line_sum(1, acc, high, "rows", line_sum(0, acc, low, "rows"))
 
 

time: 169 us -> 165 us (0.976)
  the two profiles are of different devices: /device:TPU:12 before, /device:TPU:0 now
where the time goes in v4:
time: 165 us; the launch traced here: 166 us
  starting transfers between devices  77.8 us (47%)
  waiting for transfers between devices  66.3 us (40%)
  Pallas kernels  19.2 us (12%)
    ppermute x16, starting transfers between devices, move(): return lax.ppermute(x, 'col', chip_moves(moves))  50.9 us
    ppermute x18, waiting for transfers between devices, across(): return lax.ppermute(x, 'row', [(r, r ^ flip) for r in range(4)])  33.2 us
    ppermute x16, waiting for transfers between devices, move(): return lax.ppermute(x, 'col', chip_moves(moves))  28.6 us
    ppermute x18, starting transfers between devices, across(): return lax.ppermute(x, 'row', [(r, r ^ flip) for r in range(4)])  25.8 us
    pallas_call x2, Pallas kernels, block_product(): pl.pallas_call(functools.partial(product_kernel, place, halves, shard), o...  8.04 us
    ppermute x4, waiting for transfers between devices, swap_cores(): lax.ppermute(msg, 'col', [(c, c ^ 1) for c in range(2 * msg.shape[0])])  4.4 us
    pallas_call x2, Pallas kernels, prepare(): pl.pallas_call(functools.partial(prepare_kernel, blocks is not None), out...  4.23 us
    pallas_call x8, Pallas kernels, combine(): pl.pallas_call(functools.partial(combine_kernel, half, which, gates, form...  3.58 us
  transfers between devices with their start and end apart: 38, of which 20 were waited for; matrix products, arithmetic and copies ran while one was open for 0% of the time, Pallas kernels for 6%

profile of v4, /device:TPU:0, one launch (start us, length us, event | category | flops | bytes accessed | tf_op | source)
XLA Modules:
  0.0 165.5 jit_solution(16981617041004415201)
XLA Ops:
  1.2 3.0 %collective-permute-start.1 = (bf16[16,64,128]{2,1,0:T(8,128)(2,1)S(1)}, bf16[16,64,128]{2,1,0:T(8,128)(2,1)S(1)}, u32[]{:S(2)}, u32[]{:S(2)}) collective-permute-start(bf16[16,64,128]{2,1,0:T(8,128)(2,1)S(1)} %get-tuple-element.43.refs_1_), channel_id=1, source_target_pairs={{0,8},{8,0},{16,24},{24,16},{1,9},{9,1},{17,25},{25,17},{2,10},{10... | collective-permute-start | bytes 786440 | tf_op jit(solution)/shard_map/ppermute | solution.py:384
  4.3 1.5 collective-permute-start.2
  6.4 5.0 %collective-permute-done.1.refs_3_ = bf16[16,64,128]{2,1,0:T(8,128)(2,1)S(1)} collective-permute-done((bf16[16,64,128]{2,1,0:T(8,128)(2,1)S(1)}, bf16[16,64,128]{2,1,0:T(8,128)(2,1)S(1)}, u32[]{:S(2)}, u32[]{:S(2)}) %collective-permute-start.1) | collective-permute-done | bytes 262176 | tf_op jit(solution)/shard_map/ppermute | solution.py:384
  11.4 2.0 %collective-permute-start.5 = (bf16[16,64,128]{2,1,0:T(8,128)(2,1)S(1)}, bf16[16,64,128]{2,1,0:T(8,128)(2,1)S(1)}, u32[]{:S(2)}, u32[]{:S(2)}) collective-permute-start(bf16[16,64,128]{2,1,0:T(8,128)(2,1)S(1)} %collective-permute-done.1.refs_3_), channel_id=1, source_target_pairs={{0,16},{8,24},{16,0},{24,8},{1,17},{9,25},{17,1},{25,9},{2,18},{10... | collective-permute-start | bytes 786440 | tf_op jit(solution)/shard_map/ppermute | solution.py:384
  13.5 1.5 collective-permute-start.4
  15.6 3.4 %collective-permute-done.3.refs_5_ = bf16[16,64,128]{2,1,0:T(8,128)(2,1)S(1)} collective-permute-done((bf16[16,64,128]{2,1,0:T(8,128)(2,1)S(1)}, bf16[16,64,128]{2,1,0:T(8,128)(2,1)S(1)}, u32[]{:S(2)}, u32[]{:S(2)}) %collective-permute-start.3) | collective-permute-done | bytes 262176 | tf_op jit(solution)/shard_map/ppermute | solution.py:384
  19.1 2.7 %prepare.2 = (bf16[128,64,128]{2,1,0:T(8,128)(2,1)S(1)}, f32[257,64,128]{2,1,0:T(8,128)S(1)}, bf16[512,128,128]{2,1,0:T(8,128)(2,1)S(1)}) custom-call(s32[1,1]{1,0:T(1,128)S(6)} %copy.19.count, bf16[16,64,128]{2,1,0:T(8,128)(2,1)S(1)} %get-tuple-element.44.refs_0_, bf16[16,64,128]{2,1,0:T(8,128)(2,1)S(1)} %get-tuple-element.43.refs_1_, ...), custom_call_target="tpu_custom_call" | custom-call | tf_op jit(solution)/shard_map/prepare/pallas_call | solution.py:108
  21.8 1.5 collective-permute-done.5.refs_1_
  23.3 4.0 %block_product.2 = (bf16[128,64,128]{2,1,0:T(8,128)(2,1)S(1)}, f32[257,64,128]{2,1,0:T(8,128)S(1)}, s16[4,2,528,128]{3,2,1,0:T(8,128)(2,1)S(1)}, s16[4,2,528,128]{3,2,1,0:T(8,128)(2,1)S(1)}) custom-call(s32[1,512]{1,0:T(1,128)S(1)} %copy-done.2, s32[1,512]{1,0:T(1,128)S(1)} %copy-done.3, ...), custom_call_target="tpu_custom_call", output_to_operand_aliasing={{0}: (3, {}), {1}: (4, {})} | custom-call | tf_op jit(solution)/shard_map/block_product/pallas_call | solution.py:177
  27.9 2.2 %collective-permute-done.6.sib = s16[4,2,528,128]{3,2,1,0:T(8,128)(2,1)S(1)} collective-permute-done((s16[4,2,528,128]{3,2,1,0:T(8,128)(2,1)S(1)}, s16[4,2,528,128]{3,2,1,0:T(8,128)(2,1)S(1)}, u32[]{:S(2)}, u32[]{:S(2)}) %collective-permute-start.6) | collective-permute-done | bytes 1081376 | tf_op jit(solution)/shard_map/ppermute | solution.py:295
  30.9 2.9 %collective-permute-start.8 = (s16[2,528,128]{2,1,0:T(8,128)(2,1)S(1)}, s16[2,528,128]{2,1,0:T(8,128)(2,1)S(1)}, u32[]{:S(2)}, u32[]{:S(2)}) collective-permute-start(s16[2,528,128]{2,1,0:T(8,128)(2,1)S(1)} %get-tuple-element.31), channel_id=1, source_target_pairs={{0,16},{8,24},{16,0},{24,8},{1,17},{9,25},{17,1},{25,9},{2,18},{10... | collective-permute-start | bytes 811016 | tf_op jit(solution)/shard_map/ppermute | solution.py:384
  36.2 2.0 %collective-permute-start.16 = (s16[2,528,128]{2,1,0:T(8,128)(2,1)S(1)}, s16[2,528,128]{2,1,0:T(8,128)(2,1)S(1)}, u32[]{:S(2)}, u32[]{:S(2)}) collective-permute-start(s16[2,528,128]{2,1,0:T(8,128)(2,1)S(1)} %get-tuple-element.36), channel_id=1, source_target_pairs={{0,16},{8,24},{16,0},{24,8},{1,17},{9,25},{17,1},{25,9},{2,18},{10... | collective-permute-start | bytes 811016 | tf_op jit(solution)/shard_map/ppermute | solution.py:384
  38.2 2.0 %collective-permute-done.7.refs_1_ = s16[2,528,128]{2,1,0:T(8,128)(2,1)S(1)} collective-permute-done((s16[2,528,128]{2,1,0:T(8,128)(2,1)S(1)}, s16[2,528,128]{2,1,0:T(8,128)(2,1)S(1)}, u32[]{:S(2)}, u32[]{:S(2)}) %collective-permute-start.7) | collective-permute-done | bytes 270368 | tf_op jit(solution)/shard_map/ppermute | solution.py:384
  40.3 2.4 %collective-permute-start.17 = (s16[2,528,128]{2,1,0:T(8,128)(2,1)S(1)}, s16[2,528,128]{2,1,0:T(8,128)(2,1)S(1)}, u32[]{:S(2)}, u32[]{:S(2)}) collective-permute-start(s16[2,528,128]{2,1,0:T(8,128)(2,1)S(1)} %get-tuple-element.37), channel_id=1, source_target_pairs={{0,24},{8,16},{16,8},{24,0},{1,25},{9,17},{17,9},{25,1},{2,26},{10... | collective-permute-start | bytes 811016 | tf_op jit(solution)/shard_map/ppermute | solution.py:384
  42.7 4.3 %collective-permute-done.8.refs_2_ = s16[2,528,128]{2,1,0:T(8,128)(2,1)S(1)} collective-permute-done((s16[2,528,128]{2,1,0:T(8,128)(2,1)S(1)}, s16[2,528,128]{2,1,0:T(8,128)(2,1)S(1)}, u32[]{:S(2)}, u32[]{:S(2)}) %collective-permute-start.8) | collective-permute-done | bytes 270368 | tf_op jit(solution)/shard_map/ppermute | solution.py:384
  47.0 1.7 %collective-permute-start.10 = (s16[2,528,128]{2,1,0:T(8,128)(2,1)S(1)}, s16[2,528,128]{2,1,0:T(8,128)(2,1)S(1)}, u32[]{:S(2)}, u32[]{:S(2)}) collective-permute-start(s16[2,528,128]{2,1,0:T(8,128)(2,1)S(1)} %relay_message.6), channel_id=1, source_target_pairs={{0,2},{1,3},{2,0},{3,1},{4,6},{5,7},{6,4},{7,5},{8,10},{9,11},{10,... | collective-permute-start | bytes 811016 | tf_op jit(solution)/shard_map/ppermute | solution.py:284
  48.7 3.2 %collective-permute-done.15.refs_1_ = s16[2,528,128]{2,1,0:T(8,128)(2,1)S(1)} collective-permute-done((s16[2,528,128]{2,1,0:T(8,128)(2,1)S(1)}, s16[2,528,128]{2,1,0:T(8,128)(2,1)S(1)}, u32[]{:S(2)}, u32[]{:S(2)}) %collective-permute-start.15) | collective-permute-done | bytes 270368 | tf_op jit(solution)/shard_map/ppermute | solution.py:384
  51.9 5.9 %collective-permute-done.16.refs_2_ = s16[2,528,128]{2,1,0:T(8,128)(2,1)S(1)} collective-permute-done((s16[2,528,128]{2,1,0:T(8,128)(2,1)S(1)}, s16[2,528,128]{2,1,0:T(8,128)(2,1)S(1)}, u32[]{:S(2)}, u32[]{:S(2)}) %collective-permute-start.16) | collective-permute-done | bytes 270368 | tf_op jit(solution)/shard_map/ppermute | solution.py:384
  57.8 1.7 %collective-permute-start.18 = (s16[2,528,128]{2,1,0:T(8,128)(2,1)S(1)}, s16[2,528,128]{2,1,0:T(8,128)(2,1)S(1)}, u32[]{:S(2)}, u32[]{:S(2)}) collective-permute-start(s16[2,528,128]{2,1,0:T(8,128)(2,1)S(1)} %relay_message.9), channel_id=1, source_target_pairs={{0,2},{1,3},{2,0},{3,1},{4,6},{5,7},{6,4},{7,5},{8,10},{9,11},{10,... | collective-permute-start | bytes 811016 | tf_op jit(solution)/shard_map/ppermute | solution.py:284
  60.2 6.2 %collective-permute-done.18.refs_4_ = s16[2,528,128]{2,1,0:T(8,128)(2,1)S(1)} collective-permute-done((s16[2,528,128]{2,1,0:T(8,128)(2,1)S(1)}, s16[2,528,128]{2,1,0:T(8,128)(2,1)S(1)}, u32[]{:S(2)}, u32[]{:S(2)}) %collective-permute-start.18) | collective-permute-done | bytes 270368 | tf_op jit(solution)/shard_map/ppermute | solution.py:284
  66.6 2.5 %collective-permute-start.19 = (s16[2,528,128]{2,1,0:T(8,128)(2,1)S(1)}, s16[2,528,128]{2,1,0:T(8,128)(2,1)S(1)}, u32[]{:S(2)}, u32[]{:S(2)}) collective-permute-start(s16[2,528,128]{2,1,0:T(8,128)(2,1)S(1)} %relay_message.10), channel_id=1, source_target_pairs={{0,2},{1,3},{6,4},{7,5},{2,6},{3,7},{4,0},{5,1},{8,10},{9,11},{14,... | collective-permute-start | bytes 811016 | tf_op jit(solution)/shard_map/ppermute | solution.py:284
  69.2 3.5 %collective-permute-done.11.refs_4_.refs_5_ = s16[2,528,128]{2,1,0:T(8,128)(2,1)S(1)} collective-permute-done((s16[2,528,128]{2,1,0:T(8,128)(2,1)S(1)}, s16[2,528,128]{2,1,0:T(8,128)(2,1)S(1)}, u32[]{:S(2)}, u32[]{:S(2)}) %collective-permute-start.11) | collective-permute-done | bytes 270368 | tf_op jit(solution)/shard_map/ppermute | solution.py:284
  73.6 10.9 %collective-permute-start.12 = (s16[2,528,128]{2,1,0:T(8,128)(2,1)S(1)}, s16[2,528,128]{2,1,0:T(8,128)(2,1)S(1)}, u32[]{:S(2)}, u32[]{:S(2)}) collective-permute-start(s16[2,528,128]{2,1,0:T(8,128)(2,1)S(1)} %relay_message.8), channel_id=1, source_target_pairs={{0,2},{1,3},{6,4},{7,5},{8,10},{9,11},{14,12},{15,13},{16,18},{17,... | collective-permute-start | bytes 811016 | tf_op jit(solution)/shard_map/ppermute | solution.py:284
  85.6 5.9 %collective-permute-start.20 = (s16[2,528,128]{2,1,0:T(8,128)(2,1)S(1)}, s16[2,528,128]{2,1,0:T(8,128)(2,1)S(1)}, u32[]{:S(2)}, u32[]{:S(2)}) collective-permute-start(s16[2,528,128]{2,1,0:T(8,128)(2,1)S(1)} %relay_message.11), channel_id=1, source_target_pairs={{0,2},{1,3},{6,4},{7,5},{8,10},{9,11},{14,12},{15,13},{16,18},{17,... | collective-permute-start | bytes 811016 | tf_op jit(solution)/shard_map/ppermute | solution.py:284
  91.9 1.5 collective-permute-start.24
  93.4 2.0 %collective-permute-done.20.refs_6_ = s16[2,528,128]{2,1,0:T(8,128)(2,1)S(1)} collective-permute-done((s16[2,528,128]{2,1,0:T(8,128)(2,1)S(1)}, s16[2,528,128]{2,1,0:T(8,128)(2,1)S(1)}, u32[]{:S(2)}, u32[]{:S(2)}) %collective-permute-start.20) | collective-permute-done | bytes 270368 | tf_op jit(solution)/shard_map/ppermute | solution.py:284
  95.8 1.6 collective-permute-start.23
  97.9 1.4 collective-permute-start.25
  100.2 1.7 %collective-permute-start.26 = (bf16[16,64,128]{2,1,0:T(8,128)(2,1)S(1)}, bf16[16,64,128]{2,1,0:T(8,128)(2,1)S(1)}, u32[]{:S(2)}, u32[]{:S(2)}) collective-permute-start(bf16[16,64,128]{2,1,0:T(8,128)(2,1)S(1)} %collective-permute-done.24.refs_4_), channel_id=1, source_target_pairs={{0,8},{8,0},{16,24},{24,16},{1,9},{9,1},{17,25},{25,17},{2,10},{10... | collective-permute-start | bytes 786440 | tf_op jit(solution)/shard_map/ppermute | solution.py:384
  101.9 3.1 %collective-permute-done.23.refs_3_ = bf16[16,64,128]{2,1,0:T(8,128)(2,1)S(1)} collective-permute-done((bf16[16,64,128]{2,1,0:T(8,128)(2,1)S(1)}, bf16[16,64,128]{2,1,0:T(8,128)(2,1)S(1)}, u32[]{:S(2)}, u32[]{:S(2)}) %collective-permute-start.23) | collective-permute-done | bytes 262176 | tf_op jit(solution)/shard_map/ppermute | solution.py:384
  105.0 1.4 collective-permute-start.27
  106.4 2.5 %collective-permute-done.22.refs_2_ = bf16[16,64,128]{2,1,0:T(8,128)(2,1)S(1)} collective-permute-done((bf16[16,64,128]{2,1,0:T(8,128)(2,1)S(1)}, bf16[16,64,128]{2,1,0:T(8,128)(2,1)S(1)}, u32[]{:S(2)}, u32[]{:S(2)}) %collective-permute-start.22) | collective-permute-done | bytes 262176 | tf_op jit(solution)/shard_map/ppermute | solution.py:384
  109.0 1.5 prepare.3
  110.5 1.3 collective-permute-done.26.refs_0_
  111.8 4.0 %block_product.3 = (bf16[128,64,128]{2,1,0:T(8,128)(2,1)S(1)}, f32[257,64,128]{2,1,0:T(8,128)S(1)}, s16[4,2,528,128]{3,2,1,0:T(8,128)(2,1)S(1)}, s16[4,2,528,128]{3,2,1,0:T(8,128)(2,1)S(1)}) custom-call(s32[1,512]{1,0:T(1,128)S(1)} %copy-done.2, s32[1,512]{1,0:T(1,128)S(1)} %copy-done.3, ...), custom_call_target="tpu_custom_call", output_to_operand_aliasing={{0}: (3, {}), {1}: (4, {})} | custom-call | tf_op jit(solution)/shard_map/block_product/pallas_call | solution.py:177
  116.4 2.2 %collective-permute-done.33.sib = s16[4,2,528,128]{3,2,1,0:T(8,128)(2,1)S(1)} collective-permute-done((s16[4,2,528,128]{3,2,1,0:T(8,128)(2,1)S(1)}, s16[4,2,528,128]{3,2,1,0:T(8,128)(2,1)S(1)}, u32[]{:S(2)}, u32[]{:S(2)}) %collective-permute-start.33) | collective-permute-done | bytes 1081376 | tf_op jit(solution)/shard_map/ppermute | solution.py:295
  118.8 3.6 %collective-permute-start.34 = (s16[2,528,128]{2,1,0:T(8,128)(2,1)S(1)}, s16[2,528,128]{2,1,0:T(8,128)(2,1)S(1)}, u32[]{:S(2)}, u32[]{:S(2)}) collective-permute-start(s16[2,528,128]{2,1,0:T(8,128)(2,1)S(1)} %combine_message.9), channel_id=1, source_target_pairs={{0,2},{1,3},{2,0},{3,1},{4,6},{5,7},{6,4},{7,5},{8,10},{9,11},{10,... | collective-permute-start | bytes 811016 | tf_op jit(solution)/shard_map/ppermute | solution.py:284
  122.5 1.4 collective-permute-start.29
  123.9 5.8 %collective-permute-done.34.refs_0_ = s16[2,528,128]{2,1,0:T(8,128)(2,1)S(1)} collective-permute-done((s16[2,528,128]{2,1,0:T(8,128)(2,1)S(1)}, s16[2,528,128]{2,1,0:T(8,128)(2,1)S(1)}, u32[]{:S(2)}, u32[]{:S(2)}) %collective-permute-start.34) | collective-permute-done | bytes 270368 | tf_op jit(solution)/shard_map/ppermute | solution.py:284
  129.9 2.1 %collective-permute-start.35 = (s16[2,528,128]{2,1,0:T(8,128)(2,1)S(1)}, s16[2,528,128]{2,1,0:T(8,128)(2,1)S(1)}, u32[]{:S(2)}, u32[]{:S(2)}) collective-permute-start(s16[2,528,128]{2,1,0:T(8,128)(2,1)S(1)} %combine_message.10), channel_id=1, source_target_pairs={{0,2},{1,3},{6,4},{7,5},{2,6},{3,7},{4,0},{5,1},{8,10},{9,11},{14,... | collective-permute-start | bytes 811016 | tf_op jit(solution)/shard_map/ppermute | solution.py:284
  132.0 3.0 %collective-permute-done.29.refs_0_ = s16[2,528,128]{2,1,0:T(8,128)(2,1)S(1)} collective-permute-done((s16[2,528,128]{2,1,0:T(8,128)(2,1)S(1)}, s16[2,528,128]{2,1,0:T(8,128)(2,1)S(1)}, u32[]{:S(2)}, u32[]{:S(2)}) %collective-permute-start.29) | collective-permute-done | bytes 270368 | tf_op jit(solution)/shard_map/ppermute | solution.py:284
  135.3 3.0 %collective-permute-start.30 = (s16[2,528,128]{2,1,0:T(8,128)(2,1)S(1)}, s16[2,528,128]{2,1,0:T(8,128)(2,1)S(1)}, u32[]{:S(2)}, u32[]{:S(2)}) collective-permute-start(s16[2,528,128]{2,1,0:T(8,128)(2,1)S(1)} %combine_message.7), channel_id=1, source_target_pairs={{0,2},{1,3},{6,4},{7,5},{2,6},{3,7},{4,0},{5,1},{8,10},{9,11},{14,... | collective-permute-start | bytes 811016 | tf_op jit(solution)/shard_map/ppermute | solution.py:284
  138.3 4.8 %collective-permute-done.35.refs_0_.refs_1_ = s16[2,528,128]{2,1,0:T(8,128)(2,1)S(1)} collective-permute-done((s16[2,528,128]{2,1,0:T(8,128)(2,1)S(1)}, s16[2,528,128]{2,1,0:T(8,128)(2,1)S(1)}, u32[]{:S(2)}, u32[]{:S(2)}) %collective-permute-start.35) | collective-permute-done | bytes 270368 | tf_op jit(solution)/shard_map/ppermute | solution.py:284
  144.0 9.1 %collective-permute-start.36 = (s16[2,528,128]{2,1,0:T(8,128)(2,1)S(1)}, s16[2,528,128]{2,1,0:T(8,128)(2,1)S(1)}, u32[]{:S(2)}, u32[]{:S(2)}) collective-permute-start(s16[2,528,128]{2,1,0:T(8,128)(2,1)S(1)} %combine_message.11), channel_id=1, source_target_pairs={{0,2},{1,3},{6,4},{7,5},{8,10},{9,11},{14,12},{15,13},{16,18},{17,... | collective-permute-start | bytes 811016 | tf_op jit(solution)/shard_map/ppermute | solution.py:284
  154.1 5.9 %collective-permute-start.31 = (s16[2,528,128]{2,1,0:T(8,128)(2,1)S(1)}, s16[2,528,128]{2,1,0:T(8,128)(2,1)S(1)}, u32[]{:S(2)}, u32[]{:S(2)}) collective-permute-start(s16[2,528,128]{2,1,0:T(8,128)(2,1)S(1)} %combine_message.8), channel_id=1, source_target_pairs={{0,2},{1,3},{6,4},{7,5},{8,10},{9,11},{14,12},{15,13},{16,18},{17,... | collective-permute-start | bytes 811016 | tf_op jit(solution)/shard_map/ppermute | solution.py:284
  160.0 1.1 combine_rows.2.refs_4_
  161.1 3.3 %collective-permute-done.31.refs_2_ = s16[2,528,128]{2,1,0:T(8,128)(2,1)S(1)} collective-permute-done((s16[2,528,128]{2,1,0:T(8,128)(2,1)S(1)}, s16[2,528,128]{2,1,0:T(8,128)(2,1)S(1)}, u32[]{:S(2)}, u32[]{:S(2)}) %collective-permute-start.31) | collective-permute-done | bytes 270368 | tf_op jit(solution)/shard_map/ppermute | solution.py:284
  164.4 1.1 combine_rows.3
  (60 shorter events, 14.0 us)
Async XLA Ops:
  0.0 1.0 copy-start
  1.2 10.2 %collective-permute-start.1 = (bf16[16,64,128]{2,1,0:T(8,128)(2,1)S(1)}, bf16[16,64,128]{2,1,0:T(8,128)(2,1)S(1)}, u32[]{:S(2)}, u32[]{:S(2)}) collective-permute-start(bf16[16,64,128]{2,1,0:T(8,128)(2,1)S(1)} %get-tuple-element.43.refs_1_), channel_id=1, source_target_pairs={{0,8},{8,0},{16,24},{24,16},{1,9},{9,1},{17,25},{25,17},{2,10},{10... | collective-permute-start | bytes 786440 | tf_op jit(solution)/shard_map/ppermute | solution.py:384
  4.3 9.2 %collective-permute-start.2 = (bf16[16,64,128]{2,1,0:T(8,128)(2,1)S(1)}, bf16[16,64,128]{2,1,0:T(8,128)(2,1)S(1)}, u32[]{:S(2)}, u32[]{:S(2)}) collective-permute-start(bf16[16,64,128]{2,1,0:T(8,128)(2,1)S(1)} %get-tuple-element.44.refs_0_), channel_id=1, source_target_pairs={{0,16},{8,24},{16,0},{24,8},{1,17},{9,25},{17,1},{25,9},{2,18},{10... | collective-permute-start | bytes 786440 | tf_op jit(solution)/shard_map/ppermute | solution.py:384
  5.8 13.3 %collective-permute-start.3 = (bf16[16,64,128]{2,1,0:T(8,128)(2,1)S(1)}, bf16[16,64,128]{2,1,0:T(8,128)(2,1)S(1)}, u32[]{:S(2)}, u32[]{:S(2)}) collective-permute-start(bf16[16,64,128]{2,1,0:T(8,128)(2,1)S(1)} %get-tuple-element.43.refs_1_), channel_id=1, source_target_pairs={{0,16},{8,24},{16,0},{24,8},{1,17},{9,25},{17,1},{25,9},{2,18},{10... | collective-permute-start | bytes 786440 | tf_op jit(solution)/shard_map/ppermute | solution.py:384
  6.3 12.8 %collective-permute-start = (bf16[16,64,128]{2,1,0:T(8,128)(2,1)S(1)}, bf16[16,64,128]{2,1,0:T(8,128)(2,1)S(1)}, u32[]{:S(2)}, u32[]{:S(2)}) collective-permute-start(bf16[16,64,128]{2,1,0:T(8,128)(2,1)S(1)} %get-tuple-element.44.refs_0_), channel_id=1, source_target_pairs={{0,8},{8,0},{16,24},{24,16},{1,9},{9,1},{17,25},{25,17},{2,10},{10... | collective-permute-start | bytes 786440 | tf_op jit(solution)/shard_map/ppermute | solution.py:384
  11.4 11.8 %collective-permute-start.5 = (bf16[16,64,128]{2,1,0:T(8,128)(2,1)S(1)}, bf16[16,64,128]{2,1,0:T(8,128)(2,1)S(1)}, u32[]{:S(2)}, u32[]{:S(2)}) collective-permute-start(bf16[16,64,128]{2,1,0:T(8,128)(2,1)S(1)} %collective-permute-done.1.refs_3_), channel_id=1, source_target_pairs={{0,16},{8,24},{16,0},{24,8},{1,17},{9,25},{17,1},{25,9},{2,18},{10... | collective-permute-start | bytes 786440 | tf_op jit(solution)/shard_map/ppermute | solution.py:384
  13.5 9.8 %collective-permute-start.4 = (bf16[16,64,128]{2,1,0:T(8,128)(2,1)S(1)}, bf16[16,64,128]{2,1,0:T(8,128)(2,1)S(1)}, u32[]{:S(2)}, u32[]{:S(2)}) collective-permute-start(bf16[16,64,128]{2,1,0:T(8,128)(2,1)S(1)} %collective-permute-done.2.refs_4_), channel_id=1, source_target_pairs={{0,8},{8,0},{16,24},{24,16},{1,9},{9,1},{17,25},{25,17},{2,10},{10... | collective-permute-start | bytes 786440 | tf_op jit(solution)/shard_map/ppermute | solution.py:384
  19.1 4.2 %copy-start.2 = (s32[1,512]{1,0:T(1,128)S(1)}, s32[1,512]{1,0:T(1,128)}, u32[]{:S(2)}) copy-start(s32[1,512]{1,0:T(1,128)} %rows.3) | copy-start | bytes 6148
  19.1 4.2 %copy-start.3 = (s32[1,512]{1,0:T(1,128)S(1)}, s32[1,512]{1,0:T(1,128)}, u32[]{:S(2)}) copy-start(s32[1,512]{1,0:T(1,128)} %cols.3) | copy-start | bytes 6148
  27.3 2.8 %collective-permute-start.6 = (s16[4,2,528,128]{3,2,1,0:T(8,128)(2,1)S(1)}, s16[4,2,528,128]{3,2,1,0:T(8,128)(2,1)S(1)}, u32[]{:S(2)}, u32[]{:S(2)}) collective-permute-start(s16[4,2,528,128]{3,2,1,0:T(8,128)(2,1)S(1)} %get-tuple-element.28), channel_id=1, source_target_pairs={{0,1},{1,0},{2,3},{3,2},{4,5},{5,4},{6,7},{7,6},{8,9},{9,8},{10,11... | collective-permute-start | bytes 3244040 | tf_op jit(solution)/shard_map/ppermute | solution.py:295
  27.4 7.0 %collective-permute-start.14 = (s16[4,2,528,128]{3,2,1,0:T(8,128)(2,1)S(1)}, s16[4,2,528,128]{3,2,1,0:T(8,128)(2,1)S(1)}, u32[]{:S(2)}, u32[]{:S(2)}) collective-permute-start(s16[4,2,528,128]{3,2,1,0:T(8,128)(2,1)S(1)} %get-tuple-element.33), channel_id=1, source_target_pairs={{0,1},{1,0},{2,3},{3,2},{4,5},{5,4},{6,7},{7,6},{8,9},{9,8},{10,11... | collective-permute-start | bytes 3244040 | tf_op jit(solution)/shard_map/ppermute | solution.py:295
  30.9 9.4 %collective-permute-start.7 = (s16[2,528,128]{2,1,0:T(8,128)(2,1)S(1)}, s16[2,528,128]{2,1,0:T(8,128)(2,1)S(1)}, u32[]{:S(2)}, u32[]{:S(2)}) collective-permute-start(s16[2,528,128]{2,1,0:T(8,128)(2,1)S(1)} %get-tuple-element.30), channel_id=1, source_target_pairs={{0,8},{8,0},{16,24},{24,16},{1,9},{9,1},{17,25},{25,17},{2,10},{10... | collective-permute-start | bytes 811016 | tf_op jit(solution)/shard_map/ppermute | solution.py:384
  30.9 16.1 %collective-permute-start.8 = (s16[2,528,128]{2,1,0:T(8,128)(2,1)S(1)}, s16[2,528,128]{2,1,0:T(8,128)(2,1)S(1)}, u32[]{:S(2)}, u32[]{:S(2)}) collective-permute-start(s16[2,528,128]{2,1,0:T(8,128)(2,1)S(1)} %get-tuple-element.31), channel_id=1, source_target_pairs={{0,16},{8,24},{16,0},{24,8},{1,17},{9,25},{17,1},{25,9},{2,18},{10... | collective-permute-start | bytes 811016 | tf_op jit(solution)/shard_map/ppermute | solution.py:384
  33.9 13.1 %collective-permute-start.9 = (s16[2,528,128]{2,1,0:T(8,128)(2,1)S(1)}, s16[2,528,128]{2,1,0:T(8,128)(2,1)S(1)}, u32[]{:S(2)}, u32[]{:S(2)}) collective-permute-start(s16[2,528,128]{2,1,0:T(8,128)(2,1)S(1)} %get-tuple-element.32), channel_id=1, source_target_pairs={{0,24},{8,16},{16,8},{24,0},{1,25},{9,17},{17,9},{25,1},{2,26},{10... | collective-permute-start | bytes 811016 | tf_op jit(solution)/shard_map/ppermute | solution.py:384
  35.2 16.7 %collective-permute-start.15 = (s16[2,528,128]{2,1,0:T(8,128)(2,1)S(1)}, s16[2,528,128]{2,1,0:T(8,128)(2,1)S(1)}, u32[]{:S(2)}, u32[]{:S(2)}) collective-permute-start(s16[2,528,128]{2,1,0:T(8,128)(2,1)S(1)} %get-tuple-element.35), channel_id=1, source_target_pairs={{0,8},{8,0},{16,24},{24,16},{1,9},{9,1},{17,25},{25,17},{2,10},{10... | collective-permute-start | bytes 811016 | tf_op jit(solution)/shard_map/ppermute | solution.py:384
  36.2 21.6 %collective-permute-start.16 = (s16[2,528,128]{2,1,0:T(8,128)(2,1)S(1)}, s16[2,528,128]{2,1,0:T(8,128)(2,1)S(1)}, u32[]{:S(2)}, u32[]{:S(2)}) collective-permute-start(s16[2,528,128]{2,1,0:T(8,128)(2,1)S(1)} %get-tuple-element.36), channel_id=1, source_target_pairs={{0,16},{8,24},{16,0},{24,8},{1,17},{9,25},{17,1},{25,9},{2,18},{10... | collective-permute-start | bytes 811016 | tf_op jit(solution)/shard_map/ppermute | solution.py:384
  40.3 17.5 %collective-permute-start.17 = (s16[2,528,128]{2,1,0:T(8,128)(2,1)S(1)}, s16[2,528,128]{2,1,0:T(8,128)(2,1)S(1)}, u32[]{:S(2)}, u32[]{:S(2)}) collective-permute-start(s16[2,528,128]{2,1,0:T(8,128)(2,1)S(1)} %get-tuple-element.37), channel_id=1, source_target_pairs={{0,24},{8,16},{16,8},{24,0},{1,25},{9,17},{17,9},{25,1},{2,26},{10... | collective-permute-start | bytes 811016 | tf_op jit(solution)/shard_map/ppermute | solution.py:384
  47.0 12.5 %collective-permute-start.10 = (s16[2,528,128]{2,1,0:T(8,128)(2,1)S(1)}, s16[2,528,128]{2,1,0:T(8,128)(2,1)S(1)}, u32[]{:S(2)}, u32[]{:S(2)}) collective-permute-start(s16[2,528,128]{2,1,0:T(8,128)(2,1)S(1)} %relay_message.6), channel_id=1, source_target_pairs={{0,2},{1,3},{2,0},{3,1},{4,6},{5,7},{6,4},{7,5},{8,10},{9,11},{10,... | collective-permute-start | bytes 811016 | tf_op jit(solution)/shard_map/ppermute | solution.py:284
  57.8 8.6 %collective-permute-start.18 = (s16[2,528,128]{2,1,0:T(8,128)(2,1)S(1)}, s16[2,528,128]{2,1,0:T(8,128)(2,1)S(1)}, u32[]{:S(2)}, u32[]{:S(2)}) collective-permute-start(s16[2,528,128]{2,1,0:T(8,128)(2,1)S(1)} %relay_message.9), channel_id=1, source_target_pairs={{0,2},{1,3},{2,0},{3,1},{4,6},{5,7},{6,4},{7,5},{8,10},{9,11},{10,... | collective-permute-start | bytes 811016 | tf_op jit(solution)/shard_map/ppermute | solution.py:284
  59.8 12.9 %collective-permute-start.11 = (s16[2,528,128]{2,1,0:T(8,128)(2,1)S(1)}, s16[2,528,128]{2,1,0:T(8,128)(2,1)S(1)}, u32[]{:S(2)}, u32[]{:S(2)}) collective-permute-start(s16[2,528,128]{2,1,0:T(8,128)(2,1)S(1)} %relay_message.7), channel_id=1, source_target_pairs={{0,2},{1,3},{6,4},{7,5},{2,6},{3,7},{4,0},{5,1},{8,10},{9,11},{14,... | collective-permute-start | bytes 811016 | tf_op jit(solution)/shard_map/ppermute | solution.py:284
  66.6 17.9 %collective-permute-start.19 = (s16[2,528,128]{2,1,0:T(8,128)(2,1)S(1)}, s16[2,528,128]{2,1,0:T(8,128)(2,1)S(1)}, u32[]{:S(2)}, u32[]{:S(2)}) collective-permute-start(s16[2,528,128]{2,1,0:T(8,128)(2,1)S(1)} %relay_message.10), channel_id=1, source_target_pairs={{0,2},{1,3},{6,4},{7,5},{2,6},{3,7},{4,0},{5,1},{8,10},{9,11},{14,... | collective-permute-start | bytes 811016 | tf_op jit(solution)/shard_map/ppermute | solution.py:284
  72.9 18.5 %collective-permute-start.13 = (s16[2,528,128]{2,1,0:T(8,128)(2,1)S(1)}, s16[2,528,128]{2,1,0:T(8,128)(2,1)S(1)}, u32[]{:S(2)}, u32[]{:S(2)}) collective-permute-start(s16[2,528,128]{2,1,0:T(8,128)(2,1)S(1)} %relay_message.8), channel_id=1, source_target_pairs={{2,4},{3,5},{4,2},{5,3},{10,12},{11,13},{12,10},{13,11},{18,20},{1... | collective-permute-start | bytes 811016 | tf_op jit(solution)/shard_map/ppermute | solution.py:284
  73.6 17.8 %collective-permute-start.12 = (s16[2,528,128]{2,1,0:T(8,128)(2,1)S(1)}, s16[2,528,128]{2,1,0:T(8,128)(2,1)S(1)}, u32[]{:S(2)}, u32[]{:S(2)}) collective-permute-start(s16[2,528,128]{2,1,0:T(8,128)(2,1)S(1)} %relay_message.8), channel_id=1, source_target_pairs={{0,2},{1,3},{6,4},{7,5},{8,10},{9,11},{14,12},{15,13},{16,18},{17,... | collective-permute-start | bytes 811016 | tf_op jit(solution)/shard_map/ppermute | solution.py:284
  84.9 8.5 %collective-permute-start.21 = (s16[2,528,128]{2,1,0:T(8,128)(2,1)S(1)}, s16[2,528,128]{2,1,0:T(8,128)(2,1)S(1)}, u32[]{:S(2)}, u32[]{:S(2)}) collective-permute-start(s16[2,528,128]{2,1,0:T(8,128)(2,1)S(1)} %relay_message.11), channel_id=1, source_target_pairs={{2,4},{3,5},{4,2},{5,3},{10,12},{11,13},{12,10},{13,11},{18,20},{1... | collective-permute-start | bytes 811016 | tf_op jit(solution)/shard_map/ppermute | solution.py:284
  85.6 9.8 %collective-permute-start.20 = (s16[2,528,128]{2,1,0:T(8,128)(2,1)S(1)}, s16[2,528,128]{2,1,0:T(8,128)(2,1)S(1)}, u32[]{:S(2)}, u32[]{:S(2)}) collective-permute-start(s16[2,528,128]{2,1,0:T(8,128)(2,1)S(1)} %relay_message.11), channel_id=1, source_target_pairs={{0,2},{1,3},{6,4},{7,5},{8,10},{9,11},{14,12},{15,13},{16,18},{17,... | collective-permute-start | bytes 811016 | tf_op jit(solution)/shard_map/ppermute | solution.py:284
  91.9 8.3 %collective-permute-start.24 = (bf16[16,64,128]{2,1,0:T(8,128)(2,1)S(1)}, bf16[16,64,128]{2,1,0:T(8,128)(2,1)S(1)}, u32[]{:S(2)}, u32[]{:S(2)}) collective-permute-start(bf16[16,64,128]{2,1,0:T(8,128)(2,1)S(1)} %relay_tiles.2.refs_0_), channel_id=1, source_target_pairs={{0,16},{8,24},{16,0},{24,8},{1,17},{9,25},{17,1},{25,9},{2,18},{10... | collective-permute-start | bytes 786440 | tf_op jit(solution)/shard_map/ppermute | solution.py:384
  95.8 9.2 %collective-permute-start.23 = (bf16[16,64,128]{2,1,0:T(8,128)(2,1)S(1)}, bf16[16,64,128]{2,1,0:T(8,128)(2,1)S(1)}, u32[]{:S(2)}, u32[]{:S(2)}) collective-permute-start(bf16[16,64,128]{2,1,0:T(8,128)(2,1)S(1)} %relay_tiles.3.refs_1_), channel_id=1, source_target_pairs={{0,8},{8,0},{16,24},{24,16},{1,9},{9,1},{17,25},{25,17},{2,10},{10... | collective-permute-start | bytes 786440 | tf_op jit(solution)/shard_map/ppermute | solution.py:384
  97.3 11.6 %collective-permute-start.22 = (bf16[16,64,128]{2,1,0:T(8,128)(2,1)S(1)}, bf16[16,64,128]{2,1,0:T(8,128)(2,1)S(1)}, u32[]{:S(2)}, u32[]{:S(2)}) collective-permute-start(bf16[16,64,128]{2,1,0:T(8,128)(2,1)S(1)} %relay_tiles.2.refs_0_), channel_id=1, source_target_pairs={{0,8},{8,0},{16,24},{24,16},{1,9},{9,1},{17,25},{25,17},{2,10},{10... | collective-permute-start | bytes 786440 | tf_op jit(solution)/shard_map/ppermute | solution.py:384
  97.9 11.1 %collective-permute-start.25 = (bf16[16,64,128]{2,1,0:T(8,128)(2,1)S(1)}, bf16[16,64,128]{2,1,0:T(8,128)(2,1)S(1)}, u32[]{:S(2)}, u32[]{:S(2)}) collective-permute-start(bf16[16,64,128]{2,1,0:T(8,128)(2,1)S(1)} %relay_tiles.3.refs_1_), channel_id=1, source_target_pairs={{0,16},{8,24},{16,0},{24,8},{1,17},{9,25},{17,1},{25,9},{2,18},{10... | collective-permute-start | bytes 786440 | tf_op jit(solution)/shard_map/ppermute | solution.py:384
  100.2 11.6 %collective-permute-start.26 = (bf16[16,64,128]{2,1,0:T(8,128)(2,1)S(1)}, bf16[16,64,128]{2,1,0:T(8,128)(2,1)S(1)}, u32[]{:S(2)}, u32[]{:S(2)}) collective-permute-start(bf16[16,64,128]{2,1,0:T(8,128)(2,1)S(1)} %collective-permute-done.24.refs_4_), channel_id=1, source_target_pairs={{0,8},{8,0},{16,24},{24,16},{1,9},{9,1},{17,25},{25,17},{2,10},{10... | collective-permute-start | bytes 786440 | tf_op jit(solution)/shard_map/ppermute | solution.py:384
  105.0 6.8 %collective-permute-start.27 = (bf16[16,64,128]{2,1,0:T(8,128)(2,1)S(1)}, bf16[16,64,128]{2,1,0:T(8,128)(2,1)S(1)}, u32[]{:S(2)}, u32[]{:S(2)}) collective-permute-start(bf16[16,64,128]{2,1,0:T(8,128)(2,1)S(1)} %collective-permute-done.23.refs_3_), channel_id=1, source_target_pairs={{0,16},{8,24},{16,0},{24,8},{1,17},{9,25},{17,1},{25,9},{2,18},{10... | collective-permute-start | bytes 786440 | tf_op jit(solution)/shard_map/ppermute | solution.py:384
  115.8 2.8 %collective-permute-start.33 = (s16[4,2,528,128]{3,2,1,0:T(8,128)(2,1)S(1)}, s16[4,2,528,128]{3,2,1,0:T(8,128)(2,1)S(1)}, u32[]{:S(2)}, u32[]{:S(2)}) collective-permute-start(s16[4,2,528,128]{3,2,1,0:T(8,128)(2,1)S(1)} %get-tuple-element.42), channel_id=1, source_target_pairs={{0,1},{1,0},{2,3},{3,2},{4,5},{5,4},{6,7},{7,6},{8,9},{9,8},{10,11... | collective-permute-start | bytes 3244040 | tf_op jit(solution)/shard_map/ppermute | solution.py:295
  115.9 6.5 %collective-permute-start.28 = (s16[4,2,528,128]{3,2,1,0:T(8,128)(2,1)S(1)}, s16[4,2,528,128]{3,2,1,0:T(8,128)(2,1)S(1)}, u32[]{:S(2)}, u32[]{:S(2)}) collective-permute-start(s16[4,2,528,128]{3,2,1,0:T(8,128)(2,1)S(1)} %get-tuple-element.41), channel_id=1, source_target_pairs={{0,1},{1,0},{2,3},{3,2},{4,5},{5,4},{6,7},{7,6},{8,9},{9,8},{10,11... | collective-permute-start | bytes 3244040 | tf_op jit(solution)/shard_map/ppermute | solution.py:295
  118.8 10.9 %collective-permute-start.34 = (s16[2,528,128]{2,1,0:T(8,128)(2,1)S(1)}, s16[2,528,128]{2,1,0:T(8,128)(2,1)S(1)}, u32[]{:S(2)}, u32[]{:S(2)}) collective-permute-start(s16[2,528,128]{2,1,0:T(8,128)(2,1)S(1)} %combine_message.9), channel_id=1, source_target_pairs={{0,2},{1,3},{2,0},{3,1},{4,6},{5,7},{6,4},{7,5},{8,10},{9,11},{10,... | collective-permute-start | bytes 811016 | tf_op jit(solution)/shard_map/ppermute | solution.py:284
  122.5 12.5 %collective-permute-start.29 = (s16[2,528,128]{2,1,0:T(8,128)(2,1)S(1)}, s16[2,528,128]{2,1,0:T(8,128)(2,1)S(1)}, u32[]{:S(2)}, u32[]{:S(2)}) collective-permute-start(s16[2,528,128]{2,1,0:T(8,128)(2,1)S(1)} %combine_message.6), channel_id=1, source_target_pairs={{0,2},{1,3},{2,0},{3,1},{4,6},{5,7},{6,4},{7,5},{8,10},{9,11},{10,... | collective-permute-start | bytes 811016 | tf_op jit(solution)/shard_map/ppermute | solution.py:284
  129.9 13.1 %collective-permute-start.35 = (s16[2,528,128]{2,1,0:T(8,128)(2,1)S(1)}, s16[2,528,128]{2,1,0:T(8,128)(2,1)S(1)}, u32[]{:S(2)}, u32[]{:S(2)}) collective-permute-start(s16[2,528,128]{2,1,0:T(8,128)(2,1)S(1)} %combine_message.10), channel_id=1, source_target_pairs={{0,2},{1,3},{6,4},{7,5},{2,6},{3,7},{4,0},{5,1},{8,10},{9,11},{14,... | collective-permute-start | bytes 811016 | tf_op jit(solution)/shard_map/ppermute | solution.py:284
  135.3 17.8 %collective-permute-start.30 = (s16[2,528,128]{2,1,0:T(8,128)(2,1)S(1)}, s16[2,528,128]{2,1,0:T(8,128)(2,1)S(1)}, u32[]{:S(2)}, u32[]{:S(2)}) collective-permute-start(s16[2,528,128]{2,1,0:T(8,128)(2,1)S(1)} %combine_message.7), channel_id=1, source_target_pairs={{0,2},{1,3},{6,4},{7,5},{2,6},{3,7},{4,0},{5,1},{8,10},{9,11},{14,... | collective-permute-start | bytes 811016 | tf_op jit(solution)/shard_map/ppermute | solution.py:284
  143.3 16.7 %collective-permute-start.37 = (s16[2,528,128]{2,1,0:T(8,128)(2,1)S(1)}, s16[2,528,128]{2,1,0:T(8,128)(2,1)S(1)}, u32[]{:S(2)}, u32[]{:S(2)}) collective-permute-start(s16[2,528,128]{2,1,0:T(8,128)(2,1)S(1)} %combine_message.11), channel_id=1, source_target_pairs={{2,4},{3,5},{4,2},{5,3},{10,12},{11,13},{12,10},{13,11},{18,20},{1... | collective-permute-start | bytes 811016 | tf_op jit(solution)/shard_map/ppermute | solution.py:284
  144.0 16.0 %collective-permute-start.36 = (s16[2,528,128]{2,1,0:T(8,128)(2,1)S(1)}, s16[2,528,128]{2,1,0:T(8,128)(2,1)S(1)}, u32[]{:S(2)}, u32[]{:S(2)}) collective-permute-start(s16[2,528,128]{2,1,0:T(8,128)(2,1)S(1)} %combine_message.11), channel_id=1, source_target_pairs={{0,2},{1,3},{6,4},{7,5},{8,10},{9,11},{14,12},{15,13},{16,18},{17,... | collective-permute-start | bytes 811016 | tf_op jit(solution)/shard_map/ppermute | solution.py:284
  153.4 7.7 %collective-permute-start.32 = (s16[2,528,128]{2,1,0:T(8,128)(2,1)S(1)}, s16[2,528,128]{2,1,0:T(8,128)(2,1)S(1)}, u32[]{:S(2)}, u32[]{:S(2)}) collective-permute-start(s16[2,528,128]{2,1,0:T(8,128)(2,1)S(1)} %combine_message.8), channel_id=1, source_target_pairs={{2,4},{3,5},{4,2},{5,3},{10,12},{11,13},{12,10},{13,11},{18,20},{1... | collective-permute-start | bytes 811016 | tf_op jit(solution)/shard_map/ppermute | solution.py:284
  154.1 10.4 %collective-permute-start.31 = (s16[2,528,128]{2,1,0:T(8,128)(2,1)S(1)}, s16[2,528,128]{2,1,0:T(8,128)(2,1)S(1)}, u32[]{:S(2)}, u32[]{:S(2)}) collective-permute-start(s16[2,528,128]{2,1,0:T(8,128)(2,1)S(1)} %combine_message.8), channel_id=1, source_target_pairs={{0,2},{1,3},{6,4},{7,5},{8,10},{9,11},{14,12},{15,13},{16,18},{17,... | collective-permute-start | bytes 811016 | tf_op jit(solution)/shard_map/ppermute | solution.py:284
  164.4 1.1 copy-start.1

commit v5 on v4

--- a/solution.py
+++ b/solution.py
@@ -8,7 +8,7 @@
 from jax.sharding import PartitionSpec as P
 
 GROUP = 8
-STEP = 32
+STEP = 64
 TOP = 14.0
 SMALL = 4 * 1024 * 1024
 

time: 165 us -> 162 us (0.982); the launches traced: 166 us -> 160 us
  starting transfers between devices: 77.8 us -> 69.2 us
  waiting for transfers between devices: 66.3 us -> 69.4 us
    ppermute x16, starting transfers between devices: 50.9 us -> 40.5 us  [move(): return lax.ppermute(x, 'col', chip_moves(moves))]
    ppermute x16, waiting for transfers between devices: 28.6 us -> 33 us  [move(): return lax.ppermute(x, 'col', chip_moves(moves))]
    ppermute x18, starting transfers between devices: 25.8 us -> 27.5 us  [across(): return lax.ppermute(x, 'row', [(r, r ^ flip) for r in range(4)])]
  transfers between devices with their start and end apart: 38 -> 38, of which waited for: 20 -> 20; matrix products, arithmetic and copies ran while one was open for 0% -> 0% of each run, Pallas kernels for 6% -> 7%
where the time goes in v5:
time: 162 us; the launch traced here: 160 us
  waiting for transfers between devices  69.4 us (43%)
  starting transfers between devices  69.2 us (43%)
  Pallas kernels  19.4 us (12%)
    ppermute x16, starting transfers between devices, move(): return lax.ppermute(x, 'col', chip_moves(moves))  40.5 us
    ppermute x16, waiting for transfers between devices, move(): return lax.ppermute(x, 'col', chip_moves(moves))  33 us
    ppermute x18, waiting for transfers between devices, across(): return lax.ppermute(x, 'row', [(r, r ^ flip) for r in range(4)])  32 us
    ppermute x18, starting transfers between devices, across(): return lax.ppermute(x, 'row', [(r, r ^ flip) for r in range(4)])  27.5 us
    pallas_call x2, Pallas kernels, block_product(): pl.pallas_call(functools.partial(product_kernel, place, halves, shard), o...  7.92 us
    pallas_call x2, Pallas kernels, prepare(): pl.pallas_call(functools.partial(prepare_kernel, blocks is not None), out...  4.53 us
    ppermute x4, waiting for transfers between devices, swap_cores(): lax.ppermute(msg, 'col', [(c, c ^ 1) for c in range(2 * msg.shape[0])])  4.4 us
    pallas_call x8, Pallas kernels, combine(): pl.pallas_call(functools.partial(combine_kernel, half, which, gates, form...  3.58 us
  transfers between devices with their start and end apart: 38, of which 20 were waited for; matrix products, arithmetic and copies ran while one was open for 0% of the time, Pallas kernels for 7%

profile of v5, /device:TPU:0, one launch (start us, length us, event | category | flops | bytes accessed | tf_op | source)
XLA Modules:
  0.0 160.3 jit_solution(8899686059439407760)
XLA Ops:
  1.2 3.0 %collective-permute-start.1 = (bf16[16,64,128]{2,1,0:T(8,128)(2,1)S(1)}, bf16[16,64,128]{2,1,0:T(8,128)(2,1)S(1)}, u32[]{:S(2)}, u32[]{:S(2)}) collective-permute-start(bf16[16,64,128]{2,1,0:T(8,128)(2,1)S(1)} %get-tuple-element.43.refs_1_), channel_id=1, source_target_pairs={{0,8},{8,0},{16,24},{24,16},{1,9},{9,1},{17,25},{25,17},{2,10},{10... | collective-permute-start | bytes 786440 | tf_op jit(solution)/shard_map/ppermute | solution.py:384
  4.3 1.5 collective-permute-start.2
  6.4 5.0 %collective-permute-done.1.refs_3_ = bf16[16,64,128]{2,1,0:T(8,128)(2,1)S(1)} collective-permute-done((bf16[16,64,128]{2,1,0:T(8,128)(2,1)S(1)}, bf16[16,64,128]{2,1,0:T(8,128)(2,1)S(1)}, u32[]{:S(2)}, u32[]{:S(2)}) %collective-permute-start.1) | collective-permute-done | bytes 262176 | tf_op jit(solution)/shard_map/ppermute | solution.py:384
  11.4 2.0 %collective-permute-start.5 = (bf16[16,64,128]{2,1,0:T(8,128)(2,1)S(1)}, bf16[16,64,128]{2,1,0:T(8,128)(2,1)S(1)}, u32[]{:S(2)}, u32[]{:S(2)}) collective-permute-start(bf16[16,64,128]{2,1,0:T(8,128)(2,1)S(1)} %collective-permute-done.1.refs_3_), channel_id=1, source_target_pairs={{0,16},{8,24},{16,0},{24,8},{1,17},{9,25},{17,1},{25,9},{2,18},{10... | collective-permute-start | bytes 786440 | tf_op jit(solution)/shard_map/ppermute | solution.py:384
  13.5 1.5 collective-permute-start.4
  15.6 3.4 %collective-permute-done.3.refs_5_ = bf16[16,64,128]{2,1,0:T(8,128)(2,1)S(1)} collective-permute-done((bf16[16,64,128]{2,1,0:T(8,128)(2,1)S(1)}, bf16[16,64,128]{2,1,0:T(8,128)(2,1)S(1)}, u32[]{:S(2)}, u32[]{:S(2)}) %collective-permute-start.3) | collective-permute-done | bytes 262176 | tf_op jit(solution)/shard_map/ppermute | solution.py:384
  19.1 3.0 %prepare.2 = (bf16[128,64,128]{2,1,0:T(8,128)(2,1)S(1)}, f32[257,64,128]{2,1,0:T(8,128)S(1)}, bf16[512,128,128]{2,1,0:T(8,128)(2,1)S(1)}) custom-call(s32[1,1]{1,0:T(1,128)S(6)} %copy.19.count, bf16[16,64,128]{2,1,0:T(8,128)(2,1)S(1)} %get-tuple-element.44.refs_0_, bf16[16,64,128]{2,1,0:T(8,128)(2,1)S(1)} %get-tuple-element.43.refs_1_, ...), custom_call_target="tpu_custom_call" | custom-call | tf_op jit(solution)/shard_map/prepare/pallas_call | solution.py:108
  22.1 1.2 collective-permute-done.5.refs_1_
  23.3 4.0 %block_product.2 = (bf16[128,64,128]{2,1,0:T(8,128)(2,1)S(1)}, f32[257,64,128]{2,1,0:T(8,128)S(1)}, s16[4,2,528,128]{3,2,1,0:T(8,128)(2,1)S(1)}, s16[4,2,528,128]{3,2,1,0:T(8,128)(2,1)S(1)}) custom-call(s32[1,512]{1,0:T(1,128)S(1)} %copy-done.2, s32[1,512]{1,0:T(1,128)S(1)} %copy-done.3, ...), custom_call_target="tpu_custom_call", output_to_operand_aliasing={{0}: (3, {}), {1}: (4, {})} | custom-call | tf_op jit(solution)/shard_map/block_product/pallas_call | solution.py:177
  27.8 2.2 %collective-permute-done.6.sib = s16[4,2,528,128]{3,2,1,0:T(8,128)(2,1)S(1)} collective-permute-done((s16[4,2,528,128]{3,2,1,0:T(8,128)(2,1)S(1)}, s16[4,2,528,128]{3,2,1,0:T(8,128)(2,1)S(1)}, u32[]{:S(2)}, u32[]{:S(2)}) %collective-permute-start.6) | collective-permute-done | bytes 1081376 | tf_op jit(solution)/shard_map/ppermute | solution.py:295
  30.8 3.1 %collective-permute-start.7 = (s16[2,528,128]{2,1,0:T(8,128)(2,1)S(1)}, s16[2,528,128]{2,1,0:T(8,128)(2,1)S(1)}, u32[]{:S(2)}, u32[]{:S(2)}) collective-permute-start(s16[2,528,128]{2,1,0:T(8,128)(2,1)S(1)} %get-tuple-element.30), channel_id=1, source_target_pairs={{0,8},{8,0},{16,24},{24,16},{1,9},{9,1},{17,25},{25,17},{2,10},{10... | collective-permute-start | bytes 811016 | tf_op jit(solution)/shard_map/ppermute | solution.py:384
  33.9 1.4 collective-permute-start.8
  35.3 1.4 collective-permute-start.9
  38.2 1.4 collective-permute-start.16
  39.6 1.6 collective-permute-done.7.refs_1_
  41.2 2.8 %collective-permute-start.17 = (s16[2,528,128]{2,1,0:T(8,128)(2,1)S(1)}, s16[2,528,128]{2,1,0:T(8,128)(2,1)S(1)}, u32[]{:S(2)}, u32[]{:S(2)}) collective-permute-start(s16[2,528,128]{2,1,0:T(8,128)(2,1)S(1)} %get-tuple-element.37), channel_id=1, source_target_pairs={{0,24},{8,16},{16,8},{24,0},{1,25},{9,17},{17,9},{25,1},{2,26},{10... | collective-permute-start | bytes 811016 | tf_op jit(solution)/shard_map/ppermute | solution.py:384
  44.0 3.9 %collective-permute-done.8.refs_2_ = s16[2,528,128]{2,1,0:T(8,128)(2,1)S(1)} collective-permute-done((s16[2,528,128]{2,1,0:T(8,128)(2,1)S(1)}, s16[2,528,128]{2,1,0:T(8,128)(2,1)S(1)}, u32[]{:S(2)}, u32[]{:S(2)}) %collective-permute-start.8) | collective-permute-done | bytes 270368 | tf_op jit(solution)/shard_map/ppermute | solution.py:384
  48.0 1.9 %collective-permute-done.9.refs_3_ = s16[2,528,128]{2,1,0:T(8,128)(2,1)S(1)} collective-permute-done((s16[2,528,128]{2,1,0:T(8,128)(2,1)S(1)}, s16[2,528,128]{2,1,0:T(8,128)(2,1)S(1)}, u32[]{:S(2)}, u32[]{:S(2)}) %collective-permute-start.9) | collective-permute-done | bytes 270368 | tf_op jit(solution)/shard_map/ppermute | solution.py:384
  49.9 3.8 %collective-permute-start.10 = (s16[2,528,128]{2,1,0:T(8,128)(2,1)S(1)}, s16[2,528,128]{2,1,0:T(8,128)(2,1)S(1)}, u32[]{:S(2)}, u32[]{:S(2)}) collective-permute-start(s16[2,528,128]{2,1,0:T(8,128)(2,1)S(1)} %relay_message.6), channel_id=1, source_target_pairs={{0,2},{1,3},{2,0},{3,1},{4,6},{5,7},{6,4},{7,5},{8,10},{9,11},{10,... | collective-permute-start | bytes 811016 | tf_op jit(solution)/shard_map/ppermute | solution.py:284
  53.7 5.0 %collective-permute-done.16.refs_2_ = s16[2,528,128]{2,1,0:T(8,128)(2,1)S(1)} collective-permute-done((s16[2,528,128]{2,1,0:T(8,128)(2,1)S(1)}, s16[2,528,128]{2,1,0:T(8,128)(2,1)S(1)}, u32[]{:S(2)}, u32[]{:S(2)}) %collective-permute-start.16) | collective-permute-done | bytes 270368 | tf_op jit(solution)/shard_map/ppermute | solution.py:384
  58.7 1.9 %collective-permute-done.17.refs_3_ = s16[2,528,128]{2,1,0:T(8,128)(2,1)S(1)} collective-permute-done((s16[2,528,128]{2,1,0:T(8,128)(2,1)S(1)}, s16[2,528,128]{2,1,0:T(8,128)(2,1)S(1)}, u32[]{:S(2)}, u32[]{:S(2)}) %collective-permute-start.17) | collective-permute-done | bytes 270368 | tf_op jit(solution)/shard_map/ppermute | solution.py:384
  60.6 3.5 %collective-permute-start.18 = (s16[2,528,128]{2,1,0:T(8,128)(2,1)S(1)}, s16[2,528,128]{2,1,0:T(8,128)(2,1)S(1)}, u32[]{:S(2)}, u32[]{:S(2)}) collective-permute-start(s16[2,528,128]{2,1,0:T(8,128)(2,1)S(1)} %relay_message.9), channel_id=1, source_target_pairs={{0,2},{1,3},{2,0},{3,1},{4,6},{5,7},{6,4},{7,5},{8,10},{9,11},{10,... | collective-permute-start | bytes 811016 | tf_op jit(solution)/shard_map/ppermute | solution.py:284
  64.5 11.1 %collective-permute-done.18.refs_4_ = s16[2,528,128]{2,1,0:T(8,128)(2,1)S(1)} collective-permute-done((s16[2,528,128]{2,1,0:T(8,128)(2,1)S(1)}, s16[2,528,128]{2,1,0:T(8,128)(2,1)S(1)}, u32[]{:S(2)}, u32[]{:S(2)}) %collective-permute-start.18) | collective-permute-done | bytes 270368 | tf_op jit(solution)/shard_map/ppermute | solution.py:284
  76.9 7.6 %collective-permute-start.12 = (s16[2,528,128]{2,1,0:T(8,128)(2,1)S(1)}, s16[2,528,128]{2,1,0:T(8,128)(2,1)S(1)}, u32[]{:S(2)}, u32[]{:S(2)}) collective-permute-start(s16[2,528,128]{2,1,0:T(8,128)(2,1)S(1)} %relay_message.8), channel_id=1, source_target_pairs={{0,2},{1,3},{6,4},{7,5},{8,10},{9,11},{14,12},{15,13},{16,18},{17,... | collective-permute-start | bytes 811016 | tf_op jit(solution)/shard_map/ppermute | solution.py:284
  85.5 5.9 %collective-permute-start.20 = (s16[2,528,128]{2,1,0:T(8,128)(2,1)S(1)}, s16[2,528,128]{2,1,0:T(8,128)(2,1)S(1)}, u32[]{:S(2)}, u32[]{:S(2)}) collective-permute-start(s16[2,528,128]{2,1,0:T(8,128)(2,1)S(1)} %relay_message.11), channel_id=1, source_target_pairs={{0,2},{1,3},{6,4},{7,5},{8,10},{9,11},{14,12},{15,13},{16,18},{17,... | collective-permute-start | bytes 811016 | tf_op jit(solution)/shard_map/ppermute | solution.py:284
  91.8 1.5 collective-permute-start.24
  93.4 2.0 %collective-permute-done.20.refs_6_ = s16[2,528,128]{2,1,0:T(8,128)(2,1)S(1)} collective-permute-done((s16[2,528,128]{2,1,0:T(8,128)(2,1)S(1)}, s16[2,528,128]{2,1,0:T(8,128)(2,1)S(1)}, u32[]{:S(2)}, u32[]{:S(2)}) %collective-permute-start.20) | collective-permute-done | bytes 270368 | tf_op jit(solution)/shard_map/ppermute | solution.py:284
  95.7 1.5 collective-permute-start.23
  97.8 1.5 collective-permute-start.25
  100.1 1.4 collective-permute-start.26
  101.5 3.4 %collective-permute-done.23.refs_3_ = bf16[16,64,128]{2,1,0:T(8,128)(2,1)S(1)} collective-permute-done((bf16[16,64,128]{2,1,0:T(8,128)(2,1)S(1)}, bf16[16,64,128]{2,1,0:T(8,128)(2,1)S(1)}, u32[]{:S(2)}, u32[]{:S(2)}) %collective-permute-start.23) | collective-permute-done | bytes 262176 | tf_op jit(solution)/shard_map/ppermute | solution.py:384
  104.9 1.5 collective-permute-start.27
  106.4 2.5 %collective-permute-done.22.refs_2_ = bf16[16,64,128]{2,1,0:T(8,128)(2,1)S(1)} collective-permute-done((bf16[16,64,128]{2,1,0:T(8,128)(2,1)S(1)}, bf16[16,64,128]{2,1,0:T(8,128)(2,1)S(1)}, u32[]{:S(2)}, u32[]{:S(2)}) %collective-permute-start.22) | collective-permute-done | bytes 262176 | tf_op jit(solution)/shard_map/ppermute | solution.py:384
  109.0 1.5 prepare.3
  110.5 1.3 collective-permute-done.26.refs_0_
  111.8 4.0 %block_product.3 = (bf16[128,64,128]{2,1,0:T(8,128)(2,1)S(1)}, f32[257,64,128]{2,1,0:T(8,128)S(1)}, s16[4,2,528,128]{3,2,1,0:T(8,128)(2,1)S(1)}, s16[4,2,528,128]{3,2,1,0:T(8,128)(2,1)S(1)}) custom-call(s32[1,512]{1,0:T(1,128)S(1)} %copy-done.2, s32[1,512]{1,0:T(1,128)S(1)} %copy-done.3, ...), custom_call_target="tpu_custom_call", output_to_operand_aliasing={{0}: (3, {}), {1}: (4, {})} | custom-call | tf_op jit(solution)/shard_map/block_product/pallas_call | solution.py:177
  116.3 2.2 %collective-permute-done.33.sib = s16[4,2,528,128]{3,2,1,0:T(8,128)(2,1)S(1)} collective-permute-done((s16[4,2,528,128]{3,2,1,0:T(8,128)(2,1)S(1)}, s16[4,2,528,128]{3,2,1,0:T(8,128)(2,1)S(1)}, u32[]{:S(2)}, u32[]{:S(2)}) %collective-permute-start.33) | collective-permute-done | bytes 1081376 | tf_op jit(solution)/shard_map/ppermute | solution.py:295
  118.7 3.5 %collective-permute-start.34 = (s16[2,528,128]{2,1,0:T(8,128)(2,1)S(1)}, s16[2,528,128]{2,1,0:T(8,128)(2,1)S(1)}, u32[]{:S(2)}, u32[]{:S(2)}) collective-permute-start(s16[2,528,128]{2,1,0:T(8,128)(2,1)S(1)} %combine_message.9), channel_id=1, source_target_pairs={{0,2},{1,3},{2,0},{3,1},{4,6},{5,7},{6,4},{7,5},{8,10},{9,11},{10,... | collective-permute-start | bytes 811016 | tf_op jit(solution)/shard_map/ppermute | solution.py:284
  122.3 1.4 collective-permute-start.29
  123.7 5.8 %collective-permute-done.34.refs_0_ = s16[2,528,128]{2,1,0:T(8,128)(2,1)S(1)} collective-permute-done((s16[2,528,128]{2,1,0:T(8,128)(2,1)S(1)}, s16[2,528,128]{2,1,0:T(8,128)(2,1)S(1)}, u32[]{:S(2)}, u32[]{:S(2)}) %collective-permute-start.34) | collective-permute-done | bytes 270368 | tf_op jit(solution)/shard_map/ppermute | solution.py:284
  129.7 2.1 %collective-permute-start.35 = (s16[2,528,128]{2,1,0:T(8,128)(2,1)S(1)}, s16[2,528,128]{2,1,0:T(8,128)(2,1)S(1)}, u32[]{:S(2)}, u32[]{:S(2)}) collective-permute-start(s16[2,528,128]{2,1,0:T(8,128)(2,1)S(1)} %combine_message.10), channel_id=1, source_target_pairs={{0,2},{1,3},{6,4},{7,5},{2,6},{3,7},{4,0},{5,1},{8,10},{9,11},{14,... | collective-permute-start | bytes 811016 | tf_op jit(solution)/shard_map/ppermute | solution.py:284
  131.8 8.7 %collective-permute-done.29.refs_0_ = s16[2,528,128]{2,1,0:T(8,128)(2,1)S(1)} collective-permute-done((s16[2,528,128]{2,1,0:T(8,128)(2,1)S(1)}, s16[2,528,128]{2,1,0:T(8,128)(2,1)S(1)}, u32[]{:S(2)}, u32[]{:S(2)}) %collective-permute-start.29) | collective-permute-done | bytes 270368 | tf_op jit(solution)/shard_map/ppermute | solution.py:284
  141.8 6.6 %collective-permute-start.36 = (s16[2,528,128]{2,1,0:T(8,128)(2,1)S(1)}, s16[2,528,128]{2,1,0:T(8,128)(2,1)S(1)}, u32[]{:S(2)}, u32[]{:S(2)}) collective-permute-start(s16[2,528,128]{2,1,0:T(8,128)(2,1)S(1)} %combine_message.11), channel_id=1, source_target_pairs={{0,2},{1,3},{6,4},{7,5},{8,10},{9,11},{14,12},{15,13},{16,18},{17,... | collective-permute-start | bytes 811016 | tf_op jit(solution)/shard_map/ppermute | solution.py:284
  148.4 2.6 %collective-permute-done.30.refs_0_.refs_1_ = s16[2,528,128]{2,1,0:T(8,128)(2,1)S(1)} collective-permute-done((s16[2,528,128]{2,1,0:T(8,128)(2,1)S(1)}, s16[2,528,128]{2,1,0:T(8,128)(2,1)S(1)}, u32[]{:S(2)}, u32[]{:S(2)}) %collective-permute-start.30) | collective-permute-done | bytes 270368 | tf_op jit(solution)/shard_map/ppermute | solution.py:284
  152.0 3.3 %collective-permute-start.31 = (s16[2,528,128]{2,1,0:T(8,128)(2,1)S(1)}, s16[2,528,128]{2,1,0:T(8,128)(2,1)S(1)}, u32[]{:S(2)}, u32[]{:S(2)}) collective-permute-start(s16[2,528,128]{2,1,0:T(8,128)(2,1)S(1)} %combine_message.8), channel_id=1, source_target_pairs={{0,2},{1,3},{6,4},{7,5},{8,10},{9,11},{14,12},{15,13},{16,18},{17,... | collective-permute-start | bytes 811016 | tf_op jit(solution)/shard_map/ppermute | solution.py:284
  155.3 1.1 combine_rows.2.refs_4_
  156.4 2.8 %collective-permute-done.31.refs_2_ = s16[2,528,128]{2,1,0:T(8,128)(2,1)S(1)} collective-permute-done((s16[2,528,128]{2,1,0:T(8,128)(2,1)S(1)}, s16[2,528,128]{2,1,0:T(8,128)(2,1)S(1)}, u32[]{:S(2)}, u32[]{:S(2)}) %collective-permute-start.31) | collective-permute-done | bytes 270368 | tf_op jit(solution)/shard_map/ppermute | solution.py:284
  159.2 1.1 combine_rows.3
  (60 shorter events, 12.9 us)
Async XLA Ops:
  0.0 1.0 copy-start
  1.2 10.2 %collective-permute-start.1 = (bf16[16,64,128]{2,1,0:T(8,128)(2,1)S(1)}, bf16[16,64,128]{2,1,0:T(8,128)(2,1)S(1)}, u32[]{:S(2)}, u32[]{:S(2)}) collective-permute-start(bf16[16,64,128]{2,1,0:T(8,128)(2,1)S(1)} %get-tuple-element.43.refs_1_), channel_id=1, source_target_pairs={{0,8},{8,0},{16,24},{24,16},{1,9},{9,1},{17,25},{25,17},{2,10},{10... | collective-permute-start | bytes 786440 | tf_op jit(solution)/shard_map/ppermute | solution.py:384
  4.3 9.2 %collective-permute-start.2 = (bf16[16,64,128]{2,1,0:T(8,128)(2,1)S(1)}, bf16[16,64,128]{2,1,0:T(8,128)(2,1)S(1)}, u32[]{:S(2)}, u32[]{:S(2)}) collective-permute-start(bf16[16,64,128]{2,1,0:T(8,128)(2,1)S(1)} %get-tuple-element.44.refs_0_), channel_id=1, source_target_pairs={{0,16},{8,24},{16,0},{24,8},{1,17},{9,25},{17,1},{25,9},{2,18},{10... | collective-permute-start | bytes 786440 | tf_op jit(solution)/shard_map/ppermute | solution.py:384
  5.8 13.3 %collective-permute-start.3 = (bf16[16,64,128]{2,1,0:T(8,128)(2,1)S(1)}, bf16[16,64,128]{2,1,0:T(8,128)(2,1)S(1)}, u32[]{:S(2)}, u32[]{:S(2)}) collective-permute-start(bf16[16,64,128]{2,1,0:T(8,128)(2,1)S(1)} %get-tuple-element.43.refs_1_), channel_id=1, source_target_pairs={{0,16},{8,24},{16,0},{24,8},{1,17},{9,25},{17,1},{25,9},{2,18},{10... | collective-permute-start | bytes 786440 | tf_op jit(solution)/shard_map/ppermute | solution.py:384
  6.3 12.8 %collective-permute-start = (bf16[16,64,128]{2,1,0:T(8,128)(2,1)S(1)}, bf16[16,64,128]{2,1,0:T(8,128)(2,1)S(1)}, u32[]{:S(2)}, u32[]{:S(2)}) collective-permute-start(bf16[16,64,128]{2,1,0:T(8,128)(2,1)S(1)} %get-tuple-element.44.refs_0_), channel_id=1, source_target_pairs={{0,8},{8,0},{16,24},{24,16},{1,9},{9,1},{17,25},{25,17},{2,10},{10... | collective-permute-start | bytes 786440 | tf_op jit(solution)/shard_map/ppermute | solution.py:384
  11.4 11.8 %collective-permute-start.5 = (bf16[16,64,128]{2,1,0:T(8,128)(2,1)S(1)}, bf16[16,64,128]{2,1,0:T(8,128)(2,1)S(1)}, u32[]{:S(2)}, u32[]{:S(2)}) collective-permute-start(bf16[16,64,128]{2,1,0:T(8,128)(2,1)S(1)} %collective-permute-done.1.refs_3_), channel_id=1, source_target_pairs={{0,16},{8,24},{16,0},{24,8},{1,17},{9,25},{17,1},{25,9},{2,18},{10... | collective-permute-start | bytes 786440 | tf_op jit(solution)/shard_map/ppermute | solution.py:384
  13.5 9.8 %collective-permute-start.4 = (bf16[16,64,128]{2,1,0:T(8,128)(2,1)S(1)}, bf16[16,64,128]{2,1,0:T(8,128)(2,1)S(1)}, u32[]{:S(2)}, u32[]{:S(2)}) collective-permute-start(bf16[16,64,128]{2,1,0:T(8,128)(2,1)S(1)} %collective-permute-done.2.refs_4_), channel_id=1, source_target_pairs={{0,8},{8,0},{16,24},{24,16},{1,9},{9,1},{17,25},{25,17},{2,10},{10... | collective-permute-start | bytes 786440 | tf_op jit(solution)/shard_map/ppermute | solution.py:384
  19.1 4.2 %copy-start.2 = (s32[1,512]{1,0:T(1,128)S(1)}, s32[1,512]{1,0:T(1,128)}, u32[]{:S(2)}) copy-start(s32[1,512]{1,0:T(1,128)} %rows.3) | copy-start | bytes 6148
  19.1 4.2 %copy-start.3 = (s32[1,512]{1,0:T(1,128)S(1)}, s32[1,512]{1,0:T(1,128)}, u32[]{:S(2)}) copy-start(s32[1,512]{1,0:T(1,128)} %cols.3) | copy-start | bytes 6148
  27.3 2.8 %collective-permute-start.6 = (s16[4,2,528,128]{3,2,1,0:T(8,128)(2,1)S(1)}, s16[4,2,528,128]{3,2,1,0:T(8,128)(2,1)S(1)}, u32[]{:S(2)}, u32[]{:S(2)}) collective-permute-start(s16[4,2,528,128]{3,2,1,0:T(8,128)(2,1)S(1)} %get-tuple-element.28), channel_id=1, source_target_pairs={{0,1},{1,0},{2,3},{3,2},{4,5},{5,4},{6,7},{7,6},{8,9},{9,8},{10,11... | collective-permute-start | bytes 3244040 | tf_op jit(solution)/shard_map/ppermute | solution.py:295
  27.3 9.3 %collective-permute-start.14 = (s16[4,2,528,128]{3,2,1,0:T(8,128)(2,1)S(1)}, s16[4,2,528,128]{3,2,1,0:T(8,128)(2,1)S(1)}, u32[]{:S(2)}, u32[]{:S(2)}) collective-permute-start(s16[4,2,528,128]{3,2,1,0:T(8,128)(2,1)S(1)} %get-tuple-element.33), channel_id=1, source_target_pairs={{0,1},{1,0},{2,3},{3,2},{4,5},{5,4},{6,7},{7,6},{8,9},{9,8},{10,11... | collective-permute-start | bytes 3244040 | tf_op jit(solution)/shard_map/ppermute | solution.py:295
  30.8 10.4 %collective-permute-start.7 = (s16[2,528,128]{2,1,0:T(8,128)(2,1)S(1)}, s16[2,528,128]{2,1,0:T(8,128)(2,1)S(1)}, u32[]{:S(2)}, u32[]{:S(2)}) collective-permute-start(s16[2,528,128]{2,1,0:T(8,128)(2,1)S(1)} %get-tuple-element.30), channel_id=1, source_target_pairs={{0,8},{8,0},{16,24},{24,16},{1,9},{9,1},{17,25},{25,17},{2,10},{10... | collective-permute-start | bytes 811016 | tf_op jit(solution)/shard_map/ppermute | solution.py:384
  33.9 14.1 %collective-permute-start.8 = (s16[2,528,128]{2,1,0:T(8,128)(2,1)S(1)}, s16[2,528,128]{2,1,0:T(8,128)(2,1)S(1)}, u32[]{:S(2)}, u32[]{:S(2)}) collective-permute-start(s16[2,528,128]{2,1,0:T(8,128)(2,1)S(1)} %get-tuple-element.31), channel_id=1, source_target_pairs={{0,16},{8,24},{16,0},{24,8},{1,17},{9,25},{17,1},{25,9},{2,18},{10... | collective-permute-start | bytes 811016 | tf_op jit(solution)/shard_map/ppermute | solution.py:384
  35.3 14.5 %collective-permute-start.9 = (s16[2,528,128]{2,1,0:T(8,128)(2,1)S(1)}, s16[2,528,128]{2,1,0:T(8,128)(2,1)S(1)}, u32[]{:S(2)}, u32[]{:S(2)}) collective-permute-start(s16[2,528,128]{2,1,0:T(8,128)(2,1)S(1)} %get-tuple-element.32), channel_id=1, source_target_pairs={{0,24},{8,16},{16,8},{24,0},{1,25},{9,17},{17,9},{25,1},{2,26},{10... | collective-permute-start | bytes 811016 | tf_op jit(solution)/shard_map/ppermute | solution.py:384
  37.5 16.2 %collective-permute-start.15 = (s16[2,528,128]{2,1,0:T(8,128)(2,1)S(1)}, s16[2,528,128]{2,1,0:T(8,128)(2,1)S(1)}, u32[]{:S(2)}, u32[]{:S(2)}) collective-permute-start(s16[2,528,128]{2,1,0:T(8,128)(2,1)S(1)} %get-tuple-element.35), channel_id=1, source_target_pairs={{0,8},{8,0},{16,24},{24,16},{1,9},{9,1},{17,25},{25,17},{2,10},{10... | collective-permute-start | bytes 811016 | tf_op jit(solution)/shard_map/ppermute | solution.py:384
  38.2 20.5 %collective-permute-start.16 = (s16[2,528,128]{2,1,0:T(8,128)(2,1)S(1)}, s16[2,528,128]{2,1,0:T(8,128)(2,1)S(1)}, u32[]{:S(2)}, u32[]{:S(2)}) collective-permute-start(s16[2,528,128]{2,1,0:T(8,128)(2,1)S(1)} %get-tuple-element.36), channel_id=1, source_target_pairs={{0,16},{8,24},{16,0},{24,8},{1,17},{9,25},{17,1},{25,9},{2,18},{10... | collective-permute-start | bytes 811016 | tf_op jit(solution)/shard_map/ppermute | solution.py:384
  41.2 19.4 %collective-permute-start.17 = (s16[2,528,128]{2,1,0:T(8,128)(2,1)S(1)}, s16[2,528,128]{2,1,0:T(8,128)(2,1)S(1)}, u32[]{:S(2)}, u32[]{:S(2)}) collective-permute-start(s16[2,528,128]{2,1,0:T(8,128)(2,1)S(1)} %get-tuple-element.37), channel_id=1, source_target_pairs={{0,24},{8,16},{16,8},{24,0},{1,25},{9,17},{17,9},{25,1},{2,26},{10... | collective-permute-start | bytes 811016 | tf_op jit(solution)/shard_map/ppermute | solution.py:384
  49.9 14.3 %collective-permute-start.10 = (s16[2,528,128]{2,1,0:T(8,128)(2,1)S(1)}, s16[2,528,128]{2,1,0:T(8,128)(2,1)S(1)}, u32[]{:S(2)}, u32[]{:S(2)}) collective-permute-start(s16[2,528,128]{2,1,0:T(8,128)(2,1)S(1)} %relay_message.6), channel_id=1, source_target_pairs={{0,2},{1,3},{2,0},{3,1},{4,6},{5,7},{6,4},{7,5},{8,10},{9,11},{10,... | collective-permute-start | bytes 811016 | tf_op jit(solution)/shard_map/ppermute | solution.py:284
  60.6 15.0 %collective-permute-start.18 = (s16[2,528,128]{2,1,0:T(8,128)(2,1)S(1)}, s16[2,528,128]{2,1,0:T(8,128)(2,1)S(1)}, u32[]{:S(2)}, u32[]{:S(2)}) collective-permute-start(s16[2,528,128]{2,1,0:T(8,128)(2,1)S(1)} %relay_message.9), channel_id=1, source_target_pairs={{0,2},{1,3},{2,0},{3,1},{4,6},{5,7},{6,4},{7,5},{8,10},{9,11},{10,... | collective-permute-start | bytes 811016 | tf_op jit(solution)/shard_map/ppermute | solution.py:284
  64.4 11.5 %collective-permute-start.11 = (s16[2,528,128]{2,1,0:T(8,128)(2,1)S(1)}, s16[2,528,128]{2,1,0:T(8,128)(2,1)S(1)}, u32[]{:S(2)}, u32[]{:S(2)}) collective-permute-start(s16[2,528,128]{2,1,0:T(8,128)(2,1)S(1)} %relay_message.7), channel_id=1, source_target_pairs={{0,2},{1,3},{6,4},{7,5},{2,6},{3,7},{4,0},{5,1},{8,10},{9,11},{14,... | collective-permute-start | bytes 811016 | tf_op jit(solution)/shard_map/ppermute | solution.py:284
  75.9 8.7 %collective-permute-start.19 = (s16[2,528,128]{2,1,0:T(8,128)(2,1)S(1)}, s16[2,528,128]{2,1,0:T(8,128)(2,1)S(1)}, u32[]{:S(2)}, u32[]{:S(2)}) collective-permute-start(s16[2,528,128]{2,1,0:T(8,128)(2,1)S(1)} %relay_message.10), channel_id=1, source_target_pairs={{0,2},{1,3},{6,4},{7,5},{2,6},{3,7},{4,0},{5,1},{8,10},{9,11},{14,... | collective-permute-start | bytes 811016 | tf_op jit(solution)/shard_map/ppermute | solution.py:284
  76.2 15.2 %collective-permute-start.13 = (s16[2,528,128]{2,1,0:T(8,128)(2,1)S(1)}, s16[2,528,128]{2,1,0:T(8,128)(2,1)S(1)}, u32[]{:S(2)}, u32[]{:S(2)}) collective-permute-start(s16[2,528,128]{2,1,0:T(8,128)(2,1)S(1)} %relay_message.8), channel_id=1, source_target_pairs={{2,4},{3,5},{4,2},{5,3},{10,12},{11,13},{12,10},{13,11},{18,20},{1... | collective-permute-start | bytes 811016 | tf_op jit(solution)/shard_map/ppermute | solution.py:284
  76.9 14.5 %collective-permute-start.12 = (s16[2,528,128]{2,1,0:T(8,128)(2,1)S(1)}, s16[2,528,128]{2,1,0:T(8,128)(2,1)S(1)}, u32[]{:S(2)}, u32[]{:S(2)}) collective-permute-start(s16[2,528,128]{2,1,0:T(8,128)(2,1)S(1)} %relay_message.8), channel_id=1, source_target_pairs={{0,2},{1,3},{6,4},{7,5},{8,10},{9,11},{14,12},{15,13},{16,18},{17,... | collective-permute-start | bytes 811016 | tf_op jit(solution)/shard_map/ppermute | solution.py:284
  84.8 8.5 %collective-permute-start.21 = (s16[2,528,128]{2,1,0:T(8,128)(2,1)S(1)}, s16[2,528,128]{2,1,0:T(8,128)(2,1)S(1)}, u32[]{:S(2)}, u32[]{:S(2)}) collective-permute-start(s16[2,528,128]{2,1,0:T(8,128)(2,1)S(1)} %relay_message.11), channel_id=1, source_target_pairs={{2,4},{3,5},{4,2},{5,3},{10,12},{11,13},{12,10},{13,11},{18,20},{1... | collective-permute-start | bytes 811016 | tf_op jit(solution)/shard_map/ppermute | solution.py:284
  85.5 9.8 %collective-permute-start.20 = (s16[2,528,128]{2,1,0:T(8,128)(2,1)S(1)}, s16[2,528,128]{2,1,0:T(8,128)(2,1)S(1)}, u32[]{:S(2)}, u32[]{:S(2)}) collective-permute-start(s16[2,528,128]{2,1,0:T(8,128)(2,1)S(1)} %relay_message.11), channel_id=1, source_target_pairs={{0,2},{1,3},{6,4},{7,5},{8,10},{9,11},{14,12},{15,13},{16,18},{17,... | collective-permute-start | bytes 811016 | tf_op jit(solution)/shard_map/ppermute | solution.py:284
  91.8 8.3 %collective-permute-start.24 = (bf16[16,64,128]{2,1,0:T(8,128)(2,1)S(1)}, bf16[16,64,128]{2,1,0:T(8,128)(2,1)S(1)}, u32[]{:S(2)}, u32[]{:S(2)}) collective-permute-start(bf16[16,64,128]{2,1,0:T(8,128)(2,1)S(1)} %relay_tiles.2.refs_0_), channel_id=1, source_target_pairs={{0,16},{8,24},{16,0},{24,8},{1,17},{9,25},{17,1},{25,9},{2,18},{10... | collective-permute-start | bytes 786440 | tf_op jit(solution)/shard_map/ppermute | solution.py:384
  95.7 9.2 %collective-permute-start.23 = (bf16[16,64,128]{2,1,0:T(8,128)(2,1)S(1)}, bf16[16,64,128]{2,1,0:T(8,128)(2,1)S(1)}, u32[]{:S(2)}, u32[]{:S(2)}) collective-permute-start(bf16[16,64,128]{2,1,0:T(8,128)(2,1)S(1)} %relay_tiles.3.refs_1_), channel_id=1, source_target_pairs={{0,8},{8,0},{16,24},{24,16},{1,9},{9,1},{17,25},{25,17},{2,10},{10... | collective-permute-start | bytes 786440 | tf_op jit(solution)/shard_map/ppermute | solution.py:384
  97.2 11.8 %collective-permute-start.22 = (bf16[16,64,128]{2,1,0:T(8,128)(2,1)S(1)}, bf16[16,64,128]{2,1,0:T(8,128)(2,1)S(1)}, u32[]{:S(2)}, u32[]{:S(2)}) collective-permute-start(bf16[16,64,128]{2,1,0:T(8,128)(2,1)S(1)} %relay_tiles.2.refs_0_), channel_id=1, source_target_pairs={{0,8},{8,0},{16,24},{24,16},{1,9},{9,1},{17,25},{25,17},{2,10},{10... | collective-permute-start | bytes 786440 | tf_op jit(solution)/shard_map/ppermute | solution.py:384
  97.8 11.2 %collective-permute-start.25 = (bf16[16,64,128]{2,1,0:T(8,128)(2,1)S(1)}, bf16[16,64,128]{2,1,0:T(8,128)(2,1)S(1)}, u32[]{:S(2)}, u32[]{:S(2)}) collective-permute-start(bf16[16,64,128]{2,1,0:T(8,128)(2,1)S(1)} %relay_tiles.3.refs_1_), channel_id=1, source_target_pairs={{0,16},{8,24},{16,0},{24,8},{1,17},{9,25},{17,1},{25,9},{2,18},{10... | collective-permute-start | bytes 786440 | tf_op jit(solution)/shard_map/ppermute | solution.py:384
  100.1 11.7 %collective-permute-start.26 = (bf16[16,64,128]{2,1,0:T(8,128)(2,1)S(1)}, bf16[16,64,128]{2,1,0:T(8,128)(2,1)S(1)}, u32[]{:S(2)}, u32[]{:S(2)}) collective-permute-start(bf16[16,64,128]{2,1,0:T(8,128)(2,1)S(1)} %collective-permute-done.24.refs_4_), channel_id=1, source_target_pairs={{0,8},{8,0},{16,24},{24,16},{1,9},{9,1},{17,25},{25,17},{2,10},{10... | collective-permute-start | bytes 786440 | tf_op jit(solution)/shard_map/ppermute | solution.py:384
  104.9 6.8 %collective-permute-start.27 = (bf16[16,64,128]{2,1,0:T(8,128)(2,1)S(1)}, bf16[16,64,128]{2,1,0:T(8,128)(2,1)S(1)}, u32[]{:S(2)}, u32[]{:S(2)}) collective-permute-start(bf16[16,64,128]{2,1,0:T(8,128)(2,1)S(1)} %collective-permute-done.23.refs_3_), channel_id=1, source_target_pairs={{0,16},{8,24},{16,0},{24,8},{1,17},{9,25},{17,1},{25,9},{2,18},{10... | collective-permute-start | bytes 786440 | tf_op jit(solution)/shard_map/ppermute | solution.py:384
  115.7 2.8 %collective-permute-start.33 = (s16[4,2,528,128]{3,2,1,0:T(8,128)(2,1)S(1)}, s16[4,2,528,128]{3,2,1,0:T(8,128)(2,1)S(1)}, u32[]{:S(2)}, u32[]{:S(2)}) collective-permute-start(s16[4,2,528,128]{3,2,1,0:T(8,128)(2,1)S(1)} %get-tuple-element.42), channel_id=1, source_target_pairs={{0,1},{1,0},{2,3},{3,2},{4,5},{5,4},{6,7},{7,6},{8,9},{9,8},{10,11... | collective-permute-start | bytes 3244040 | tf_op jit(solution)/shard_map/ppermute | solution.py:295
  115.8 6.3 %collective-permute-start.28 = (s16[4,2,528,128]{3,2,1,0:T(8,128)(2,1)S(1)}, s16[4,2,528,128]{3,2,1,0:T(8,128)(2,1)S(1)}, u32[]{:S(2)}, u32[]{:S(2)}) collective-permute-start(s16[4,2,528,128]{3,2,1,0:T(8,128)(2,1)S(1)} %get-tuple-element.41), channel_id=1, source_target_pairs={{0,1},{1,0},{2,3},{3,2},{4,5},{5,4},{6,7},{7,6},{8,9},{9,8},{10,11... | collective-permute-start | bytes 3244040 | tf_op jit(solution)/shard_map/ppermute | solution.py:295
  118.7 10.8 %collective-permute-start.34 = (s16[2,528,128]{2,1,0:T(8,128)(2,1)S(1)}, s16[2,528,128]{2,1,0:T(8,128)(2,1)S(1)}, u32[]{:S(2)}, u32[]{:S(2)}) collective-permute-start(s16[2,528,128]{2,1,0:T(8,128)(2,1)S(1)} %combine_message.9), channel_id=1, source_target_pairs={{0,2},{1,3},{2,0},{3,1},{4,6},{5,7},{6,4},{7,5},{8,10},{9,11},{10,... | collective-permute-start | bytes 811016 | tf_op jit(solution)/shard_map/ppermute | solution.py:284
  122.3 18.2 %collective-permute-start.29 = (s16[2,528,128]{2,1,0:T(8,128)(2,1)S(1)}, s16[2,528,128]{2,1,0:T(8,128)(2,1)S(1)}, u32[]{:S(2)}, u32[]{:S(2)}) collective-permute-start(s16[2,528,128]{2,1,0:T(8,128)(2,1)S(1)} %combine_message.6), channel_id=1, source_target_pairs={{0,2},{1,3},{2,0},{3,1},{4,6},{5,7},{6,4},{7,5},{8,10},{9,11},{10,... | collective-permute-start | bytes 811016 | tf_op jit(solution)/shard_map/ppermute | solution.py:284
  129.7 11.1 %collective-permute-start.35 = (s16[2,528,128]{2,1,0:T(8,128)(2,1)S(1)}, s16[2,528,128]{2,1,0:T(8,128)(2,1)S(1)}, u32[]{:S(2)}, u32[]{:S(2)}) collective-permute-start(s16[2,528,128]{2,1,0:T(8,128)(2,1)S(1)} %combine_message.10), channel_id=1, source_target_pairs={{0,2},{1,3},{6,4},{7,5},{2,6},{3,7},{4,0},{5,1},{8,10},{9,11},{14,... | collective-permute-start | bytes 811016 | tf_op jit(solution)/shard_map/ppermute | solution.py:284
  140.8 10.3 %collective-permute-start.30 = (s16[2,528,128]{2,1,0:T(8,128)(2,1)S(1)}, s16[2,528,128]{2,1,0:T(8,128)(2,1)S(1)}, u32[]{:S(2)}, u32[]{:S(2)}) collective-permute-start(s16[2,528,128]{2,1,0:T(8,128)(2,1)S(1)} %combine_message.7), channel_id=1, source_target_pairs={{0,2},{1,3},{6,4},{7,5},{2,6},{3,7},{4,0},{5,1},{8,10},{9,11},{14,... | collective-permute-start | bytes 811016 | tf_op jit(solution)/shard_map/ppermute | solution.py:284
  141.1 14.2 %collective-permute-start.37 = (s16[2,528,128]{2,1,0:T(8,128)(2,1)S(1)}, s16[2,528,128]{2,1,0:T(8,128)(2,1)S(1)}, u32[]{:S(2)}, u32[]{:S(2)}) collective-permute-start(s16[2,528,128]{2,1,0:T(8,128)(2,1)S(1)} %combine_message.11), channel_id=1, source_target_pairs={{2,4},{3,5},{4,2},{5,3},{10,12},{11,13},{12,10},{13,11},{18,20},{1... | collective-permute-start | bytes 811016 | tf_op jit(solution)/shard_map/ppermute | solution.py:284
  141.8 13.5 %collective-permute-start.36 = (s16[2,528,128]{2,1,0:T(8,128)(2,1)S(1)}, s16[2,528,128]{2,1,0:T(8,128)(2,1)S(1)}, u32[]{:S(2)}, u32[]{:S(2)}) collective-permute-start(s16[2,528,128]{2,1,0:T(8,128)(2,1)S(1)} %combine_message.11), channel_id=1, source_target_pairs={{0,2},{1,3},{6,4},{7,5},{8,10},{9,11},{14,12},{15,13},{16,18},{17,... | collective-permute-start | bytes 811016 | tf_op jit(solution)/shard_map/ppermute | solution.py:284
  151.3 5.1 %collective-permute-start.32 = (s16[2,528,128]{2,1,0:T(8,128)(2,1)S(1)}, s16[2,528,128]{2,1,0:T(8,128)(2,1)S(1)}, u32[]{:S(2)}, u32[]{:S(2)}) collective-permute-start(s16[2,528,128]{2,1,0:T(8,128)(2,1)S(1)} %combine_message.8), channel_id=1, source_target_pairs={{2,4},{3,5},{4,2},{5,3},{10,12},{11,13},{12,10},{13,11},{18,20},{1... | collective-permute-start | bytes 811016 | tf_op jit(solution)/shard_map/ppermute | solution.py:284
  152.0 7.2 %collective-permute-start.31 = (s16[2,528,128]{2,1,0:T(8,128)(2,1)S(1)}, s16[2,528,128]{2,1,0:T(8,128)(2,1)S(1)}, u32[]{:S(2)}, u32[]{:S(2)}) collective-permute-start(s16[2,528,128]{2,1,0:T(8,128)(2,1)S(1)} %combine_message.8), channel_id=1, source_target_pairs={{0,2},{1,3},{6,4},{7,5},{8,10},{9,11},{14,12},{15,13},{16,18},{17,... | collective-permute-start | bytes 811016 | tf_op jit(solution)/shard_map/ppermute | solution.py:284
  159.2 1.1 copy-start.1

commit v6 on v5

--- a/solution.py
+++ b/solution.py
@@ -117,10 +117,9 @@
 
 
 def product_kernel(place, halves, shard, rows, cols, count, panel_in, acc_in, held, *refs):
-    total = len(refs) - 5
+    total = len(refs) - 4
     pieces = refs[:total]
-    panel, acc, msg_low, msg_high, sem = refs[total:]
-    chips, groups = msg_low.shape[:2]
+    panel, acc, msg_low, sem = refs[total:]
     k = panel.shape[1]
     row_total = acc.shape[0] - 1
     n = count[0, 0]
@@ -159,31 +158,36 @@
             at = jnp.where(base + u < n, rows[0, base + u], row_total)
             acc[at] += products[u]
 
-    other = 1 - col_owner % 2
-    for half, msg in enumerate((msg_low, msg_high)):
-
-        @pl.loop(0, chips * groups)
-        def _(i):
-            d, g = i // groups, i % groups
-            owner = other * chips + d if halves else 2 * d + other
-            base = owner * shard + (half * groups + g) * GROUP
-            encode([acc[base + t] for t in range(GROUP)], msg.at[d, g])
+    encode_half(0, halves, shard, acc, msg_low)
+
+
+def encode_half(half, halves, shard, acc, msg):
+    chips, groups = msg.shape[:2]
+    other = 1 - lax.axis_index("col") % 2
+
+    @pl.loop(0, chips * groups)
+    def _(i):
+        d, g = i // groups, i % groups
+        owner = other * chips + d if halves else 2 * d + other
+        base = owner * shard + (half * groups + g) * GROUP
+        encode([acc[base + t] for t in range(GROUP)], msg.at[d, g])
 
 
 def block_product(late, place, halves, panel, acc, held, block_rows, block_cols, counts, shard, col_total):
     _, k, order = panel.shape
     scalars = pl.BlockSpec(memory_space=pltpu.SMEM)
     message = pltpu.VMEM((col_total // 2, shard // GROUP // 2, message_rows(k), order), jnp.int16)
-    return pl.pallas_call(
+    _, acc, low = pl.pallas_call(
         functools.partial(product_kernel, place, halves, shard),
-        out_shape=(pltpu.VMEM(panel.shape, panel.dtype), pltpu.VMEM(acc.shape, acc.dtype), message, message),
+        out_shape=(pltpu.VMEM(panel.shape, panel.dtype), pltpu.VMEM(acc.shape, acc.dtype), message),
         in_specs=[scalars] * 3 + [NEAR] * (3 + len(late)),
-        out_specs=(NEAR,) * 4,
+        out_specs=(NEAR,) * 3,
         input_output_aliases={3: 0, 4: 1},
         scratch_shapes=[pltpu.SemaphoreType.DMA((max(len(late), 1),))],
         compiler_params=pltpu.CompilerParams(vmem_limit_bytes=SMALL),
         name="block_product",
-    )(block_rows, block_cols, counts, near(panel), near(acc), near(held), *[near(p) for p in late])[1:]
+    )(block_rows, block_cols, counts, near(panel), near(acc), near(held), *[near(p) for p in late])
+    return acc, low, small_call(functools.partial(encode_half, 1, halves, shard), "encode_half", message, (acc,))
 
 
 def combine_kernel(half, which, gates, form, acc, sib, *refs):

time: 162 us -> 162 us (level); the launches traced: 160 us -> 162 us
  starting transfers between devices: 69.2 us -> 54.1 us
  Pallas kernels: 19.4 us -> 29.7 us
  waiting for transfers between devices: 69.4 us -> 76.1 us
    ppermute x16, starting transfers between devices: 40.5 us -> 32 us  [move(): return lax.ppermute(x, 'col', chip_moves(moves))]
    ppermute x18, starting transfers between devices: 27.5 us -> 21 us  [across(): return lax.ppermute(x, 'row', [(r, r ^ flip) for r in range(4)])]
    pallas_call x2, Pallas kernels: 7.92 us -> 14 us  [block_product(): pl.pallas_call(functools.partial(product_kernel, place, halves, shard), o...]
    ppermute x18, waiting for transfers between devices: 32 us -> 37.2 us  [across(): return lax.ppermute(x, 'row', [(r, r ^ flip) for r in range(4)])]
    pallas_call x2, Pallas kernels: 4.53 us -> 7.52 us  [prepare(): pl.pallas_call(functools.partial(prepare_kernel, blocks is not None), out...]
    ppermute x16, waiting for transfers between devices: 33 us -> 35.2 us  [move(): return lax.ppermute(x, 'col', chip_moves(moves))]
    pallas_call x10 -> x12, Pallas kernels: 3.42 us -> 4.55 us  [small_call(): pl.pallas_call(kernel, out_shape=out_shape, in_specs=[NEAR] * len(operand...]
  transfers between devices with their start and end apart: 38 -> 38, of which waited for: 20 -> 19; matrix products, arithmetic and copies ran while one was open for 0% -> 0% of each run, Pallas kernels for 7% -> 9%
where the time goes in v6:
time: 162 us
  waiting for transfers between devices  76.1 us (47%)
  starting transfers between devices  54.1 us (33%)
  Pallas kernels  29.7 us (18%)
    ppermute x18, waiting for transfers between devices, across(): return lax.ppermute(x, 'row', [(r, r ^ flip) for r in range(4)])  37.2 us
    ppermute x16, waiting for transfers between devices, move(): return lax.ppermute(x, 'col', chip_moves(moves))  35.2 us
    ppermute x16, starting transfers between devices, move(): return lax.ppermute(x, 'col', chip_moves(moves))  32 us
    ppermute x18, starting transfers between devices, across(): return lax.ppermute(x, 'row', [(r, r ^ flip) for r in range(4)])  21 us
    pallas_call x2, Pallas kernels, block_product(): pl.pallas_call(functools.partial(product_kernel, place, halves, shard), o...  14 us
    pallas_call x2, Pallas kernels, prepare(): pl.pallas_call(functools.partial(prepare_kernel, blocks is not None), out...  7.52 us
    pallas_call x12, Pallas kernels, small_call(): pl.pallas_call(kernel, out_shape=out_shape, in_specs=[NEAR] * len(operand...  4.55 us
    ppermute x4, waiting for transfers between devices, swap_cores(): lax.ppermute(msg, 'col', [(c, c ^ 1) for c in range(2 * msg.shape[0])])  3.78 us
  transfers between devices with their start and end apart: 38, of which 19 were waited for; matrix products, arithmetic and copies ran while one was open for 0% of the time, Pallas kernels for 9%

profile of v6, /device:TPU:0, one launch (start us, length us, event | category | flops | bytes accessed | tf_op | source)
XLA Modules:
  0.0 162.2 jit_solution(12118414177055085055)
XLA Ops:
  0.0 1.0 copy-done
  1.2 3.0 %collective-permute-start.1 = (bf16[16,64,128]{2,1,0:T(8,128)(2,1)S(1)}, bf16[16,64,128]{2,1,0:T(8,128)(2,1)S(1)}, u32[]{:S(2)}, u32[]{:S(2)}) collective-permute-start(bf16[16,64,128]{2,1,0:T(8,128)(2,1)S(1)} %get-tuple-element.39.refs_1_), channel_id=1, source_target_pairs={{0,8},{8,0},{16,24},{24,16},{1,9},{9,1},{17,25},{25,17},{2,10},{10... | collective-permute-start | bytes 786440 | tf_op jit(solution)/shard_map/ppermute | solution.py:388
  4.3 1.5 collective-permute-start.2
  6.4 5.0 %collective-permute-done.1.refs_3_ = bf16[16,64,128]{2,1,0:T(8,128)(2,1)S(1)} collective-permute-done((bf16[16,64,128]{2,1,0:T(8,128)(2,1)S(1)}, bf16[16,64,128]{2,1,0:T(8,128)(2,1)S(1)}, u32[]{:S(2)}, u32[]{:S(2)}) %collective-permute-start.1) | collective-permute-done | bytes 262176 | tf_op jit(solution)/shard_map/ppermute | solution.py:388
  11.4 2.0 %collective-permute-start.5 = (bf16[16,64,128]{2,1,0:T(8,128)(2,1)S(1)}, bf16[16,64,128]{2,1,0:T(8,128)(2,1)S(1)}, u32[]{:S(2)}, u32[]{:S(2)}) collective-permute-start(bf16[16,64,128]{2,1,0:T(8,128)(2,1)S(1)} %collective-permute-done.1.refs_3_), channel_id=1, source_target_pairs={{0,16},{8,24},{16,0},{24,8},{1,17},{9,25},{17,1},{25,9},{2,18},{10... | collective-permute-start | bytes 786440 | tf_op jit(solution)/shard_map/ppermute | solution.py:388
  13.5 1.5 collective-permute-start.4
  15.6 3.4 %collective-permute-done.3.refs_5_ = bf16[16,64,128]{2,1,0:T(8,128)(2,1)S(1)} collective-permute-done((bf16[16,64,128]{2,1,0:T(8,128)(2,1)S(1)}, bf16[16,64,128]{2,1,0:T(8,128)(2,1)S(1)}, u32[]{:S(2)}, u32[]{:S(2)}) %collective-permute-start.3) | collective-permute-done | bytes 262176 | tf_op jit(solution)/shard_map/ppermute | solution.py:388
  19.1 6.0 %prepare.2 = (bf16[128,64,128]{2,1,0:T(8,128)(2,1)S(1)}, f32[257,64,128]{2,1,0:T(8,128)S(1)}, bf16[512,128,128]{2,1,0:T(8,128)(2,1)S(1)}) custom-call(s32[1,1]{1,0:T(1,128)S(6)} %copy.19.count, bf16[16,64,128]{2,1,0:T(8,128)(2,1)S(1)} %get-tuple-element.40.refs_0_, bf16[16,64,128]{2,1,0:T(8,128)(2,1)S(1)} %get-tuple-element.39.refs_1_, ...), custom_call_target="tpu_custom_call" | custom-call | tf_op jit(solution)/shard_map/prepare/pallas_call | solution.py:108
  25.1 7.0 %block_product.2 = (bf16[128,64,128]{2,1,0:T(8,128)(2,1)S(1)}, f32[257,64,128]{2,1,0:T(8,128)S(1)}, s16[4,2,528,128]{3,2,1,0:T(8,128)(2,1)S(1)}) custom-call(s32[1,512]{1,0:T(1,128)S(1)} %copy-done.2, s32[1,512]{1,0:T(1,128)S(1)} %copy-done.3, s32[1,1]{1,0:T(1,128)S(6)} %copy.19.count, ...), custom_call_target="tpu_custom_call", output_to_operand_aliasing={{0}: (3, {}), {1}: (4, {})} | custom-call | tf_op jit(solution)/shard_map/block_product/pallas_call | solution.py:180
  33.3 2.2 %collective-permute-done.14.sib = s16[4,2,528,128]{3,2,1,0:T(8,128)(2,1)S(1)} collective-permute-done((s16[4,2,528,128]{3,2,1,0:T(8,128)(2,1)S(1)}, s16[4,2,528,128]{3,2,1,0:T(8,128)(2,1)S(1)}, u32[]{:S(2)}, u32[]{:S(2)}) %collective-permute-start.14) | collective-permute-done | bytes 1081376 | tf_op jit(solution)/shard_map/ppermute | solution.py:299
  35.5 0.8 spread.3
  36.4 3.4 %collective-permute-start.17 = (s16[2,528,128]{2,1,0:T(8,128)(2,1)S(1)}, s16[2,528,128]{2,1,0:T(8,128)(2,1)S(1)}, u32[]{:S(2)}, u32[]{:S(2)}) collective-permute-start(s16[2,528,128]{2,1,0:T(8,128)(2,1)S(1)} %get-tuple-element.34), channel_id=1, source_target_pairs={{0,24},{8,16},{16,8},{24,0},{1,25},{9,17},{17,9},{25,1},{2,26},{10... | collective-permute-start | bytes 811016 | tf_op jit(solution)/shard_map/ppermute | solution.py:388
  39.8 0.8 spread.2
  41.3 4.4 %collective-permute-done.15.refs_1_ = s16[2,528,128]{2,1,0:T(8,128)(2,1)S(1)} collective-permute-done((s16[2,528,128]{2,1,0:T(8,128)(2,1)S(1)}, s16[2,528,128]{2,1,0:T(8,128)(2,1)S(1)}, u32[]{:S(2)}, u32[]{:S(2)}) %collective-permute-start.15) | collective-permute-done | bytes 270368 | tf_op jit(solution)/shard_map/ppermute | solution.py:388
  45.7 6.6 %collective-permute-done.16.refs_2_ = s16[2,528,128]{2,1,0:T(8,128)(2,1)S(1)} collective-permute-done((s16[2,528,128]{2,1,0:T(8,128)(2,1)S(1)}, s16[2,528,128]{2,1,0:T(8,128)(2,1)S(1)}, u32[]{:S(2)}, u32[]{:S(2)}) %collective-permute-start.16) | collective-permute-done | bytes 270368 | tf_op jit(solution)/shard_map/ppermute | solution.py:388
  52.4 4.9 %collective-permute-done.7.refs_1_ = s16[2,528,128]{2,1,0:T(8,128)(2,1)S(1)} collective-permute-done((s16[2,528,128]{2,1,0:T(8,128)(2,1)S(1)}, s16[2,528,128]{2,1,0:T(8,128)(2,1)S(1)}, u32[]{:S(2)}, u32[]{:S(2)}) %collective-permute-start.7) | collective-permute-done | bytes 270368 | tf_op jit(solution)/shard_map/ppermute | solution.py:388
  57.3 5.0 %collective-permute-done.8.refs_2_ = s16[2,528,128]{2,1,0:T(8,128)(2,1)S(1)} collective-permute-done((s16[2,528,128]{2,1,0:T(8,128)(2,1)S(1)}, s16[2,528,128]{2,1,0:T(8,128)(2,1)S(1)}, u32[]{:S(2)}, u32[]{:S(2)}) %collective-permute-start.8) | collective-permute-done | bytes 270368 | tf_op jit(solution)/shard_map/ppermute | solution.py:388
  62.7 2.0 %collective-permute-start.19 = (s16[2,528,128]{2,1,0:T(8,128)(2,1)S(1)}, s16[2,528,128]{2,1,0:T(8,128)(2,1)S(1)}, u32[]{:S(2)}, u32[]{:S(2)}) collective-permute-start(s16[2,528,128]{2,1,0:T(8,128)(2,1)S(1)} %relay_message.10), channel_id=1, source_target_pairs={{0,2},{1,3},{6,4},{7,5},{2,6},{3,7},{4,0},{5,1},{8,10},{9,11},{14,... | collective-permute-start | bytes 811016 | tf_op jit(solution)/shard_map/ppermute | solution.py:288
  64.8 11.1 %collective-permute-done.10.refs_4_ = s16[2,528,128]{2,1,0:T(8,128)(2,1)S(1)} collective-permute-done((s16[2,528,128]{2,1,0:T(8,128)(2,1)S(1)}, s16[2,528,128]{2,1,0:T(8,128)(2,1)S(1)}, u32[]{:S(2)}, u32[]{:S(2)}) %collective-permute-start.10) | collective-permute-done | bytes 270368 | tf_op jit(solution)/shard_map/ppermute | solution.py:288
  76.5 0.7 collective-permute-start.21
  77.2 6.6 %collective-permute-start.20 = (s16[2,528,128]{2,1,0:T(8,128)(2,1)S(1)}, s16[2,528,128]{2,1,0:T(8,128)(2,1)S(1)}, u32[]{:S(2)}, u32[]{:S(2)}) collective-permute-start(s16[2,528,128]{2,1,0:T(8,128)(2,1)S(1)} %relay_message.11), channel_id=1, source_target_pairs={{0,2},{1,3},{6,4},{7,5},{8,10},{9,11},{14,12},{15,13},{16,18},{17,... | collective-permute-start | bytes 811016 | tf_op jit(solution)/shard_map/ppermute | solution.py:288
  83.8 2.7 %collective-permute-done.11.refs_4_.refs_5_ = s16[2,528,128]{2,1,0:T(8,128)(2,1)S(1)} collective-permute-done((s16[2,528,128]{2,1,0:T(8,128)(2,1)S(1)}, s16[2,528,128]{2,1,0:T(8,128)(2,1)S(1)}, u32[]{:S(2)}, u32[]{:S(2)}) %collective-permute-start.11) | collective-permute-done | bytes 270368 | tf_op jit(solution)/shard_map/ppermute | solution.py:288
  86.7 0.7 collective-permute-start.13
  87.4 3.3 %collective-permute-start.12 = (s16[2,528,128]{2,1,0:T(8,128)(2,1)S(1)}, s16[2,528,128]{2,1,0:T(8,128)(2,1)S(1)}, u32[]{:S(2)}, u32[]{:S(2)}) collective-permute-start(s16[2,528,128]{2,1,0:T(8,128)(2,1)S(1)} %relay_message.8), channel_id=1, source_target_pairs={{0,2},{1,3},{6,4},{7,5},{8,10},{9,11},{14,12},{15,13},{16,18},{17,... | collective-permute-start | bytes 811016 | tf_op jit(solution)/shard_map/ppermute | solution.py:288
  91.1 1.6 collective-permute-start.23
  92.7 1.9 %collective-permute-done.12.refs_6_ = s16[2,528,128]{2,1,0:T(8,128)(2,1)S(1)} collective-permute-done((s16[2,528,128]{2,1,0:T(8,128)(2,1)S(1)}, s16[2,528,128]{2,1,0:T(8,128)(2,1)S(1)}, u32[]{:S(2)}, u32[]{:S(2)}) %collective-permute-start.12) | collective-permute-done | bytes 270368 | tf_op jit(solution)/shard_map/ppermute | solution.py:288
  95.0 1.5 collective-permute-start.24
  97.1 1.5 collective-permute-start.22
  98.6 1.1 collective-permute-done.23.refs_3_
  99.7 1.5 collective-permute-start.27
  101.1 3.1 %collective-permute-done.24.refs_4_ = bf16[16,64,128]{2,1,0:T(8,128)(2,1)S(1)} collective-permute-done((bf16[16,64,128]{2,1,0:T(8,128)(2,1)S(1)}, bf16[16,64,128]{2,1,0:T(8,128)(2,1)S(1)}, u32[]{:S(2)}, u32[]{:S(2)}) %collective-permute-start.24) | collective-permute-done | bytes 262176 | tf_op jit(solution)/shard_map/ppermute | solution.py:388
  104.2 1.5 collective-permute-start.26
  105.7 2.2 %collective-permute-done.25.refs_5_ = bf16[16,64,128]{2,1,0:T(8,128)(2,1)S(1)} collective-permute-done((bf16[16,64,128]{2,1,0:T(8,128)(2,1)S(1)}, bf16[16,64,128]{2,1,0:T(8,128)(2,1)S(1)}, u32[]{:S(2)}, u32[]{:S(2)}) %collective-permute-start.25) | collective-permute-done | bytes 262176 | tf_op jit(solution)/shard_map/ppermute | solution.py:388
  108.0 1.5 prepare.3
  109.5 1.3 collective-permute-done.27.refs_1_
  110.8 7.0 %block_product.3 = (bf16[128,64,128]{2,1,0:T(8,128)(2,1)S(1)}, f32[257,64,128]{2,1,0:T(8,128)S(1)}, s16[4,2,528,128]{3,2,1,0:T(8,128)(2,1)S(1)}) custom-call(s32[1,512]{1,0:T(1,128)S(1)} %copy-done.2, s32[1,512]{1,0:T(1,128)S(1)} %copy-done.3, s32[1,1]{1,0:T(1,128)S(6)} %copy.19.count, ...), custom_call_target="tpu_custom_call", output_to_operand_aliasing={{0}: (3, {}), {1}: (4, {})} | custom-call | tf_op jit(solution)/shard_map/block_product/pallas_call | solution.py:180
  118.9 1.6 collective-permute-done.33.sib
  120.7 2.0 %collective-permute-start.34 = (s16[2,528,128]{2,1,0:T(8,128)(2,1)S(1)}, s16[2,528,128]{2,1,0:T(8,128)(2,1)S(1)}, u32[]{:S(2)}, u32[]{:S(2)}) collective-permute-start(s16[2,528,128]{2,1,0:T(8,128)(2,1)S(1)} %combine_message.9), channel_id=1, source_target_pairs={{0,2},{1,3},{2,0},{3,1},{4,6},{5,7},{6,4},{7,5},{8,10},{9,11},{10,... | collective-permute-start | bytes 811016 | tf_op jit(solution)/shard_map/ppermute | solution.py:288
  122.9 1.4 collective-permute-start.29
  124.3 5.8 %collective-permute-done.34.refs_0_ = s16[2,528,128]{2,1,0:T(8,128)(2,1)S(1)} collective-permute-done((s16[2,528,128]{2,1,0:T(8,128)(2,1)S(1)}, s16[2,528,128]{2,1,0:T(8,128)(2,1)S(1)}, u32[]{:S(2)}, u32[]{:S(2)}) %collective-permute-start.34) | collective-permute-done | bytes 270368 | tf_op jit(solution)/shard_map/ppermute | solution.py:288
  130.4 2.0 %collective-permute-start.35 = (s16[2,528,128]{2,1,0:T(8,128)(2,1)S(1)}, s16[2,528,128]{2,1,0:T(8,128)(2,1)S(1)}, u32[]{:S(2)}, u32[]{:S(2)}) collective-permute-start(s16[2,528,128]{2,1,0:T(8,128)(2,1)S(1)} %combine_message.10), channel_id=1, source_target_pairs={{0,2},{1,3},{6,4},{7,5},{2,6},{3,7},{4,0},{5,1},{8,10},{9,11},{14,... | collective-permute-start | bytes 811016 | tf_op jit(solution)/shard_map/ppermute | solution.py:288
  132.4 8.7 %collective-permute-done.29.refs_0_ = s16[2,528,128]{2,1,0:T(8,128)(2,1)S(1)} collective-permute-done((s16[2,528,128]{2,1,0:T(8,128)(2,1)S(1)}, s16[2,528,128]{2,1,0:T(8,128)(2,1)S(1)}, u32[]{:S(2)}, u32[]{:S(2)}) %collective-permute-start.29) | collective-permute-done | bytes 270368 | tf_op jit(solution)/shard_map/ppermute | solution.py:288
  142.4 7.4 %collective-permute-start.36 = (s16[2,528,128]{2,1,0:T(8,128)(2,1)S(1)}, s16[2,528,128]{2,1,0:T(8,128)(2,1)S(1)}, u32[]{:S(2)}, u32[]{:S(2)}) collective-permute-start(s16[2,528,128]{2,1,0:T(8,128)(2,1)S(1)} %combine_message.11), channel_id=1, source_target_pairs={{0,2},{1,3},{6,4},{7,5},{8,10},{9,11},{14,12},{15,13},{16,18},{17,... | collective-permute-start | bytes 811016 | tf_op jit(solution)/shard_map/ppermute | solution.py:288
  149.8 1.5 collective-permute-done.30.refs_0_.refs_1_
  152.3 4.4 %collective-permute-start.31 = (s16[2,528,128]{2,1,0:T(8,128)(2,1)S(1)}, s16[2,528,128]{2,1,0:T(8,128)(2,1)S(1)}, u32[]{:S(2)}, u32[]{:S(2)}) collective-permute-start(s16[2,528,128]{2,1,0:T(8,128)(2,1)S(1)} %combine_message.8), channel_id=1, source_target_pairs={{0,2},{1,3},{6,4},{7,5},{8,10},{9,11},{14,12},{15,13},{16,18},{17,... | collective-permute-start | bytes 811016 | tf_op jit(solution)/shard_map/ppermute | solution.py:288
  156.6 1.1 combine_rows.2.refs_4_
  157.8 3.3 %collective-permute-done.31.refs_2_ = s16[2,528,128]{2,1,0:T(8,128)(2,1)S(1)} collective-permute-done((s16[2,528,128]{2,1,0:T(8,128)(2,1)S(1)}, s16[2,528,128]{2,1,0:T(8,128)(2,1)S(1)}, u32[]{:S(2)}, u32[]{:S(2)}) %collective-permute-start.31) | collective-permute-done | bytes 270368 | tf_op jit(solution)/shard_map/ppermute | solution.py:288
  161.1 1.1 combine_rows.3
  (62 shorter events, 9.4 us)
Async XLA Ops:
  0.0 1.0 copy-start
  1.2 10.2 %collective-permute-start.1 = (bf16[16,64,128]{2,1,0:T(8,128)(2,1)S(1)}, bf16[16,64,128]{2,1,0:T(8,128)(2,1)S(1)}, u32[]{:S(2)}, u32[]{:S(2)}) collective-permute-start(bf16[16,64,128]{2,1,0:T(8,128)(2,1)S(1)} %get-tuple-element.39.refs_1_), channel_id=1, source_target_pairs={{0,8},{8,0},{16,24},{24,16},{1,9},{9,1},{17,25},{25,17},{2,10},{10... | collective-permute-start | bytes 786440 | tf_op jit(solution)/shard_map/ppermute | solution.py:388
  4.3 9.2 %collective-permute-start.2 = (bf16[16,64,128]{2,1,0:T(8,128)(2,1)S(1)}, bf16[16,64,128]{2,1,0:T(8,128)(2,1)S(1)}, u32[]{:S(2)}, u32[]{:S(2)}) collective-permute-start(bf16[16,64,128]{2,1,0:T(8,128)(2,1)S(1)} %get-tuple-element.40.refs_0_), channel_id=1, source_target_pairs={{0,16},{8,24},{16,0},{24,8},{1,17},{9,25},{17,1},{25,9},{2,18},{10... | collective-permute-start | bytes 786440 | tf_op jit(solution)/shard_map/ppermute | solution.py:388
  5.8 13.3 %collective-permute-start.3 = (bf16[16,64,128]{2,1,0:T(8,128)(2,1)S(1)}, bf16[16,64,128]{2,1,0:T(8,128)(2,1)S(1)}, u32[]{:S(2)}, u32[]{:S(2)}) collective-permute-start(bf16[16,64,128]{2,1,0:T(8,128)(2,1)S(1)} %get-tuple-element.39.refs_1_), channel_id=1, source_target_pairs={{0,16},{8,24},{16,0},{24,8},{1,17},{9,25},{17,1},{25,9},{2,18},{10... | collective-permute-start | bytes 786440 | tf_op jit(solution)/shard_map/ppermute | solution.py:388
  6.3 12.8 %collective-permute-start = (bf16[16,64,128]{2,1,0:T(8,128)(2,1)S(1)}, bf16[16,64,128]{2,1,0:T(8,128)(2,1)S(1)}, u32[]{:S(2)}, u32[]{:S(2)}) collective-permute-start(bf16[16,64,128]{2,1,0:T(8,128)(2,1)S(1)} %get-tuple-element.40.refs_0_), channel_id=1, source_target_pairs={{0,8},{8,0},{16,24},{24,16},{1,9},{9,1},{17,25},{25,17},{2,10},{10... | collective-permute-start | bytes 786440 | tf_op jit(solution)/shard_map/ppermute | solution.py:388
  11.4 13.7 %collective-permute-start.5 = (bf16[16,64,128]{2,1,0:T(8,128)(2,1)S(1)}, bf16[16,64,128]{2,1,0:T(8,128)(2,1)S(1)}, u32[]{:S(2)}, u32[]{:S(2)}) collective-permute-start(bf16[16,64,128]{2,1,0:T(8,128)(2,1)S(1)} %collective-permute-done.1.refs_3_), channel_id=1, source_target_pairs={{0,16},{8,24},{16,0},{24,8},{1,17},{9,25},{17,1},{25,9},{2,18},{10... | collective-permute-start | bytes 786440 | tf_op jit(solution)/shard_map/ppermute | solution.py:388
  13.5 11.6 %collective-permute-start.4 = (bf16[16,64,128]{2,1,0:T(8,128)(2,1)S(1)}, bf16[16,64,128]{2,1,0:T(8,128)(2,1)S(1)}, u32[]{:S(2)}, u32[]{:S(2)}) collective-permute-start(bf16[16,64,128]{2,1,0:T(8,128)(2,1)S(1)} %collective-permute-done.2.refs_4_), channel_id=1, source_target_pairs={{0,8},{8,0},{16,24},{24,16},{1,9},{9,1},{17,25},{25,17},{2,10},{10... | collective-permute-start | bytes 786440 | tf_op jit(solution)/shard_map/ppermute | solution.py:388
  19.1 6.0 %copy-start.2 = (s32[1,512]{1,0:T(1,128)S(1)}, s32[1,512]{1,0:T(1,128)}, u32[]{:S(2)}) copy-start(s32[1,512]{1,0:T(1,128)} %rows.3) | copy-start | bytes 6148
  19.1 6.0 %copy-start.3 = (s32[1,512]{1,0:T(1,128)S(1)}, s32[1,512]{1,0:T(1,128)}, u32[]{:S(2)}) copy-start(s32[1,512]{1,0:T(1,128)} %cols.3) | copy-start | bytes 6148
  32.7 2.8 %collective-permute-start.14 = (s16[4,2,528,128]{3,2,1,0:T(8,128)(2,1)S(1)}, s16[4,2,528,128]{3,2,1,0:T(8,128)(2,1)S(1)}, u32[]{:S(2)}, u32[]{:S(2)}) collective-permute-start(s16[4,2,528,128]{3,2,1,0:T(8,128)(2,1)S(1)} %encode_half.2), channel_id=1, source_target_pairs={{0,1},{1,0},{2,3},{3,2},{4,5},{5,4},{6,7},{7,6},{8,9},{9,8},{10,11... | collective-permute-start | bytes 3244040 | tf_op jit(solution)/shard_map/ppermute | solution.py:299
  32.8 7.0 %collective-permute-start.6 = (s16[4,2,528,128]{3,2,1,0:T(8,128)(2,1)S(1)}, s16[4,2,528,128]{3,2,1,0:T(8,128)(2,1)S(1)}, u32[]{:S(2)}, u32[]{:S(2)}) collective-permute-start(s16[4,2,528,128]{3,2,1,0:T(8,128)(2,1)S(1)} %get-tuple-element.26), channel_id=1, source_target_pairs={{0,1},{1,0},{2,3},{3,2},{4,5},{5,4},{6,7},{7,6},{8,9},{9,8},{10,11... | collective-permute-start | bytes 3244040 | tf_op jit(solution)/shard_map/ppermute | solution.py:299
  36.3 9.4 %collective-permute-start.15 = (s16[2,528,128]{2,1,0:T(8,128)(2,1)S(1)}, s16[2,528,128]{2,1,0:T(8,128)(2,1)S(1)}, u32[]{:S(2)}, u32[]{:S(2)}) collective-permute-start(s16[2,528,128]{2,1,0:T(8,128)(2,1)S(1)} %get-tuple-element.32), channel_id=1, source_target_pairs={{0,8},{8,0},{16,24},{24,16},{1,9},{9,1},{17,25},{25,17},{2,10},{10... | collective-permute-start | bytes 811016 | tf_op jit(solution)/shard_map/ppermute | solution.py:388
  36.4 16.0 %collective-permute-start.16 = (s16[2,528,128]{2,1,0:T(8,128)(2,1)S(1)}, s16[2,528,128]{2,1,0:T(8,128)(2,1)S(1)}, u32[]{:S(2)}, u32[]{:S(2)}) collective-permute-start(s16[2,528,128]{2,1,0:T(8,128)(2,1)S(1)} %get-tuple-element.33), channel_id=1, source_target_pairs={{0,16},{8,24},{16,0},{24,8},{1,17},{9,25},{17,1},{25,9},{2,18},{10... | collective-permute-start | bytes 811016 | tf_op jit(solution)/shard_map/ppermute | solution.py:388
  36.4 15.9 %collective-permute-start.17 = (s16[2,528,128]{2,1,0:T(8,128)(2,1)S(1)}, s16[2,528,128]{2,1,0:T(8,128)(2,1)S(1)}, u32[]{:S(2)}, u32[]{:S(2)}) collective-permute-start(s16[2,528,128]{2,1,0:T(8,128)(2,1)S(1)} %get-tuple-element.34), channel_id=1, source_target_pairs={{0,24},{8,16},{16,8},{24,0},{1,25},{9,17},{17,9},{25,1},{2,26},{10... | collective-permute-start | bytes 811016 | tf_op jit(solution)/shard_map/ppermute | solution.py:388
  40.6 16.7 %collective-permute-start.7 = (s16[2,528,128]{2,1,0:T(8,128)(2,1)S(1)}, s16[2,528,128]{2,1,0:T(8,128)(2,1)S(1)}, u32[]{:S(2)}, u32[]{:S(2)}) collective-permute-start(s16[2,528,128]{2,1,0:T(8,128)(2,1)S(1)} %get-tuple-element.28), channel_id=1, source_target_pairs={{0,8},{8,0},{16,24},{24,16},{1,9},{9,1},{17,25},{25,17},{2,10},{10... | collective-permute-start | bytes 811016 | tf_op jit(solution)/shard_map/ppermute | solution.py:388
  40.8 21.6 %collective-permute-start.8 = (s16[2,528,128]{2,1,0:T(8,128)(2,1)S(1)}, s16[2,528,128]{2,1,0:T(8,128)(2,1)S(1)}, u32[]{:S(2)}, u32[]{:S(2)}) collective-permute-start(s16[2,528,128]{2,1,0:T(8,128)(2,1)S(1)} %get-tuple-element.29), channel_id=1, source_target_pairs={{0,16},{8,24},{16,0},{24,8},{1,17},{9,25},{17,1},{25,9},{2,18},{10... | collective-permute-start | bytes 811016 | tf_op jit(solution)/shard_map/ppermute | solution.py:388
  45.7 16.6 %collective-permute-start.9 = (s16[2,528,128]{2,1,0:T(8,128)(2,1)S(1)}, s16[2,528,128]{2,1,0:T(8,128)(2,1)S(1)}, u32[]{:S(2)}, u32[]{:S(2)}) collective-permute-start(s16[2,528,128]{2,1,0:T(8,128)(2,1)S(1)} %get-tuple-element.30), channel_id=1, source_target_pairs={{0,24},{8,16},{16,8},{24,0},{1,25},{9,17},{17,9},{25,1},{2,26},{10... | collective-permute-start | bytes 811016 | tf_op jit(solution)/shard_map/ppermute | solution.py:388
  52.3 10.1 %collective-permute-start.18 = (s16[2,528,128]{2,1,0:T(8,128)(2,1)S(1)}, s16[2,528,128]{2,1,0:T(8,128)(2,1)S(1)}, u32[]{:S(2)}, u32[]{:S(2)}) collective-permute-start(s16[2,528,128]{2,1,0:T(8,128)(2,1)S(1)} %relay_message.9), channel_id=1, source_target_pairs={{0,2},{1,3},{2,0},{3,1},{4,6},{5,7},{6,4},{7,5},{8,10},{9,11},{10,... | collective-permute-start | bytes 811016 | tf_op jit(solution)/shard_map/ppermute | solution.py:288
  62.4 13.5 %collective-permute-start.10 = (s16[2,528,128]{2,1,0:T(8,128)(2,1)S(1)}, s16[2,528,128]{2,1,0:T(8,128)(2,1)S(1)}, u32[]{:S(2)}, u32[]{:S(2)}) collective-permute-start(s16[2,528,128]{2,1,0:T(8,128)(2,1)S(1)} %relay_message.6), channel_id=1, source_target_pairs={{0,2},{1,3},{2,0},{3,1},{4,6},{5,7},{6,4},{7,5},{8,10},{9,11},{10,... | collective-permute-start | bytes 811016 | tf_op jit(solution)/shard_map/ppermute | solution.py:288
  62.7 13.5 %collective-permute-start.19 = (s16[2,528,128]{2,1,0:T(8,128)(2,1)S(1)}, s16[2,528,128]{2,1,0:T(8,128)(2,1)S(1)}, u32[]{:S(2)}, u32[]{:S(2)}) collective-permute-start(s16[2,528,128]{2,1,0:T(8,128)(2,1)S(1)} %relay_message.10), channel_id=1, source_target_pairs={{0,2},{1,3},{6,4},{7,5},{2,6},{3,7},{4,0},{5,1},{8,10},{9,11},{14,... | collective-permute-start | bytes 811016 | tf_op jit(solution)/shard_map/ppermute | solution.py:288
  76.1 10.3 %collective-permute-start.11 = (s16[2,528,128]{2,1,0:T(8,128)(2,1)S(1)}, s16[2,528,128]{2,1,0:T(8,128)(2,1)S(1)}, u32[]{:S(2)}, u32[]{:S(2)}) collective-permute-start(s16[2,528,128]{2,1,0:T(8,128)(2,1)S(1)} %relay_message.7), channel_id=1, source_target_pairs={{0,2},{1,3},{6,4},{7,5},{2,6},{3,7},{4,0},{5,1},{8,10},{9,11},{14,... | collective-permute-start | bytes 811016 | tf_op jit(solution)/shard_map/ppermute | solution.py:288
  76.5 14.2 %collective-permute-start.21 = (s16[2,528,128]{2,1,0:T(8,128)(2,1)S(1)}, s16[2,528,128]{2,1,0:T(8,128)(2,1)S(1)}, u32[]{:S(2)}, u32[]{:S(2)}) collective-permute-start(s16[2,528,128]{2,1,0:T(8,128)(2,1)S(1)} %relay_message.11), channel_id=1, source_target_pairs={{2,4},{3,5},{4,2},{5,3},{10,12},{11,13},{12,10},{13,11},{18,20},{1... | collective-permute-start | bytes 811016 | tf_op jit(solution)/shard_map/ppermute | solution.py:288
  77.2 13.5 %collective-permute-start.20 = (s16[2,528,128]{2,1,0:T(8,128)(2,1)S(1)}, s16[2,528,128]{2,1,0:T(8,128)(2,1)S(1)}, u32[]{:S(2)}, u32[]{:S(2)}) collective-permute-start(s16[2,528,128]{2,1,0:T(8,128)(2,1)S(1)} %relay_message.11), channel_id=1, source_target_pairs={{0,2},{1,3},{6,4},{7,5},{8,10},{9,11},{14,12},{15,13},{16,18},{17,... | collective-permute-start | bytes 811016 | tf_op jit(solution)/shard_map/ppermute | solution.py:288
  86.7 5.9 %collective-permute-start.13 = (s16[2,528,128]{2,1,0:T(8,128)(2,1)S(1)}, s16[2,528,128]{2,1,0:T(8,128)(2,1)S(1)}, u32[]{:S(2)}, u32[]{:S(2)}) collective-permute-start(s16[2,528,128]{2,1,0:T(8,128)(2,1)S(1)} %relay_message.8), channel_id=1, source_target_pairs={{2,4},{3,5},{4,2},{5,3},{10,12},{11,13},{12,10},{13,11},{18,20},{1... | collective-permute-start | bytes 811016 | tf_op jit(solution)/shard_map/ppermute | solution.py:288
  87.4 7.2 %collective-permute-start.12 = (s16[2,528,128]{2,1,0:T(8,128)(2,1)S(1)}, s16[2,528,128]{2,1,0:T(8,128)(2,1)S(1)}, u32[]{:S(2)}, u32[]{:S(2)}) collective-permute-start(s16[2,528,128]{2,1,0:T(8,128)(2,1)S(1)} %relay_message.8), channel_id=1, source_target_pairs={{0,2},{1,3},{6,4},{7,5},{8,10},{9,11},{14,12},{15,13},{16,18},{17,... | collective-permute-start | bytes 811016 | tf_op jit(solution)/shard_map/ppermute | solution.py:288
  91.1 8.6 %collective-permute-start.23 = (bf16[16,64,128]{2,1,0:T(8,128)(2,1)S(1)}, bf16[16,64,128]{2,1,0:T(8,128)(2,1)S(1)}, u32[]{:S(2)}, u32[]{:S(2)}) collective-permute-start(bf16[16,64,128]{2,1,0:T(8,128)(2,1)S(1)} %relay_tiles.3.refs_1_), channel_id=1, source_target_pairs={{0,8},{8,0},{16,24},{24,16},{1,9},{9,1},{17,25},{25,17},{2,10},{10... | collective-permute-start | bytes 786440 | tf_op jit(solution)/shard_map/ppermute | solution.py:388
  95.0 9.2 %collective-permute-start.24 = (bf16[16,64,128]{2,1,0:T(8,128)(2,1)S(1)}, bf16[16,64,128]{2,1,0:T(8,128)(2,1)S(1)}, u32[]{:S(2)}, u32[]{:S(2)}) collective-permute-start(bf16[16,64,128]{2,1,0:T(8,128)(2,1)S(1)} %relay_tiles.2.refs_0_), channel_id=1, source_target_pairs={{0,16},{8,24},{16,0},{24,8},{1,17},{9,25},{17,1},{25,9},{2,18},{10... | collective-permute-start | bytes 786440 | tf_op jit(solution)/shard_map/ppermute | solution.py:388
  96.5 11.5 %collective-permute-start.25 = (bf16[16,64,128]{2,1,0:T(8,128)(2,1)S(1)}, bf16[16,64,128]{2,1,0:T(8,128)(2,1)S(1)}, u32[]{:S(2)}, u32[]{:S(2)}) collective-permute-start(bf16[16,64,128]{2,1,0:T(8,128)(2,1)S(1)} %relay_tiles.3.refs_1_), channel_id=1, source_target_pairs={{0,16},{8,24},{16,0},{24,8},{1,17},{9,25},{17,1},{25,9},{2,18},{10... | collective-permute-start | bytes 786440 | tf_op jit(solution)/shard_map/ppermute | solution.py:388
  97.1 10.9 %collective-permute-start.22 = (bf16[16,64,128]{2,1,0:T(8,128)(2,1)S(1)}, bf16[16,64,128]{2,1,0:T(8,128)(2,1)S(1)}, u32[]{:S(2)}, u32[]{:S(2)}) collective-permute-start(bf16[16,64,128]{2,1,0:T(8,128)(2,1)S(1)} %relay_tiles.2.refs_0_), channel_id=1, source_target_pairs={{0,8},{8,0},{16,24},{24,16},{1,9},{9,1},{17,25},{25,17},{2,10},{10... | collective-permute-start | bytes 786440 | tf_op jit(solution)/shard_map/ppermute | solution.py:388
  99.7 11.1 %collective-permute-start.27 = (bf16[16,64,128]{2,1,0:T(8,128)(2,1)S(1)}, bf16[16,64,128]{2,1,0:T(8,128)(2,1)S(1)}, u32[]{:S(2)}, u32[]{:S(2)}) collective-permute-start(bf16[16,64,128]{2,1,0:T(8,128)(2,1)S(1)} %collective-permute-done.23.refs_3_), channel_id=1, source_target_pairs={{0,16},{8,24},{16,0},{24,8},{1,17},{9,25},{17,1},{25,9},{2,18},{10... | collective-permute-start | bytes 786440 | tf_op jit(solution)/shard_map/ppermute | solution.py:388
  104.2 6.5 %collective-permute-start.26 = (bf16[16,64,128]{2,1,0:T(8,128)(2,1)S(1)}, bf16[16,64,128]{2,1,0:T(8,128)(2,1)S(1)}, u32[]{:S(2)}, u32[]{:S(2)}) collective-permute-start(bf16[16,64,128]{2,1,0:T(8,128)(2,1)S(1)} %collective-permute-done.24.refs_4_), channel_id=1, source_target_pairs={{0,8},{8,0},{16,24},{24,16},{1,9},{9,1},{17,25},{25,17},{2,10},{10... | collective-permute-start | bytes 786440 | tf_op jit(solution)/shard_map/ppermute | solution.py:388
  117.8 2.8 %collective-permute-start.33 = (s16[4,2,528,128]{3,2,1,0:T(8,128)(2,1)S(1)}, s16[4,2,528,128]{3,2,1,0:T(8,128)(2,1)S(1)}, u32[]{:S(2)}, u32[]{:S(2)}) collective-permute-start(s16[4,2,528,128]{3,2,1,0:T(8,128)(2,1)S(1)} %get-tuple-element.38), channel_id=1, source_target_pairs={{0,1},{1,0},{2,3},{3,2},{4,5},{5,4},{6,7},{7,6},{8,9},{9,8},{10,11... | collective-permute-start | bytes 3244040 | tf_op jit(solution)/shard_map/ppermute | solution.py:299
  118.4 4.3 %collective-permute-start.28 = (s16[4,2,528,128]{3,2,1,0:T(8,128)(2,1)S(1)}, s16[4,2,528,128]{3,2,1,0:T(8,128)(2,1)S(1)}, u32[]{:S(2)}, u32[]{:S(2)}) collective-permute-start(s16[4,2,528,128]{3,2,1,0:T(8,128)(2,1)S(1)} %encode_half.3), channel_id=1, source_target_pairs={{0,1},{1,0},{2,3},{3,2},{4,5},{5,4},{6,7},{7,6},{8,9},{9,8},{10,11... | collective-permute-start | bytes 3244040 | tf_op jit(solution)/shard_map/ppermute | solution.py:299
  120.7 9.4 %collective-permute-start.34 = (s16[2,528,128]{2,1,0:T(8,128)(2,1)S(1)}, s16[2,528,128]{2,1,0:T(8,128)(2,1)S(1)}, u32[]{:S(2)}, u32[]{:S(2)}) collective-permute-start(s16[2,528,128]{2,1,0:T(8,128)(2,1)S(1)} %combine_message.9), channel_id=1, source_target_pairs={{0,2},{1,3},{2,0},{3,1},{4,6},{5,7},{6,4},{7,5},{8,10},{9,11},{10,... | collective-permute-start | bytes 811016 | tf_op jit(solution)/shard_map/ppermute | solution.py:288
  122.9 18.2 %collective-permute-start.29 = (s16[2,528,128]{2,1,0:T(8,128)(2,1)S(1)}, s16[2,528,128]{2,1,0:T(8,128)(2,1)S(1)}, u32[]{:S(2)}, u32[]{:S(2)}) collective-permute-start(s16[2,528,128]{2,1,0:T(8,128)(2,1)S(1)} %combine_message.6), channel_id=1, source_target_pairs={{0,2},{1,3},{2,0},{3,1},{4,6},{5,7},{6,4},{7,5},{8,10},{9,11},{10,... | collective-permute-start | bytes 811016 | tf_op jit(solution)/shard_map/ppermute | solution.py:288
  130.4 11.0 %collective-permute-start.35 = (s16[2,528,128]{2,1,0:T(8,128)(2,1)S(1)}, s16[2,528,128]{2,1,0:T(8,128)(2,1)S(1)}, u32[]{:S(2)}, u32[]{:S(2)}) collective-permute-start(s16[2,528,128]{2,1,0:T(8,128)(2,1)S(1)} %combine_message.10), channel_id=1, source_target_pairs={{0,2},{1,3},{6,4},{7,5},{2,6},{3,7},{4,0},{5,1},{8,10},{9,11},{14,... | collective-permute-start | bytes 811016 | tf_op jit(solution)/shard_map/ppermute | solution.py:288
  141.4 9.9 %collective-permute-start.30 = (s16[2,528,128]{2,1,0:T(8,128)(2,1)S(1)}, s16[2,528,128]{2,1,0:T(8,128)(2,1)S(1)}, u32[]{:S(2)}, u32[]{:S(2)}) collective-permute-start(s16[2,528,128]{2,1,0:T(8,128)(2,1)S(1)} %combine_message.7), channel_id=1, source_target_pairs={{0,2},{1,3},{6,4},{7,5},{2,6},{3,7},{4,0},{5,1},{8,10},{9,11},{14,... | collective-permute-start | bytes 811016 | tf_op jit(solution)/shard_map/ppermute | solution.py:288
  141.7 14.9 %collective-permute-start.37 = (s16[2,528,128]{2,1,0:T(8,128)(2,1)S(1)}, s16[2,528,128]{2,1,0:T(8,128)(2,1)S(1)}, u32[]{:S(2)}, u32[]{:S(2)}) collective-permute-start(s16[2,528,128]{2,1,0:T(8,128)(2,1)S(1)} %combine_message.11), channel_id=1, source_target_pairs={{2,4},{3,5},{4,2},{5,3},{10,12},{11,13},{12,10},{13,11},{18,20},{1... | collective-permute-start | bytes 811016 | tf_op jit(solution)/shard_map/ppermute | solution.py:288
  142.4 14.2 %collective-permute-start.36 = (s16[2,528,128]{2,1,0:T(8,128)(2,1)S(1)}, s16[2,528,128]{2,1,0:T(8,128)(2,1)S(1)}, u32[]{:S(2)}, u32[]{:S(2)}) collective-permute-start(s16[2,528,128]{2,1,0:T(8,128)(2,1)S(1)} %combine_message.11), channel_id=1, source_target_pairs={{0,2},{1,3},{6,4},{7,5},{8,10},{9,11},{14,12},{15,13},{16,18},{17,... | collective-permute-start | bytes 811016 | tf_op jit(solution)/shard_map/ppermute | solution.py:288
  151.6 6.2 %collective-permute-start.32 = (s16[2,528,128]{2,1,0:T(8,128)(2,1)S(1)}, s16[2,528,128]{2,1,0:T(8,128)(2,1)S(1)}, u32[]{:S(2)}, u32[]{:S(2)}) collective-permute-start(s16[2,528,128]{2,1,0:T(8,128)(2,1)S(1)} %combine_message.8), channel_id=1, source_target_pairs={{2,4},{3,5},{4,2},{5,3},{10,12},{11,13},{12,10},{13,11},{18,20},{1... | collective-permute-start | bytes 811016 | tf_op jit(solution)/shard_map/ppermute | solution.py:288
  152.3 8.8 %collective-permute-start.31 = (s16[2,528,128]{2,1,0:T(8,128)(2,1)S(1)}, s16[2,528,128]{2,1,0:T(8,128)(2,1)S(1)}, u32[]{:S(2)}, u32[]{:S(2)}) collective-permute-start(s16[2,528,128]{2,1,0:T(8,128)(2,1)S(1)} %combine_message.8), channel_id=1, source_target_pairs={{0,2},{1,3},{6,4},{7,5},{8,10},{9,11},{14,12},{15,13},{16,18},{17,... | collective-permute-start | bytes 811016 | tf_op jit(solution)/shard_map/ppermute | solution.py:288
  161.1 1.1 copy-start.1
